TPU v7x, 32 devices: a whole 2x2x4 slice. The times are simulated.
32 devices in a mesh: streams: 2 (over x), seq: 16 (over z, y, core).
Axes of the slice: x: 2, y: 2, z: 4, core: 2. Of those that a mesh axis runs over, the one named last changes fastest.
Arguments:
- queries: bfloat16 [8192, 2048], P(('streams', 'seq')), parts along dimension 0, may hold values from -13 to 13
- keyval: bfloat16 [2, 8192, 2048], P(None, ('streams', 'seq')), parts along dimension 1, may hold values from -13 to 13
Outputs:
- attended: bfloat16 [8192, 2048], P(('streams', 'seq')), parts along dimension 0
There are 2 independent parts, one for each index of `streams`. A program takes and returns all parts, laid end to end along the dimension named above; each array names one. Nothing has to cross between parts.
All inputs are finite; a program needn't handle non-finite values.
Results may differ from a plain program's by a relative error of at most 0.0052.
Values may be sent and summed in bfloat16 or wider, within the bound.
No kernel may reach another device: no remote copies, remote signals or barrier semaphores. Data moves between devices by JAX's collectives and lax.ppermute only.
A program may use at most 128 MiB of HBM per device.

v0:
```python
import math

import jax
import jax.numpy as jnp
from jax import lax
from jax.sharding import PartitionSpec as P

HEADS = 16
HEAD_DIM = 128
BLOCK = 128


neg_large = -1e30
log_two = 0.6931471805599453


def swapped(array, axis, stride):
    return lax.ppermute(array, axis, [(i, i ^ 1 << stride) for i in range(lax.axis_size(axis))])


def padded_2(block, sides, width):
    for axis, dim in sides:
        count = lax.axis_size(axis)
        forward = [(i, i + 1) for i in range(count - 1)]
        backward = [(target, source) for source, target in forward]
        low = lax.ppermute(
            lax.slice_in_dim(block, block.shape[dim] - width, None, axis=dim), axis, forward
        )
        high = lax.ppermute(lax.slice_in_dim(block, 0, width, axis=dim), axis, backward)
        block = jnp.concatenate([low, block, high], axis=dim)
    return block


def halve_rows(pair_rows, along):
    old_shape = pair_rows.shape
    new_shape = old_shape[:along] + (old_shape[along] // 2, 2) + old_shape[along + 1 :]
    widened = pair_rows.reshape(new_shape).astype(jnp.float32)
    pooled = (jnp.take(widened, 0, axis=along + 1) + jnp.take(widened, 1, axis=along + 1)) * 0.5
    return pooled.astype(jnp.bfloat16)


def attend(query_rows, key_rows, value_rows, key_bias, scaling):
    scores = (
        jnp.einsum("gqhe,gkhe->ghqk", query_rows, key_rows, preferred_element_type=jnp.float32)
        * scaling
    )
    if key_bias is not None:
        scores = scores + key_bias[:, None, None, :]
    row_max = jnp.max(scores, axis=3)
    expons = jnp.exp(scores - row_max[..., None])
    row_sum = jnp.sum(expons, axis=3)
    weighted = jnp.einsum(
        "ghqk,gkhe->gqhe",
        expons.astype(jnp.bfloat16),
        value_rows,
        preferred_element_type=jnp.float32,
    )
    head_count = row_max.shape[1]
    return (
        jnp.transpose(row_max, (0, 2, 1)).reshape(-1, head_count),
        weighted.reshape(-1, head_count, weighted.shape[3]),
        jnp.transpose(row_sum, (0, 2, 1)).reshape(-1, head_count),
    )


def combine(results):
    level_total = len(results)
    top_max, top_weighted, top_sum = results[level_total - 1]
    peak = top_max + (level_total - 1) * log_two
    numerator = top_weighted
    denominator = top_sum
    for level_index in range(level_total - 2, -1, -1):
        row_max, weighted, row_sum = results[level_index]
        ratio = row_max.shape[0] // peak.shape[0]
        peak = jnp.repeat(peak, ratio, axis=0)
        numerator = jnp.repeat(numerator, ratio, axis=0)
        denominator = jnp.repeat(denominator, ratio, axis=0)
        level_peak = row_max + level_index * log_two
        new_peak = jnp.maximum(peak, level_peak)
        carry_factor = jnp.exp(peak - new_peak)
        level_factor = jnp.exp(level_peak - new_peak)
        numerator = carry_factor[..., None] * numerator + level_factor[..., None] * weighted
        denominator = carry_factor * denominator + level_factor * row_sum
        peak = new_peak
    return (numerator / denominator[..., None]).astype(jnp.bfloat16)


def swap_sibling(own_block, bit_index):
    return swapped(own_block, "seq", bit_index)


def on_device(queries, keyval):
    row_count = queries.shape[0]
    feature_count = queries.shape[1]
    head_count = HEADS
    head_size = HEAD_DIM
    block_size = BLOCK
    scaling = 1.0 / math.sqrt(head_size)
    axis_size = lax.axis_size("seq")
    position = lax.axis_index("seq")
    axis_bits = axis_size.bit_length() - 1
    block_count = row_count // block_size
    padded = padded_2(keyval, (("seq", 1),), block_size)
    blocked = (2, block_count, block_size, head_count, head_size)
    before = padded[:, :row_count].reshape(blocked)
    middle = padded[:, block_size : row_count + block_size].reshape(blocked)
    following = padded[:, 2 * block_size :].reshape(blocked)
    window = jnp.concatenate((before, middle, following), axis=2)
    slot_ids = jnp.arange(3 * block_size, dtype=jnp.int32) // block_size
    block_ids = jnp.arange(block_count, dtype=jnp.int32)
    masked = (slot_ids[None, :] == 0) & (block_ids[:, None] == 0) & (position == 0) | (
        slot_ids[None, :] == 2
    ) & (block_ids[:, None] == block_count - 1) & (position == axis_size - 1)
    key_bias = jnp.where(masked, neg_large, 0.0).astype(jnp.float32)
    fine_q = queries.reshape(block_count, block_size, head_count, head_size)
    results = [attend(fine_q, window[0], window[1], key_bias, scaling)]
    level_q = queries
    level_q = halve_rows(level_q, 0)
    own_block = halve_rows(keyval, 1)
    for bit_index in range(axis_bits):
        partner = swap_sibling(own_block, bit_index)
        level_rows = level_q.shape[0]
        kv_blocks = partner.reshape(2, 1, block_size, head_count, head_size)
        results.append(
            attend(
                level_q.reshape(1, level_rows, head_count, head_size),
                kv_blocks[0],
                kv_blocks[1],
                None,
                scaling,
            )
        )
        if bit_index + 1 < axis_bits:
            level_q = halve_rows(level_q, 0)
        if bit_index + 1 < axis_bits:
            upper_bit = position // (1 << bit_index) % 2
            lower_half = jnp.where(upper_bit == 0, own_block, partner)
            upper_half = jnp.where(upper_bit == 0, partner, own_block)
            own_block = halve_rows(jnp.concatenate((lower_half, upper_half), axis=1), 1)
    return combine(results).reshape(row_count, feature_count)


def solution(mesh):
    return jax.shard_map(
        on_device,
        mesh=mesh,
        in_specs=(P(("streams", "seq"), None), P(None, ("streams", "seq"), None)),
        out_specs=P(("streams", "seq"), None),
        check_vma=False,
    )
```

profile of v0, /device:TPU:0, one launch (start us, length us, event | category | flops | bytes accessed | tf_op | source)
XLA Modules:
  0.0 210.3 jit_solution(6965888495721618806)
XLA Ops:
  0.0 3.2 %fusion.89 = (bf16[2,128,2048]{2,1,0:T(8,128)(2,1)}, bf16[2,128,2048]{2,1,0:T(8,128)(2,1)}) fusion(bf16[2,256,2048]{2,1,0:T(8,128)(2,1)} %param.23), kind=kLoop, calls=%fused_computation.148 | loop fusion | bytes 4194304 | tf_op jit(solution)/shard_map/slice | solution.py:29
  3.2 1.3 collective-permute-start.5
  4.5 4.0 %collective-permute-start.4 = (bf16[2,128,2048]{2,1,0:T(8,128)(2,1)}, bf16[2,128,2048]{2,1,0:T(8,128)(2,1)}, u32[]{:S(2)}, u32[]{:S(2)}) collective-permute-start(bf16[2,128,2048]{2,1,0:T(8,128)(2,1)} %get-tuple-element.148), channel_id=1, source_target_pairs={{0,1},{1,2},{2,3},{3,4},{4,5},{5,6},{6,7},{7,8},{8,9},{9,10},{10,1... | collective-permute-start | bytes 3145736 | tf_op jit(solution)/shard_map/ppermute | solution.py:26
  8.6 2.2 %copy.272 = f32[2,256,2048]{2,0,1:T(2,128)S(1)} copy(bf16[2,256,2048]{2,1,0:T(8,128)(2,1)S(1)} %copy-done.2) | data formatting | bytes 6291456 | tf_op jit(solution)/shard_map/convert_element_type | solution.py:37
  10.8 3.4 %fusion.22 = bf16[2,128,2048]{2,0,1:T(2,128)(2,1)} fusion(f32[2,128,2,2048]{3,0,2,1:T(2,128)S(1)} %bitcast.386), kind=kLoop, calls=%fused_computation.38 | loop fusion | flops 1572864 | bytes 5242880 | tf_op jit(solution)/shard_map/convert_element_type | solution.py:39
  14.1 1.6 collective-permute-start
  15.7 3.3 %reshape.751 = f32[128,2,2048]{2,1,0:T(2,128)} reshape(bf16[256,2048]{1,0:T(8,128)(2,1)} %param.22) | data formatting | bytes 3145728 | tf_op jit(solution)/shard_map/convert_element_type | solution.py:37
  19.1 4.4 %fusion.88 = (f32[128,1,2048]{2,1,0:T(1,128)S(1)}, f32[128,1,2048]{2,1,0:T(1,128)S(1)}) fusion(f32[128,2,2048]{2,1,0:T(2,128)} %reshape.751), kind=kLoop, calls=%fused_computation.147 | loop fusion | bytes 4194304 | tf_op jit(solution)/shard_map/jit(_take) | solution.py:38
  23.4 1.5 fusion.34
  24.9 2.7 %reshape.752 = f32[64,2,2048]{2,1,0:T(2,128)} reshape(bf16[128,2048]{1,0:T(8,128)(2,1)} %fusion.34) | data formatting | bytes 1572864 | tf_op jit(solution)/shard_map/convert_element_type | solution.py:37
  27.6 2.6 %fusion.94 = (f32[64,1,2048]{2,1,0:T(1,128)S(1)}, f32[64,1,2048]{2,1,0:T(1,128)S(1)}) fusion(f32[64,2,2048]{2,1,0:T(2,128)} %reshape.752), kind=kLoop, calls=%fused_computation.153 | loop fusion | bytes 2097152 | tf_op jit(solution)/shard_map/jit(_take) | solution.py:38
  30.6 1.1 reshape.753
  31.7 1.7 fusion.95
  33.7 2.1 copy.294
  35.7 2.5 %copy.370 = bf16[32,8,16,128]{3,2,1,0:T(8,128)(2,1)} copy(bf16[32,8,16,128]{3,1,2,0:T(8,128)(2,1)} %bitcast.404) | data formatting | bytes 2097152
  38.2 2.0 copy.368
  40.2 0.9 reshape.754
  41.7 2.0 fusion.96
  43.7 1.9 pad_maximum_fusion
  45.6 1.9 copy.369
  48.1 1.9 copy_dynamic-update-slice_fusion.2
  50.0 2.3 %fusion.93 = (bf16[1,128,2048]{2,0,1:T(2,128)(2,1)}, bf16[1,128,2048]{2,0,1:T(2,128)(2,1)S(1)}) fusion(bf16[2,128,2048]{2,0,1:T(2,128)(2,1)S(1)} %collective-permute-done), kind=kLoop, calls=%fused_computation.152 | loop fusion | bytes 2097152 | tf_op jit(solution)/shard_map/slice | solution.py:128
  52.3 0.8 copy.295
  53.1 4.0 %broadcast_select_fusion.1 = (bf16[2,128,2048]{2,0,1:T(2,128)(2,1)S(1)}, bf16[2,128,2048]{2,0,1:T(2,128)(2,1)S(1)}) fusion(bf16[2,128,2048]{2,0,1:T(2,128)(2,1)S(1)} %collective-permute-done, pred[]{:T(512)S(6)} %eq.60, f32[2,128,2,2048]{3,0,2,1:T(2,128)} %bitcast.387), kind=kLoop, calls=%fused_computation.47 | loop fusion | flops 2621440 | bytes 7340033 | tf_op jit(solution)/shard_map/jit(_where)/select_n | solution.py:137
  57.1 2.7 %pad_maximum_fusion.2 = bf16[2,256,2048]{2,0,1:T(2,128)(2,1)S(1)} fusion(bf16[2,128,2048]{2,0,1:T(2,128)(2,1)S(1)} %get-tuple-element.142, bf16[2,128,2048]{2,0,1:T(2,128)(2,1)S(1)} %get-tuple-element.141), kind=kLoop, calls=%fused_computation.40 | loop fusion | flops 1048576 | bytes 4194304 | tf_op jit(solution)/shard_map/concatenate | solution.py:139
  59.8 2.1 %convert.8 = f32[2,128,2,2048]{3,0,2,1:T(2,128)S(1)} convert(bf16[2,128,2,2048]{3,0,2,1:T(2,128)(2,1)S(1)} %bitcast.389) | non-fusion elementwise | flops 1048576 | bytes 6291456 | tf_op jit(solution)/shard_map/convert_element_type | solution.py:37
  62.0 2.0 fusion.19
  64.0 2.4 %collective-permute-start.1 = (bf16[2,128,2048]{2,0,1:T(2,128)(2,1)S(1)}, bf16[2,128,2048]{2,0,1:T(2,128)(2,1)S(1)}, u32[]{:S(2)}, u32[]{:S(2)}) collective-permute-start(bf16[2,128,2048]{2,0,1:T(2,128)(2,1)S(1)} %fusion.19), channel_id=1, source_target_pairs={{0,2},{1,3},{2,0},{3,1},{4,6},{5,7},{6,4},{7,5},{8,10},{9,11},{10,... | collective-permute-start | bytes 3145736 | tf_op jit(solution)/shard_map/ppermute | solution.py:18
  67.2 0.9 copy-done.5
  70.0 1.0 bitcast_reduce_fusion
  71.1 3.2 %fusion.23 = f32[2,128,16,128]{1,3,2,0:T(8,128)} fusion(f32[2,16,384,128]{3,2,1,0:T(8,128)S(1)} %get-tuple-element.167, f32[2,16,128]{2,1,0:T(8,128)S(1)} %get-tuple-element.166, f32[2,384]{1,0:T(2,128)S(1)} %copy-done.20, bf16[2,2,384,16,128]{4,2,3,1,0:T(8,128)(2,1)S(1)} %copy_dynamic-update-slice_fusion), kind=kOutput, calls=%fused_computation.52 | convolution fusion | flops 408944640 | bytes 11553792 | tf_op jit(solution)/shard_map/ghqk,gkhe->gqhe/dot_general | solution.py:52
  74.3 15.5 %collective-permute-done.1 = bf16[2,128,2048]{2,0,1:T(2,128)(2,1)S(1)} collective-permute-done((bf16[2,128,2048]{2,0,1:T(2,128)(2,1)S(1)}, bf16[2,128,2048]{2,0,1:T(2,128)(2,1)S(1)}, u32[]{:S(2)}, u32[]{:S(2)}) %collective-permute-start.1) | collective-permute-done | bytes 1048608 | tf_op jit(solution)/shard_map/ppermute | solution.py:18
  89.8 2.4 %broadcast_select_fusion.3 = (bf16[2,128,2048]{2,0,1:T(2,128)(2,1)S(1)}, bf16[2,128,2048]{2,0,1:T(2,128)(2,1)S(1)}) fusion(bf16[2,128,2048]{2,0,1:T(2,128)(2,1)S(1)} %collective-permute-done.1, pred[]{:T(512)S(6)} %eq.59, f32[2,128,2,2048]{3,0,2,1:T(2,128)S(1)} %convert.8), kind=kLoop, calls=%fused_computation.49 | loop fusion | flops 2621440 | bytes 7340033 | tf_op jit(solution)/shard_map/jit(_where)/select_n | solution.py:137
  92.2 2.7 %pad_maximum_fusion.3 = bf16[2,256,2048]{2,0,1:T(2,128)(2,1)S(1)} fusion(bf16[2,128,2048]{2,0,1:T(2,128)(2,1)S(1)} %get-tuple-element.140, bf16[2,128,2048]{2,0,1:T(2,128)(2,1)S(1)} %get-tuple-element.139), kind=kLoop, calls=%fused_computation.41 | loop fusion | flops 1048576 | bytes 4194304 | tf_op jit(solution)/shard_map/concatenate | solution.py:139
  94.9 2.1 %convert.9 = f32[2,128,2,2048]{3,0,2,1:T(2,128)S(1)} convert(bf16[2,128,2,2048]{3,0,2,1:T(2,128)(2,1)S(1)} %bitcast.390) | non-fusion elementwise | flops 1048576 | bytes 6291456 | tf_op jit(solution)/shard_map/convert_element_type | solution.py:37
  97.1 2.9 %fusion.16 = bf16[2,128,2048]{2,0,1:T(2,128)(2,1)} fusion(f32[2,128,2,2048]{3,0,2,1:T(2,128)S(1)} %convert.9), kind=kLoop, calls=%fused_computation.28 | loop fusion | flops 1572864 | bytes 5242880 | tf_op jit(solution)/shard_map/convert_element_type | solution.py:39
  99.9 1.6 collective-permute-start.2
  102.3 3.5 %copy.319 = bf16[1,128,2048]{1,2,0:T(8,128)(2,1)} copy(bf16[1,128,2048]{2,0,1:T(2,128)(2,1)} %get-tuple-element.155) | data formatting | bytes 1048576 | tf_op jit(solution)/shard_map/slice | solution.py:128
  105.8 3.1 %copy.325 = f32[2,128,16,128]{3,2,1,0:T(8,128)} copy(f32[2,128,16,128]{1,3,2,0:T(8,128)} %fusion.23) | data formatting | bytes 4194304 | tf_op jit(solution)/shard_map/ghqk,gkhe->gqhe/transpose | solution.py:52
  108.8 4.9 %fusion.1 = f32[2,16,128]{2,1,0:T(8,128)} fusion(f32[2,16,384,128]{3,2,1,0:T(8,128)} %copy-done.3, f32[2,16,128]{2,1,0:T(8,128)S(1)} %get-tuple-element.166, f32[2,384]{1,0:T(2,128)} %or_select_fusion), kind=kLoop, calls=%fused_computation.4 | loop fusion | flops 6287360 | bytes 6327296 | tf_op jit(solution)/shard_map/reduce_sum | solution.py:51
  113.7 2.4 %fusion.92 = (bf16[1,128,2048]{2,0,1:T(2,128)(2,1)}, bf16[1,128,2048]{2,0,1:T(2,128)(2,1)}) fusion(bf16[2,128,2048]{2,0,1:T(2,128)(2,1)S(1)} %collective-permute-done.1), kind=kLoop, calls=%fused_computation.151 | loop fusion | bytes 2097152 | tf_op jit(solution)/shard_map/slice | solution.py:128
  116.2 3.5 %copy.289 = bf16[1,128,2048]{1,2,0:T(8,128)(2,1)} copy(bf16[1,128,2048]{2,0,1:T(2,128)(2,1)} %get-tuple-element.154) | data formatting | bytes 1048576 | tf_op jit(solution)/shard_map/slice | solution.py:127
  119.6 5.0 %collective-permute-done.2 = bf16[2,128,2048]{2,0,1:T(2,128)(2,1)S(1)} collective-permute-done((bf16[2,128,2048]{2,0,1:T(2,128)(2,1)}, bf16[2,128,2048]{2,0,1:T(2,128)(2,1)S(1)}, u32[]{:S(2)}, u32[]{:S(2)}) %collective-permute-start.2) | collective-permute-done | bytes 1048608 | tf_op jit(solution)/shard_map/ppermute | solution.py:18
  124.7 4.2 %broadcast_select_fusion.5 = (bf16[2,128,2048]{2,0,1:T(2,128)(2,1)S(1)}, bf16[2,128,2048]{2,0,1:T(2,128)(2,1)S(1)}) fusion(bf16[2,128,2048]{2,0,1:T(2,128)(2,1)S(1)} %collective-permute-done.2, pred[]{:T(512)S(6)} %eq.58, f32[2,128,2,2048]{3,0,2,1:T(2,128)} %copy-done.1), kind=kLoop, calls=%fused_computation.51 | loop fusion | flops 2621440 | bytes 7340033 | tf_op jit(solution)/shard_map/jit(_where)/select_n | solution.py:137
  128.9 2.7 %pad_maximum_fusion.4 = bf16[2,256,2048]{2,0,1:T(2,128)(2,1)S(1)} fusion(bf16[2,128,2048]{2,0,1:T(2,128)(2,1)S(1)} %get-tuple-element.138, bf16[2,128,2048]{2,0,1:T(2,128)(2,1)S(1)} %get-tuple-element.137), kind=kLoop, calls=%fused_computation.42 | loop fusion | flops 1048576 | bytes 4194304 | tf_op jit(solution)/shard_map/concatenate | solution.py:139
  131.6 2.1 %convert.10 = f32[2,128,2,2048]{3,0,2,1:T(2,128)S(1)} convert(bf16[2,128,2,2048]{3,0,2,1:T(2,128)(2,1)S(1)} %bitcast.391) | non-fusion elementwise | flops 1048576 | bytes 6291456 | tf_op jit(solution)/shard_map/convert_element_type | solution.py:37
  133.8 2.8 %fusion.13 = bf16[2,128,2048]{2,0,1:T(2,128)(2,1)} fusion(f32[2,128,2,2048]{3,0,2,1:T(2,128)S(1)} %convert.10), kind=kLoop, calls=%fused_computation.23 | loop fusion | flops 1572864 | bytes 5242880 | tf_op jit(solution)/shard_map/convert_element_type | solution.py:39
  136.6 2.6 %collective-permute-start.3 = (bf16[2,128,2048]{2,0,1:T(2,128)(2,1)}, bf16[2,128,2048]{2,0,1:T(2,128)(2,1)}, u32[]{:S(2)}, u32[]{:S(2)}) collective-permute-start(bf16[2,128,2048]{2,0,1:T(2,128)(2,1)} %fusion.13), channel_id=1, source_target_pairs={{0,8},{1,9},{2,10},{3,11},{4,12},{5,13},{6,14},{7,15},{8,0},{9,1},... | collective-permute-start | bytes 3145736 | tf_op jit(solution)/shard_map/ppermute | solution.py:18
  139.2 1.0 fusion.98
  140.1 3.5 %copy.315 = bf16[1,128,2048]{1,2,0:T(8,128)(2,1)} copy(bf16[1,128,2048]{2,0,1:T(2,128)(2,1)} %get-tuple-element.153) | data formatting | bytes 1048576 | tf_op jit(solution)/shard_map/slice | solution.py:128
  143.6 1.7 fusion.43
  145.3 2.4 %fusion.91 = (bf16[1,128,2048]{2,0,1:T(2,128)(2,1)}, bf16[1,128,2048]{2,0,1:T(2,128)(2,1)}) fusion(bf16[2,128,2048]{2,0,1:T(2,128)(2,1)S(1)} %collective-permute-done.2), kind=kLoop, calls=%fused_computation.150 | loop fusion | bytes 2097152 | tf_op jit(solution)/shard_map/slice | solution.py:128
  147.7 3.6 %copy.313 = bf16[1,128,2048]{1,2,0:T(8,128)(2,1)} copy(bf16[1,128,2048]{2,0,1:T(2,128)(2,1)} %get-tuple-element.151) | data formatting | bytes 1048576 | tf_op jit(solution)/shard_map/slice | solution.py:128
  151.3 0.8 copy.284
  152.5 0.9 fusion.52
  153.4 30.5 %collective-permute-done.3 = bf16[2,128,2048]{2,0,1:T(2,128)(2,1)} collective-permute-done((bf16[2,128,2048]{2,0,1:T(2,128)(2,1)}, bf16[2,128,2048]{2,0,1:T(2,128)(2,1)}, u32[]{:S(2)}, u32[]{:S(2)}) %collective-permute-start.3) | collective-permute-done | bytes 1048608 | tf_op jit(solution)/shard_map/ppermute | solution.py:18
  183.9 4.1 %fusion.90 = (bf16[1,128,2048]{2,0,1:T(2,128)(2,1)}, bf16[1,128,2048]{2,0,1:T(2,128)(2,1)S(1)}) fusion(bf16[2,128,2048]{2,0,1:T(2,128)(2,1)} %collective-permute-done.3), kind=kLoop, calls=%fused_computation.149 | loop fusion | bytes 2097152 | tf_op jit(solution)/shard_map/slice | solution.py:128
  188.0 3.5 %copy.311 = bf16[1,128,2048]{1,2,0:T(8,128)(2,1)} copy(bf16[1,128,2048]{2,0,1:T(2,128)(2,1)} %get-tuple-element.149) | data formatting | bytes 1048576 | tf_op jit(solution)/shard_map/slice | solution.py:128
  191.5 0.8 copy.280
  192.4 1.3 fusion.100
  193.9 1.5 convolution_bitcast_fusion.3
  199.8 0.9 fusion.29
  201.7 1.4 fusion.27
  206.3 3.8 %fusion.9 = bf16[256,2048]{1,0:T(8,128)(2,1)} fusion(f32[32,8,16,128]{3,2,1,0:T(8,128)S(1)} %bitcast.400, f32[32,8,16,128]{3,2,1,0:T(8,128)S(1)} %bitcast.395, f32[32,8,16,128]{3,2,1,0:T(8,128)S(1)} %bitcast.397, f32[32,8,16,128]{3,2,1,0:T(8,128)S(1)} %bitcast.396, f32[32,8,16,128]{3,2,1,0:T(8,128)S(1)} %bitcast.398), kind=kLoop, calls=%fused_computation.14 | loop fusion | flops 2621440 | bytes 11534336 | tf_op jit(solution)/shard_map/convert_element_type | solution.py:85
  (104 shorter events, 14.3 us)
Async XLA Ops:
  0.0 8.6 %copy-start.2 = (bf16[2,256,2048]{2,1,0:T(8,128)(2,1)S(1)}, bf16[2,256,2048]{2,1,0:T(8,128)(2,1)}, u32[]{:S(2)}) copy-start(bf16[2,256,2048]{2,1,0:T(8,128)(2,1)} %param.23) | copy-start | bytes 6291460
  3.2 40.5 %collective-permute-start.5 = (bf16[2,128,2048]{2,1,0:T(8,128)(2,1)}, bf16[2,128,2048]{2,1,0:T(8,128)(2,1)}, u32[]{:S(2)}, u32[]{:S(2)}) collective-permute-start(bf16[2,128,2048]{2,1,0:T(8,128)(2,1)} %get-tuple-element.147), channel_id=1, source_target_pairs={{1,0},{2,1},{3,2},{4,3},{5,4},{6,5},{7,6},{8,7},{9,8},{10,9},{11,1... | collective-permute-start | bytes 3145736 | tf_op jit(solution)/shard_map/ppermute | solution.py:29
  4.5 39.2 %collective-permute-start.4 = (bf16[2,128,2048]{2,1,0:T(8,128)(2,1)}, bf16[2,128,2048]{2,1,0:T(8,128)(2,1)}, u32[]{:S(2)}, u32[]{:S(2)}) collective-permute-start(bf16[2,128,2048]{2,1,0:T(8,128)(2,1)} %get-tuple-element.148), channel_id=1, source_target_pairs={{0,1},{1,2},{2,3},{3,4},{4,5},{5,6},{6,7},{7,8},{8,9},{9,10},{10,1... | collective-permute-start | bytes 3145736 | tf_op jit(solution)/shard_map/ppermute | solution.py:26
  10.8 3.4 %copy-start = (f32[2,256,2048]{2,0,1:T(2,128)}, f32[2,256,2048]{2,0,1:T(2,128)S(1)}, u32[]{:S(2)}) copy-start(f32[2,256,2048]{2,0,1:T(2,128)S(1)} %copy.272) | copy-start | bytes 12582916
  14.1 35.9 %collective-permute-start = (bf16[2,128,2048]{2,0,1:T(2,128)(2,1)}, bf16[2,128,2048]{2,0,1:T(2,128)(2,1)S(1)}, u32[]{:S(2)}, u32[]{:S(2)}) collective-permute-start(bf16[2,128,2048]{2,0,1:T(2,128)(2,1)} %fusion.22), channel_id=1, source_target_pairs={{0,1},{1,0},{2,3},{3,2},{4,5},{5,4},{6,7},{7,6},{8,9},{9,8},{10,11... | collective-permute-start | bytes 3145736 | tf_op jit(solution)/shard_map/ppermute | solution.py:18
  57.1 9.3 %slice-start = ((s8[6291456]{0:T(1024)(128)(4,1)}), s8[4194304]{0:T(1024)(128)(4,1)S(1)}, s32[]{:S(2)}) async-start(s8[6291456]{0:T(1024)(128)(4,1)} %bitcast.402), calls=%async_computation | async-start | bytes 8388608
  59.8 6.6 %slice-start.1 = ((s8[6291456]{0:T(1024)(128)(4,1)}), s8[2097152]{0:T(1024)(128)(4,1)S(1)}, s32[]{:S(2)}) async-start(s8[6291456]{0:T(1024)(128)(4,1)} %bitcast.402), calls=%async_computation.1 | async-start | bytes 4194304
  62.0 4.5 %copy-start.4 = (bf16[64,8,16,128]{3,2,1,0:T(8,128)(2,1)S(1)}, bf16[64,8,16,128]{3,2,1,0:T(8,128)(2,1)}, u32[]{:S(2)}) copy-start(bf16[64,8,16,128]{3,2,1,0:T(8,128)(2,1)} %copy.368) | copy-start | bytes 6291460
  64.0 25.7 %collective-permute-start.1 = (bf16[2,128,2048]{2,0,1:T(2,128)(2,1)S(1)}, bf16[2,128,2048]{2,0,1:T(2,128)(2,1)S(1)}, u32[]{:S(2)}, u32[]{:S(2)}) collective-permute-start(bf16[2,128,2048]{2,0,1:T(2,128)(2,1)S(1)} %fusion.19), channel_id=1, source_target_pairs={{0,2},{1,3},{2,0},{3,1},{4,6},{5,7},{6,4},{7,5},{8,10},{9,11},{10,... | collective-permute-start | bytes 3145736 | tf_op jit(solution)/shard_map/ppermute | solution.py:18
  66.5 1.6 copy-start.5
  68.1 1.0 copy-start.11
  68.7 1.3 copy-start.12
  68.8 1.3 copy-start.20
  69.5 32.1 %copy-start.14 = (f32[16,128]{1,0:T(8,128)}, f32[16,128]{1,0:T(8,128)S(1)}, u32[]{:S(2)}) copy-start(f32[16,128]{1,0:T(8,128)S(1)} %get-tuple-element.168) | copy-start | bytes 24580
  71.0 3.2 %copy-start.3 = (f32[2,16,384,128]{3,2,1,0:T(8,128)}, f32[2,16,384,128]{3,2,1,0:T(8,128)S(1)}, u32[]{:S(2)}) copy-start(f32[2,16,384,128]{3,2,1,0:T(8,128)S(1)} %get-tuple-element.167) | copy-start | bytes 18874372
  97.1 2.9 %copy-start.1 = (f32[2,128,2,2048]{3,0,2,1:T(2,128)}, f32[2,128,2,2048]{3,0,2,1:T(2,128)S(1)}, u32[]{:S(2)}) copy-start(f32[2,128,2,2048]{3,0,2,1:T(2,128)S(1)} %convert.9) | copy-start | bytes 12582916
  99.9 24.7 %collective-permute-start.2 = (bf16[2,128,2048]{2,0,1:T(2,128)(2,1)}, bf16[2,128,2048]{2,0,1:T(2,128)(2,1)S(1)}, u32[]{:S(2)}, u32[]{:S(2)}) collective-permute-start(bf16[2,128,2048]{2,0,1:T(2,128)(2,1)} %fusion.16), channel_id=1, source_target_pairs={{0,4},{1,5},{2,6},{3,7},{4,0},{5,1},{6,2},{7,3},{8,12},{9,13},{10,... | collective-permute-start | bytes 3145736 | tf_op jit(solution)/shard_map/ppermute | solution.py:18
  133.7 5.4 %copy-start.8 = (bf16[1,128,2048]{1,2,0:T(8,128)(2,1)S(1)}, bf16[1,128,2048]{1,2,0:T(8,128)(2,1)}, u32[]{:S(2)}) copy-start(bf16[1,128,2048]{1,2,0:T(8,128)(2,1)} %copy.289) | copy-start | bytes 1572868
  136.6 47.3 %collective-permute-start.3 = (bf16[2,128,2048]{2,0,1:T(2,128)(2,1)}, bf16[2,128,2048]{2,0,1:T(2,128)(2,1)}, u32[]{:S(2)}, u32[]{:S(2)}) collective-permute-start(bf16[2,128,2048]{2,0,1:T(2,128)(2,1)} %fusion.13), channel_id=1, source_target_pairs={{0,8},{1,9},{2,10},{3,11},{4,12},{5,13},{6,14},{7,15},{8,0},{9,1},... | collective-permute-start | bytes 3145736 | tf_op jit(solution)/shard_map/ppermute | solution.py:18
  147.7 3.6 %copy-start.7 = (bf16[1,128,2048]{2,0,1:T(2,128)(2,1)S(1)}, bf16[1,128,2048]{2,0,1:T(2,128)(2,1)}, u32[]{:S(2)}) copy-start(bf16[1,128,2048]{2,0,1:T(2,128)(2,1)} %get-tuple-element.152) | copy-start | bytes 1572868
  152.5 0.9 copy-start.17
  188.0 4.4 %copy-start.13 = (f32[16,1,2048]{2,1,0:T(1,128)S(1)}, f32[16,1,2048]{2,1,0:T(1,128)}, u32[]{:S(2)}) copy-start(f32[16,1,2048]{2,1,0:T(1,128)} %get-tuple-element.161) | copy-start | bytes 393220
  192.4 6.8 %copy-start.10 = (bf16[1,128,2048]{1,2,0:T(8,128)(2,1)S(1)}, bf16[1,128,2048]{1,2,0:T(8,128)(2,1)}, u32[]{:S(2)}) copy-start(bf16[1,128,2048]{1,2,0:T(8,128)(2,1)} %copy.313) | copy-start | bytes 1572868
  193.7 5.5 %copy-start.18 = (f32[16,32]{1,0:T(8,128)S(1)}, f32[16,32]{1,0:T(8,128)}, u32[]{:S(2)}) copy-start(f32[16,32]{1,0:T(8,128)} %copy-done.17) | copy-start | bytes 6148
  196.4 3.4 %copy-start.9 = (bf16[1,128,2048]{1,2,0:T(8,128)(2,1)S(1)}, bf16[1,128,2048]{1,2,0:T(8,128)(2,1)}, u32[]{:S(2)}) copy-start(bf16[1,128,2048]{1,2,0:T(8,128)(2,1)} %copy.315) | copy-start | bytes 1572868
  196.4 3.4 %copy-start.16 = (f32[16,64]{1,0:T(8,128)S(1)}, f32[16,64]{1,0:T(8,128)}, u32[]{:S(2)}) copy-start(f32[16,64]{1,0:T(8,128)} %get-tuple-element.170) | copy-start | bytes 12292
  201.0 0.7 copy-start.15
  201.7 1.9 copy-start.19
  204.7 1.6 copy-start.6
where the time goes:
time: 214 us; the launch traced here: 210 us
  local copies, waits for them, and re-layouts  78.5 us (37%)
  other arithmetic  55.1 us (26%)
  waiting for transfers between devices  51.1 us (24%)
  starting transfers between devices  13.5 us (6%)
  matrix products  11.3 us (5%)
    ppermute x4, waiting for transfers between devices, swapped(): lax.ppermute(array, axis, [(i, i ^ 1 << stride) for i in range(lax.axis_s...  51.1 us
    slice x8, local copies, waits for them, and re-layouts, on_device(): kv_blocks[1]  25.3 us
    convert_element_type x7, other arithmetic, halve_rows(): return pooled.astype(jnp.bfloat16)  13 us
    unnamed x52, local copies, waits for them, and re-layouts  12 us
    select_n x3, other arithmetic, on_device(): lower_half = jnp.where(upper_bit == 0, own_block, partner)  10.6 us
    convert_element_type x5, local copies, waits for them, and re-layouts, halve_rows(): widened = pair_rows.reshape(new_shape).astype(jnp.float32)  10.2 us
    reduce_sum x5, other arithmetic, attend(): row_sum = jnp.sum(expons, axis=3)  8.4 us
    ppermute x4, starting transfers between devices, swapped(): lax.ppermute(array, axis, [(i, i ^ 1 << stride) for i in range(lax.axis_s...  8.19 us
  transfers between devices with their start and end apart: 6, of which 3 were waited for; matrix products, arithmetic and copies ran while one was open for 37% of the time, Pallas kernels for 0%

commit v1 on v0

v1 whole, which is shorter than its diff:
```python
import functools
import math

import jax
import jax.numpy as jnp
from jax import lax
from jax.experimental import pallas as pl
from jax.experimental.pallas import tpu as pltpu
from jax.sharding import PartitionSpec as P

HEADS = 16
HEAD_DIM = 128
BLOCK = 128
GROUPS = 4
neg_large = -1e30
log_two = 0.6931471805599453
to_log2 = 1.0 / (math.sqrt(HEAD_DIM) * log_two)


def dot(left, right):
    return lax.dot_general(
        left, right, (((1,), (0,)), ((), ())), preferred_element_type=jnp.float32
    )


def dot_t(left, right):
    return lax.dot_general(
        left, right, (((1,), (1,)), ((), ())), preferred_element_type=jnp.float32
    )


def iota(shape, dim):
    return lax.broadcasted_iota(jnp.int32, shape, dim)


def halves(rows):
    shape = (rows // 2, rows)
    return jnp.where(iota(shape, 1) >> 1 == iota(shape, 0), 0.5, 0.0).astype(jnp.bfloat16)


def halve(rows):
    return dot(halves(rows.shape[0]), rows).astype(jnp.bfloat16)


def repeated_halve(rows, level):
    count = rows.shape[0]
    shape = (count, count)
    first = iota(shape, 0) >> level << level
    hit = (iota(shape, 1) == first) | (iota(shape, 1) == first + (1 << level - 1))
    return dot(jnp.where(hit, 0.5, 0.0).astype(jnp.bfloat16), rows).astype(jnp.bfloat16)


def pool_kernel(kv_ref, *out_refs):
    for which in range(2):
        rows = halve(kv_ref[which])
        for out_ref in out_refs:
            rows = halve(rows)
            out_ref[which] = rows


def pool(kv, first, count):
    rows = kv.shape[1]
    out_rows = [rows >> (first + step) for step in range(count)]
    return pl.pallas_call(
        pool_kernel if first == 2 else pool_once_kernel,
        grid=(2,),
        in_specs=[pl.BlockSpec((2, rows, kv.shape[2] // 2), lambda g: (0, 0, g))],
        out_specs=[
            pl.BlockSpec((2, out, kv.shape[2] // 2), lambda g: (0, 0, g)) for out in out_rows
        ],
        out_shape=[jax.ShapeDtypeStruct((2, out, kv.shape[2]), kv.dtype) for out in out_rows],
        name="pool",
    )(kv)


def pool_once_kernel(kv_ref, *out_refs):
    for which in range(2):
        rows = kv_ref[which]
        for out_ref in out_refs:
            rows = halve(rows)
            out_ref[which] = rows


def softmax_parts(queries, keys, values, state):
    exponents = []
    for query, (key, addend) in zip(queries, keys):
        exponent = dot_t(query, key) * to_log2
        if addend is not None:
            exponent = exponent + addend
        exponents.append(exponent)
    peak = functools.reduce(
        jnp.maximum, [jnp.max(exponent, axis=1, keepdims=True) for exponent in exponents]
    )
    if state is not None:
        old_peak, old_total, old_sum = state
        peak = jnp.maximum(peak, old_peak)
    expons = [jnp.exp2(exponent - peak) for exponent in exponents]
    total = functools.reduce(
        jnp.add, [jnp.sum(expon, axis=1, keepdims=True) for expon in expons]
    )
    weights = jnp.concatenate([expon.astype(jnp.bfloat16) for expon in expons], axis=1)
    weighted = dot(weights, jnp.concatenate(values, axis=0))
    if state is not None:
        factor = jnp.exp2(old_peak - peak)
        total = total + factor * old_total
        weighted = weighted + factor * old_sum
    return peak, total, weighted


def own_kernel(pos_ref, q_ref, kv_ref, sum_ref, stat_ref, edge_ref):
    per_group = q_ref.shape[1] // HEAD_DIM
    rows = q_ref.shape[0]
    lane = iota((rows, 128), 1)
    stats = jnp.zeros((rows, 128), jnp.float32)
    for head in range(per_group):
        cols = pl.ds(head * HEAD_DIM, HEAD_DIM)
        peak, total, weighted = softmax_parts(
            [q_ref[:, cols]], [(kv_ref[0, :, cols], None)], [kv_ref[1, :, cols]], None
        )
        sum_ref[:, cols] = weighted
        stats = jnp.where(lane == head, peak, stats)
        stats = jnp.where(lane == head + 64, total, stats)
    stat_ref[0] = stats
    outer = pl.ds(pl.multiple_of(pos_ref[0] * BLOCK, BLOCK), BLOCK)
    edge_ref[...] = kv_ref[:, outer, :]


def near_kernel(
    pos_ref, q_ref, inner_ref, mine_ref, theirs_ref, sum_ref, stat_ref, *out_refs
):
    new_sum_ref, new_stat_ref = out_refs[:2]
    up_refs = out_refs[2:]
    per_group = q_ref.shape[1] // HEAD_DIM
    rows = q_ref.shape[0]
    core = pos_ref[0]
    up = q_ref[...]
    ups = []
    for level in range(1, 3 + len(up_refs)):
        up = repeated_halve(up, level)
        ups.append(up)
    for up_ref, up in zip(up_refs, ups[2:]):
        up_ref[...] = up
    level_keys = halve(inner_ref[0])
    level_values = halve(inner_ref[1])
    lane = iota((BLOCK, 128), 1)
    up_1 = ups[0]
    up_2 = ups[1]
    inner_rows = pl.ds(pl.multiple_of(core * BLOCK, BLOCK), BLOCK)
    for block in range(2):
        span = slice(block * BLOCK, (block + 1) * BLOCK)
        stats = jnp.zeros((BLOCK, 128), jnp.float32)
        bias = jnp.where(core == 1 - block, 0.0, neg_large)
        for head in range(per_group):
            cols = slice(head * HEAD_DIM, (head + 1) * HEAD_DIM)
            state = (
                stat_ref[0, span, head : head + 1],
                stat_ref[0, span, head + 64 : head + 65],
                sum_ref[span, cols],
            )
            peak, total, weighted = softmax_parts(
                [q_ref[span, cols], up_1[span, cols], up_2[span, cols]],
                [
                    (inner_ref[0, inner_rows, cols], bias),
                    (level_keys[:, cols], 1.0),
                    (jnp.concatenate([mine_ref[0, :, cols], theirs_ref[0, :, cols]], 0), 2.0),
                ],
                [
                    inner_ref[1, inner_rows, cols],
                    level_values[:, cols],
                    mine_ref[1, :, cols],
                    theirs_ref[1, :, cols],
                ],
                state,
            )
            new_sum_ref[span, cols] = weighted
            stats = jnp.where(lane == head, peak, stats)
            stats = jnp.where(lane == head + 64, total, stats)
        new_stat_ref[0, span, :] = stats


def far_kernel(levels, pos_ref, q_ref, edge_ref, mine_ref, theirs_ref, sum_ref, stat_ref, *refs):
    out_ref = refs[-1]
    up_refs = refs[:levels]
    more_refs = refs[levels:-1]
    per_group = q_ref.shape[1] // HEAD_DIM
    core = pos_ref[0]
    for block in range(2):
        span = slice(block * BLOCK, (block + 1) * BLOCK)
        bias = jnp.where((core == block) & (pos_ref[1] == 1), 0.0, neg_large)
        for head in range(per_group):
            cols = slice(head * HEAD_DIM, (head + 1) * HEAD_DIM)
            state = (
                stat_ref[0, span, head : head + 1],
                stat_ref[0, span, head + 64 : head + 65],
                sum_ref[span, cols],
            )
            queries = [q_ref[span, cols]] + [up_ref[span, cols] for up_ref in up_refs]
            keys = [(edge_ref[0, :, cols], bias)]
            values = [edge_ref[1, :, cols]]
            for level in range(2):
                part = slice(level * 64, (level + 1) * 64)
                keys.append(
                    (
                        jnp.concatenate(
                            [mine_ref[0, part, cols], theirs_ref[0, part, cols]], 0
                        ),
                        level + 3.0,
                    )
                )
                values += [mine_ref[1, part, cols], theirs_ref[1, part, cols]]
            for level, more_ref in enumerate(more_refs):
                keys.append((more_ref[0, :, cols], level + 5.0))
                values.append(more_ref[1, :, cols])
            _, total, weighted = softmax_parts(queries, keys, values, state)
            out_ref[span, cols] = (weighted / total).astype(out_ref.dtype)


def specs(arrays, width):
    out = []
    for array in arrays:
        if array.ndim == 2:
            out.append(pl.BlockSpec((array.shape[0], width), lambda g, pos: (0, g)))
        elif array.shape[2] == 128:
            out.append(pl.BlockSpec((1,) + array.shape[1:], lambda g, pos: (g, 0, 0)))
        else:
            out.append(pl.BlockSpec(array.shape[:2] + (width,), lambda g, pos: (0, 0, g)))
    return out


def grouped(kernel, position, inputs, outputs, name, flops):
    width = inputs[0].shape[1] // GROUPS
    return pl.pallas_call(
        kernel,
        grid_spec=pltpu.PrefetchScalarGridSpec(
            num_scalar_prefetch=1,
            grid=(GROUPS,),
            in_specs=specs(inputs, width),
            out_specs=specs(outputs, width),
        ),
        out_shape=outputs,
        cost_estimate=pl.CostEstimate(
            flops=flops, bytes_accessed=8 << 20, transcendentals=1 << 20
        ),
        name=name,
    )(position, *inputs)


def sent(array, stride):
    count = lax.axis_size("seq")
    return lax.ppermute(array, "seq", [(i, i ^ stride) for i in range(count)])


def halve_rows(pairs):
    wide = pairs.reshape(2, pairs.shape[1] // 2, 2, pairs.shape[2]).astype(jnp.float32)
    return ((wide[:, :, 0] + wide[:, :, 1]) * 0.5).astype(jnp.bfloat16)


def on_device(queries, keyval):
    count = lax.axis_size("seq")
    levels = count.bit_length() - 1
    index = lax.axis_index("seq")
    core = index % 2
    inside = jnp.where(core == 0, index > 0, index < count - 1)
    position = jnp.stack((core, inside.astype(core.dtype)))
    rows, features = queries.shape
    sums = jax.ShapeDtypeStruct((rows, features), jnp.float32)
    stats = jax.ShapeDtypeStruct((GROUPS, rows, 128), jnp.float32)
    like_q = jax.ShapeDtypeStruct(queries.shape, queries.dtype)

    own_2, own_3, own_4 = pool(keyval, 2, 3)
    side_2 = sent(own_2, 2)
    far_4 = sent(own_4, 8)
    far_4x = sent(own_4, 12)
    far_3 = sent(own_3, 4)
    inner = sent(keyval, 1)
    sum_0, stat_0, edge = grouped(
        own_kernel,
        position,
        [queries, keyval],
        [sums, stats, jax.ShapeDtypeStruct((2, BLOCK, features), keyval.dtype)],
        "own",
        2 << 30,
    )
    links = [(i, i + 1) for i in range(1, count - 1, 2)]
    edge = lax.ppermute(edge, "seq", links + [(j, i) for i, j in links])
    side_3, side_4 = pool(side_2, 1, 2)
    late_3 = sent(side_3, 4)
    late_4 = sent(side_4, 8)
    late_4x = sent(side_4, 12)
    other_2 = sent(side_2, 1)
    sum_1, stat_1, *ups = grouped(
        near_kernel,
        position,
        [queries, inner, side_2, other_2, sum_0, stat_0],
        [sums, stats] + [like_q] * (levels - 2),
        "near",
        2 << 30,
    )
    mine = jnp.concatenate((far_3, late_3, far_4, far_4x, late_4, late_4x), axis=1)
    theirs = sent(mine, 1)
    more = []
    if levels > 4:
        own = halve_rows(halve_rows(jnp.concatenate((keyval, inner), axis=1)))
        own = halve_rows(jnp.concatenate((own, side_2, other_2), axis=1))
        own = jnp.concatenate((own, mine[:, :64], theirs[:, :64]), axis=1)
        own = jnp.concatenate((halve_rows(own), mine[:, 64:], theirs[:, 64:]), axis=1)
        own = halve_rows(own)
        for level in range(5, levels + 1):
            more.append(sent(own, 1 << level - 1))
            own = halve_rows(jnp.concatenate((own, more[-1]), axis=1))
    return grouped(
        functools.partial(far_kernel, levels - 2),
        position,
        [queries, edge, mine, theirs, sum_1, stat_1] + ups + more,
        [like_q],
        "far",
        2 << 30,
    )[0]


def solution(mesh):
    return jax.shard_map(
        on_device,
        mesh=mesh,
        in_specs=(P(("streams", "seq"), None), P(None, ("streams", "seq"), None)),
        out_specs=P(("streams", "seq"), None),
        check_vma=False,
    )
```

time: 214 us -> 98.5 us (0.46); the launches traced: 210 us -> 98.1 us
  local copies, waits for them, and re-layouts: 78.5 us -> 3.54 us
  other arithmetic: 55.1 us -> 0.6 us
  Pallas kernels: 0 us -> 48.5 us
  waiting for transfers between devices: 51.1 us -> 30 us
  matrix products: 11.3 us -> 0 us
    pallas_call x0 -> x5, Pallas kernels: none -> 48.5 us  [the longest x3 41.9 us: grouped(): pl.pallas_call(kernel, grid_spec=pltpu.PrefetchScalarGridSpec(num_scalar_...]
    slice x13 -> x0, local copies, waits for them, and re-layouts: 34.6 us -> none  [the longest x8 25.3 us: on_device(): kv_blocks[1]]
    convert_element_type x11 -> x0, other arithmetic: 23.2 us -> none  [the longest x7 13 us: halve_rows(): return pooled.astype(jnp.bfloat16)]
    ppermute x6 -> x11, waiting for transfers between devices: 51.1 us -> 30 us  [the longest x10 30 us: sent(): return lax.ppermute(array, 'seq', [(i, i ^ stride) for i in range(count)])]
    convert_element_type x6 -> x0, local copies, waits for them, and re-layouts: 12.3 us -> none  [the longest x5 10.2 us: halve_rows(): widened = pair_rows.reshape(new_shape).astype(jnp.float32)]
    dot_general x10 -> x0, matrix products: 11.3 us -> none  [the longest x5 7.36 us: attend(): jnp.einsum('ghqk,gkhe->gqhe', expons.astype(jnp.bfloat16), value_rows, pr...]
    select_n x4 -> x0, other arithmetic: 11.2 us -> none  [the longest x3 10.6 us: on_device(): lower_half = jnp.where(upper_bit == 0, own_block, partner)]
    another operation x4 -> x0, local copies, waits for them, and re-layouts: 10.7 us -> none  [the longest x2 6.99 us: halve_rows(): jnp.take(widened, 1, axis=along + 1)]
  transfers between devices with their start and end apart: 6 -> 11, of which waited for: 3 -> 3; matrix products, arithmetic and copies ran while one was open for 37% -> 3% of each run, Pallas kernels for 0% -> 29%
where the time goes in v1:
time: 98.5 us; the launch traced here: 98.1 us
  Pallas kernels  48.5 us (49%)
  waiting for transfers between devices  30 us (30%)
  starting transfers between devices  15.3 us (16%)
  local copies, waits for them, and re-layouts  3.54 us (4%)
    pallas_call x3, Pallas kernels, grouped(): pl.pallas_call(kernel, grid_spec=pltpu.PrefetchScalarGridSpec(num_scalar_...  41.9 us
    ppermute x10, waiting for transfers between devices, sent(): return lax.ppermute(array, 'seq', [(i, i ^ stride) for i in range(count)])  30 us
    ppermute x10, starting transfers between devices, sent(): return lax.ppermute(array, 'seq', [(i, i ^ stride) for i in range(count)])  13.5 us
    pallas_call x2, Pallas kernels, pool(): pl.pallas_call(pool_kernel if first == 2 else pool_once_kernel, grid=(2,)...  6.69 us
    unnamed x15, local copies, waits for them, and re-layouts  3.53 us
  transfers between devices with their start and end apart: 11, of which 3 were waited for; matrix products, arithmetic and copies ran while one was open for 3% of the time, Pallas kernels for 29%

profile of v1, /device:TPU:0, one launch (start us, length us, event | category | flops | bytes accessed | tf_op | source)
XLA Modules:
  0.0 98.1 jit_solution(2124753860690134926)
XLA Ops:
  0.0 0.0 copy-start
  0.0 4.3 %pool.2 = (bf16[2,64,2048]{2,1,0:T(8,128)(2,1)}, bf16[2,32,2048]{2,1,0:T(8,128)(2,1)}, bf16[2,16,2048]{2,1,0:T(8,128)(2,1)}) custom-call(bf16[2,256,2048]{2,1,0:T(8,128)(2,1)} %kv_ref.3), custom_call_target="tpu_custom_call" | custom-call | tf_op jit(solution)/shard_map/pool/pallas_call | solution.py:64
  4.3 3.0 %collective-permute-start.2 = (bf16[2,64,2048]{2,1,0:T(8,128)(2,1)}, bf16[2,64,2048]{2,1,0:T(8,128)(2,1)S(1)}, u32[]{:S(2)}, u32[]{:S(2)}) collective-permute-start(bf16[2,64,2048]{2,1,0:T(8,128)(2,1)} %get-tuple-element.19), channel_id=1, source_target_pairs={{0,2},{1,3},{2,0},{3,1},{4,6},{5,7},{6,4},{7,5},{8,10},{9,11},{10,... | collective-permute-start | bytes 1572872 | tf_op jit(solution)/shard_map/ppermute | solution.py:250
  7.2 0.0 copy-done
  7.2 0.0 collective-permute-start.9
  7.2 2.6 %collective-permute-start.4 = (bf16[2,16,2048]{2,1,0:T(8,128)(2,1)}, bf16[2,16,2048]{2,1,0:T(8,128)(2,1)}, u32[]{:S(2)}, u32[]{:S(2)}) collective-permute-start(bf16[2,16,2048]{2,1,0:T(8,128)(2,1)} %get-tuple-element.21), channel_id=1, source_target_pairs={{0,8},{1,9},{2,10},{3,11},{4,12},{5,13},{6,14},{7,15},{8,0},{9,1},... | collective-permute-start | bytes 393224 | tf_op jit(solution)/shard_map/ppermute | solution.py:250
  9.8 1.3 %collective-permute-start.5 = (bf16[2,16,2048]{2,1,0:T(8,128)(2,1)}, bf16[2,16,2048]{2,1,0:T(8,128)(2,1)S(1)}, u32[]{:S(2)}, u32[]{:S(2)}) collective-permute-start(bf16[2,16,2048]{2,1,0:T(8,128)(2,1)} %get-tuple-element.21), channel_id=1, source_target_pairs={{0,12},{1,13},{2,14},{3,15},{4,8},{5,9},{6,10},{7,11},{8,4},{9,5},... | collective-permute-start | bytes 393224 | tf_op jit(solution)/shard_map/ppermute | solution.py:250
  11.2 0.2 collective-permute-start.1
  11.4 0.6 pad_add_fusion.pos_ref
  12.0 7.4 %collective-permute-done.2.kv_ref.mine_ref = bf16[2,64,2048]{2,1,0:T(8,128)(2,1)S(1)} collective-permute-done((bf16[2,64,2048]{2,1,0:T(8,128)(2,1)}, bf16[2,64,2048]{2,1,0:T(8,128)(2,1)S(1)}, u32[]{:S(2)}, u32[]{:S(2)}) %collective-permute-start.2) | collective-permute-done | bytes 524320 | tf_op jit(solution)/shard_map/ppermute | solution.py:250
  19.4 0.0 copy-start.2
  19.4 0.8 copy-done.2
  20.2 2.4 %pool.3 = (bf16[2,32,2048]{2,1,0:T(8,128)(2,1)}, bf16[2,16,2048]{2,1,0:T(8,128)(2,1)}) custom-call(bf16[2,64,2048]{2,1,0:T(8,128)(2,1)} %copy-done.2), custom_call_target="tpu_custom_call" | custom-call | tf_op jit(solution)/shard_map/pool/pallas_call | solution.py:64
  22.6 1.8 %collective-permute-start.3 = (bf16[2,32,2048]{2,1,0:T(8,128)(2,1)}, bf16[2,32,2048]{2,1,0:T(8,128)(2,1)}, u32[]{:S(2)}, u32[]{:S(2)}) collective-permute-start(bf16[2,32,2048]{2,1,0:T(8,128)(2,1)} %get-tuple-element.20), channel_id=1, source_target_pairs={{0,4},{1,5},{2,6},{3,7},{4,0},{5,1},{6,2},{7,3},{8,12},{9,13},{10,... | collective-permute-start | bytes 786440 | tf_op jit(solution)/shard_map/ppermute | solution.py:250
  24.4 6.7 %own.1 = (f32[256,2048]{1,0:T(8,128)}, f32[4,256,128]{2,1,0:T(8,128)}, bf16[2,128,2048]{2,1,0:T(8,128)(2,1)}) custom-call(s32[2]{0:T(128)} %pad_add_fusion.pos_ref, bf16[256,2048]{1,0:T(8,128)(2,1)} %q_ref.5, bf16[2,256,2048]{2,1,0:T(8,128)(2,1)} %kv_ref.3), custom_call_target="tpu_custom_call" | custom-call | flops 2147483648 | bytes 8388608 | tf_op jit(solution)/shard_map/own/pallas_call | solution.py:232
  31.1 0.0 copy-start.3
  31.1 0.0 collective-permute-done.1
  31.1 1.8 %collective-permute-start = (bf16[2,128,2048]{2,1,0:T(8,128)(2,1)}, bf16[2,128,2048]{2,1,0:T(8,128)(2,1)}, u32[]{:S(2)}, u32[]{:S(2)}) collective-permute-start(bf16[2,128,2048]{2,1,0:T(8,128)(2,1)} %get-tuple-element.17), channel_id=1, source_target_pairs={{1,2},{3,4},{5,6},{7,8},{9,10},{11,12},{13,14},{2,1},{4,3},{6,5},{... | collective-permute-start | bytes 3145736 | tf_op jit(solution)/shard_map/ppermute | solution.py:285
  32.9 0.0 collective-permute-done.3
  33.0 2.9 %collective-permute-start.6 = (bf16[2,16,2048]{2,1,0:T(8,128)(2,1)}, bf16[2,16,2048]{2,1,0:T(8,128)(2,1)S(1)}, u32[]{:S(2)}, u32[]{:S(2)}) collective-permute-start(bf16[2,16,2048]{2,1,0:T(8,128)(2,1)} %get-tuple-element.22), channel_id=1, source_target_pairs={{0,8},{1,9},{2,10},{3,11},{4,12},{5,13},{6,14},{7,15},{8,0},{9,1},... | collective-permute-start | bytes 393224 | tf_op jit(solution)/shard_map/ppermute | solution.py:250
  35.9 1.0 constant_dynamic-update-slice_fusion.4
  36.9 0.0 collective-permute-done.4
  36.9 1.1 %collective-permute-start.7 = (bf16[2,16,2048]{2,1,0:T(8,128)(2,1)}, bf16[2,16,2048]{2,1,0:T(8,128)(2,1)S(1)}, u32[]{:S(2)}, u32[]{:S(2)}) collective-permute-start(bf16[2,16,2048]{2,1,0:T(8,128)(2,1)} %get-tuple-element.22), channel_id=1, source_target_pairs={{0,12},{1,13},{2,14},{3,15},{4,8},{5,9},{6,10},{7,11},{8,4},{9,5},... | collective-permute-start | bytes 393224 | tf_op jit(solution)/shard_map/ppermute | solution.py:250
  38.0 0.9 constant_dynamic-update-slice_fusion.3
  38.9 0.0 collective-permute-done.5
  38.9 19.7 %collective-permute-done.6 = bf16[2,16,2048]{2,1,0:T(8,128)(2,1)S(1)} collective-permute-done((bf16[2,16,2048]{2,1,0:T(8,128)(2,1)}, bf16[2,16,2048]{2,1,0:T(8,128)(2,1)S(1)}, u32[]{:S(2)}, u32[]{:S(2)}) %collective-permute-start.6) | collective-permute-done | bytes 131104 | tf_op jit(solution)/shard_map/ppermute | solution.py:250
  58.7 0.0 collective-permute-done.7
  58.7 0.0 copy-start.1
  58.7 0.1 collective-permute-start.8
  58.8 0.0 copy-done.3
  58.8 0.5 collective-permute-start.10
  59.3 2.9 %collective-permute-done.10.theirs_ref = bf16[2,64,2048]{2,1,0:T(8,128)(2,1)S(1)} collective-permute-done((bf16[2,64,2048]{2,1,0:T(8,128)(2,1)S(1)}, bf16[2,64,2048]{2,1,0:T(8,128)(2,1)S(1)}, u32[]{:S(2)}, u32[]{:S(2)}) %collective-permute-start.10) | collective-permute-done | bytes 524320 | tf_op jit(solution)/shard_map/ppermute | solution.py:250
  62.2 0.0 copy-start.4
  62.2 0.0 collective-permute-done.9.inner_ref
  62.2 0.8 copy-done.4
  63.0 19.2 %near.1 = (f32[256,2048]{1,0:T(8,128)}, f32[4,256,128]{2,1,0:T(8,128)}, bf16[256,2048]{1,0:T(8,128)(2,1)}, bf16[256,2048]{1,0:T(8,128)(2,1)}) custom-call(s32[2]{0:T(128)} %pad_add_fusion.pos_ref, bf16[256,2048]{1,0:T(8,128)(2,1)} %q_ref.5, bf16[2,256,2048]{2,1,0:T(8,128)(2,1)} %collective-permute-done.9.inner_ref, bf16[2,64,2048]{2,1,0:T(8,128)(2,1)} %copy-done.2, ...), custom_call_target="tpu_custom_call" | custom-call | flops 2147483648 | bytes 8388608 | tf_op jit(solution)/shard_map/near/pallas_call | solution.py:232
  82.2 0.0 copy-done.1
  82.2 0.0 collective-permute-done.edge_ref
  82.2 0.0 collective-permute-done.8.theirs_ref
  82.2 15.9 %far.1 = bf16[256,2048]{1,0:T(8,128)(2,1)} custom-call(s32[2]{0:T(128)} %pad_add_fusion.pos_ref, bf16[256,2048]{1,0:T(8,128)(2,1)} %q_ref.5, bf16[2,128,2048]{2,1,0:T(8,128)(2,1)} %collective-permute-done.edge_ref, bf16[2,128,2048]{2,1,0:T(8,128)(2,1)} %copy-done.1, bf16[2,128,2048]{2,1,0:T(8,128)(2,1)} %collective-permute-done.8.theirs_ref, ...), custom_call_target="tpu_custom_call" | custom-call | flops 2147483648 | bytes 8388608 | tf_op jit(solution)/shard_map/far/pallas_call | solution.py:232
  (4 shorter events, 0.0 us)
Async XLA Ops:
  0.0 7.2 %copy-start = (bf16[2,256,2048]{2,1,0:T(8,128)(2,1)S(1)}, bf16[2,256,2048]{2,1,0:T(8,128)(2,1)}, u32[]{:S(2)}) copy-start(bf16[2,256,2048]{2,1,0:T(8,128)(2,1)} %kv_ref.3) | copy-start | bytes 6291460
  4.3 15.1 %collective-permute-start.2 = (bf16[2,64,2048]{2,1,0:T(8,128)(2,1)}, bf16[2,64,2048]{2,1,0:T(8,128)(2,1)S(1)}, u32[]{:S(2)}, u32[]{:S(2)}) collective-permute-start(bf16[2,64,2048]{2,1,0:T(8,128)(2,1)} %get-tuple-element.19), channel_id=1, source_target_pairs={{0,2},{1,3},{2,0},{3,1},{4,6},{5,7},{6,4},{7,5},{8,10},{9,11},{10,... | collective-permute-start | bytes 1572872 | tf_op jit(solution)/shard_map/ppermute | solution.py:250
  7.2 55.0 %collective-permute-start.9 = (bf16[2,256,2048]{2,1,0:T(8,128)(2,1)S(1)}, bf16[2,256,2048]{2,1,0:T(8,128)(2,1)}, u32[]{:S(2)}, u32[]{:S(2)}) collective-permute-start(bf16[2,256,2048]{2,1,0:T(8,128)(2,1)S(1)} %copy-done), channel_id=1, source_target_pairs={{0,1},{1,0},{2,3},{3,2},{4,5},{5,4},{6,7},{7,6},{8,9},{9,8},{10,11... | collective-permute-start | bytes 6291464 | tf_op jit(solution)/shard_map/ppermute | solution.py:250
  7.2 29.6 %collective-permute-start.4 = (bf16[2,16,2048]{2,1,0:T(8,128)(2,1)}, bf16[2,16,2048]{2,1,0:T(8,128)(2,1)}, u32[]{:S(2)}, u32[]{:S(2)}) collective-permute-start(bf16[2,16,2048]{2,1,0:T(8,128)(2,1)} %get-tuple-element.21), channel_id=1, source_target_pairs={{0,8},{1,9},{2,10},{3,11},{4,12},{5,13},{6,14},{7,15},{8,0},{9,1},... | collective-permute-start | bytes 393224 | tf_op jit(solution)/shard_map/ppermute | solution.py:250
  9.8 29.1 %collective-permute-start.5 = (bf16[2,16,2048]{2,1,0:T(8,128)(2,1)}, bf16[2,16,2048]{2,1,0:T(8,128)(2,1)S(1)}, u32[]{:S(2)}, u32[]{:S(2)}) collective-permute-start(bf16[2,16,2048]{2,1,0:T(8,128)(2,1)} %get-tuple-element.21), channel_id=1, source_target_pairs={{0,12},{1,13},{2,14},{3,15},{4,8},{5,9},{6,10},{7,11},{8,4},{9,5},... | collective-permute-start | bytes 393224 | tf_op jit(solution)/shard_map/ppermute | solution.py:250
  11.2 20.0 %collective-permute-start.1 = (bf16[2,32,2048]{2,1,0:T(8,128)(2,1)}, bf16[2,32,2048]{2,1,0:T(8,128)(2,1)S(1)}, u32[]{:S(2)}, u32[]{:S(2)}) collective-permute-start(bf16[2,32,2048]{2,1,0:T(8,128)(2,1)} %get-tuple-element.18), channel_id=1, source_target_pairs={{0,4},{1,5},{2,6},{3,7},{4,0},{5,1},{6,2},{7,3},{8,12},{9,13},{10,... | collective-permute-start | bytes 786440 | tf_op jit(solution)/shard_map/ppermute | solution.py:250
  19.4 0.8 copy-start.2
  22.6 10.4 %collective-permute-start.3 = (bf16[2,32,2048]{2,1,0:T(8,128)(2,1)}, bf16[2,32,2048]{2,1,0:T(8,128)(2,1)}, u32[]{:S(2)}, u32[]{:S(2)}) collective-permute-start(bf16[2,32,2048]{2,1,0:T(8,128)(2,1)} %get-tuple-element.20), channel_id=1, source_target_pairs={{0,4},{1,5},{2,6},{3,7},{4,0},{5,1},{6,2},{7,3},{8,12},{9,13},{10,... | collective-permute-start | bytes 786440 | tf_op jit(solution)/shard_map/ppermute | solution.py:250
  31.1 27.7 %copy-start.3 = (bf16[2,64,2048]{2,1,0:T(8,128)(2,1)S(1)}, bf16[2,64,2048]{2,1,0:T(8,128)(2,1)}, u32[]{:S(2)}) copy-start(bf16[2,64,2048]{2,1,0:T(8,128)(2,1)} %copy-done.2) | copy-start | bytes 1572868
  31.1 51.1 %collective-permute-start = (bf16[2,128,2048]{2,1,0:T(8,128)(2,1)}, bf16[2,128,2048]{2,1,0:T(8,128)(2,1)}, u32[]{:S(2)}, u32[]{:S(2)}) collective-permute-start(bf16[2,128,2048]{2,1,0:T(8,128)(2,1)} %get-tuple-element.17), channel_id=1, source_target_pairs={{1,2},{3,4},{5,6},{7,8},{9,10},{11,12},{13,14},{2,1},{4,3},{6,5},{... | collective-permute-start | bytes 3145736 | tf_op jit(solution)/shard_map/ppermute | solution.py:285
  33.0 25.7 %collective-permute-start.6 = (bf16[2,16,2048]{2,1,0:T(8,128)(2,1)}, bf16[2,16,2048]{2,1,0:T(8,128)(2,1)S(1)}, u32[]{:S(2)}, u32[]{:S(2)}) collective-permute-start(bf16[2,16,2048]{2,1,0:T(8,128)(2,1)} %get-tuple-element.22), channel_id=1, source_target_pairs={{0,8},{1,9},{2,10},{3,11},{4,12},{5,13},{6,14},{7,15},{8,0},{9,1},... | collective-permute-start | bytes 393224 | tf_op jit(solution)/shard_map/ppermute | solution.py:250
  36.9 21.8 %collective-permute-start.7 = (bf16[2,16,2048]{2,1,0:T(8,128)(2,1)}, bf16[2,16,2048]{2,1,0:T(8,128)(2,1)S(1)}, u32[]{:S(2)}, u32[]{:S(2)}) collective-permute-start(bf16[2,16,2048]{2,1,0:T(8,128)(2,1)} %get-tuple-element.22), channel_id=1, source_target_pairs={{0,12},{1,13},{2,14},{3,15},{4,8},{5,9},{6,10},{7,11},{8,4},{9,5},... | collective-permute-start | bytes 393224 | tf_op jit(solution)/shard_map/ppermute | solution.py:250
  58.7 23.5 %copy-start.1 = (bf16[2,128,2048]{2,1,0:T(8,128)(2,1)}, bf16[2,128,2048]{2,1,0:T(8,128)(2,1)S(1)}, u32[]{:S(2)}) copy-start(bf16[2,128,2048]{2,1,0:T(8,128)(2,1)S(1)} %constant_dynamic-update-slice_fusion.mine_ref) | copy-start | bytes 3145732
  58.7 23.5 %collective-permute-start.8 = (bf16[2,128,2048]{2,1,0:T(8,128)(2,1)S(1)}, bf16[2,128,2048]{2,1,0:T(8,128)(2,1)}, u32[]{:S(2)}, u32[]{:S(2)}) collective-permute-start(bf16[2,128,2048]{2,1,0:T(8,128)(2,1)S(1)} %constant_dynamic-update-slice_fusion.mine_ref), channel_id=1, source_target_pairs={{0,1},{1,0},{2,3},{3,2},{4,5},{5,4},{6,7},{7,6},{8,9},{9,8},{10,11... | collective-permute-start | bytes 3145736 | tf_op jit(solution)/shard_map/ppermute | solution.py:250
  58.8 3.4 %collective-permute-start.10 = (bf16[2,64,2048]{2,1,0:T(8,128)(2,1)S(1)}, bf16[2,64,2048]{2,1,0:T(8,128)(2,1)S(1)}, u32[]{:S(2)}, u32[]{:S(2)}) collective-permute-start(bf16[2,64,2048]{2,1,0:T(8,128)(2,1)S(1)} %copy-done.3), channel_id=1, source_target_pairs={{0,1},{1,0},{2,3},{3,2},{4,5},{5,4},{6,7},{7,6},{8,9},{9,8},{10,11... | collective-permute-start | bytes 1572872 | tf_op jit(solution)/shard_map/ppermute | solution.py:250
  62.2 0.8 copy-start.4

commit v2 on v0

v2 whole, which is shorter than its diff:
```python
import functools
import math

import jax
import jax.numpy as jnp
from jax import lax
from jax.experimental import pallas as pl
from jax.experimental.pallas import tpu as pltpu
from jax.sharding import PartitionSpec as P

HEADS = 16
HEAD_DIM = 128
BLOCK = 128
neg_large = -1e30
log_two = 0.6931471805599453
to_log2 = 1.0 / (math.sqrt(HEAD_DIM) * log_two)
VMEM = pl.BlockSpec(memory_space=pltpu.VMEM)
ANY = pl.BlockSpec(memory_space=pl.ANY)
SMEM = pl.BlockSpec(memory_space=pltpu.SMEM)


def dot(left, right):
    return lax.dot_general(
        left, right, (((1,), (0,)), ((), ())), preferred_element_type=jnp.float32
    )


def dot_t(left, right):
    return lax.dot_general(
        left, right, (((1,), (1,)), ((), ())), preferred_element_type=jnp.float32
    )


def iota(shape, dim):
    return lax.broadcasted_iota(jnp.int32, shape, dim)


def halve(rows):
    shape = (rows.shape[0] // 2, rows.shape[0])
    pairs = jnp.where(iota(shape, 1) >> 1 == iota(shape, 0), 0.5, 0.0).astype(jnp.bfloat16)
    return dot(pairs, rows).astype(jnp.bfloat16)


def repeated_halve(rows, level):
    count = rows.shape[0]
    shape = (count, count)
    first = iota(shape, 0) >> level << level
    hit = (iota(shape, 1) == first) | (iota(shape, 1) == first + (1 << level - 1))
    return dot(jnp.where(hit, 0.5, 0.0).astype(jnp.bfloat16), rows).astype(jnp.bfloat16)


def with_ones(values):
    return jnp.concatenate([values, jnp.ones(values.shape, values.dtype)], axis=1)


def row_max(scores):
    return jnp.max(scores, axis=1, keepdims=True)


def own_pool_kernel(kv_ref, *out_refs):
    for which in range(2):
        rows = halve(kv_ref[which])
        for out_ref in out_refs:
            rows = halve(rows)
            out_ref[which] = rows


def side_pool_kernel(after_ref, kv_ref, *out_refs):
    for which in range(2):
        rows = kv_ref[which]
        for out_ref in out_refs:
            rows = halve(rows)
            out_ref[which] = rows


def join_kernel(after_ref, *refs):
    start = 0
    for ref in refs[:-1]:
        refs[-1][:, start : start + ref.shape[1], :] = ref[...]
        start += ref.shape[1]


def own_kernel(core_ref, q_ref, kv_ref, mean_ref, log_ref, edge_ref):
    outer = pl.ds(pl.multiple_of(core_ref[0] * BLOCK, BLOCK), BLOCK)
    edge_ref[...] = kv_ref[:, outer, :]
    for head in range(HEADS):
        cols = slice(head * HEAD_DIM, (head + 1) * HEAD_DIM)
        scores = dot_t(q_ref[:, cols], kv_ref[0, :, cols])
        peak = row_max(scores) * to_log2
        weights = jnp.exp2(scores * to_log2 - peak).astype(jnp.bfloat16)
        both = dot(weights, with_ones(kv_ref[1, :, cols]))
        total = both[:, HEAD_DIM:]
        mean_ref[:, cols] = both[:, :HEAD_DIM] / total
        log_ref[:, cols] = jnp.log2(total) + peak


def spans(core):
    edge = pl.ds(pl.multiple_of(core * BLOCK, BLOCK), BLOCK)
    other = pl.ds(pl.multiple_of((1 - core) * BLOCK, BLOCK), BLOCK)
    return edge, other


def attend(first, second, cols, fine, bias, coarse, mean_ref, log_ref):
    def rows(ref):
        return jnp.concatenate([ref[first, cols], ref[second, cols]], axis=0)

    query_ref, key, value = fine
    near = dot_t(query_ref[first, cols], key)
    if bias is not None:
        near = near + bias
    scores = [dot_t(rows(query_ref), jnp.concatenate(keys, 0)) for query_ref, keys, _, _ in coarse]
    peak = functools.reduce(jnp.maximum, [row_max(score) for score in scores])
    peak = jnp.concatenate([jnp.maximum(peak[:BLOCK], row_max(near)), peak[BLOCK:]], axis=0)
    logs = rows(log_ref)
    peak = jnp.maximum(peak * to_log2, logs)
    weights = [
        jnp.exp2(score * to_log2 - (peak - level)).astype(jnp.bfloat16)
        for score, (_, _, _, level) in zip(scores, coarse)
    ]
    values = [value for _, _, parts, _ in coarse for value in parts]
    both = dot(jnp.concatenate(weights, axis=1), with_ones(jnp.concatenate(values, axis=0)))
    weights = jnp.exp2(near * to_log2 - peak[:BLOCK]).astype(jnp.bfloat16)
    near = dot(weights, with_ones(value))
    both = jnp.concatenate([both[:BLOCK] + near, both[BLOCK:]], axis=0)
    factor = jnp.exp2(logs - peak)
    total = both[:, HEAD_DIM:] + factor
    mean = (both[:, :HEAD_DIM] + factor * rows(mean_ref)) / total
    return mean, total, peak


def near_kernel(core_ref, q_ref, inner_ref, mine_ref, theirs_ref, mean_ref, log_ref, *refs):
    new_mean_ref, new_log_ref, *up_refs = refs[:-4]
    up_1_ref, up_2_ref, keys_ref, values_ref = refs[-4:]
    core = core_ref[0]
    edge, other = spans(core)
    up = q_ref[...]
    for level, ref in enumerate([up_1_ref, up_2_ref] + up_refs, 1):
        up = repeated_halve(up, level)
        ref[...] = up
    keys_ref[...] = halve(inner_ref[0])
    values_ref[...] = halve(inner_ref[1])
    for head in range(HEADS):
        cols = slice(head * HEAD_DIM, (head + 1) * HEAD_DIM)
        mean, total, peak = attend(
            other,
            edge,
            cols,
            (q_ref, inner_ref[0, edge, cols], inner_ref[1, edge, cols]),
            None,
            [
                (up_1_ref, [keys_ref[:, cols]], [values_ref[:, cols]], 1.0),
                (
                    up_2_ref,
                    [mine_ref[0, :, cols], theirs_ref[0, :64, cols]],
                    [mine_ref[1, :, cols], theirs_ref[1, :64, cols]],
                    2.0,
                ),
            ],
            mean_ref,
            log_ref,
        )
        logs = jnp.log2(total) + peak
        new_mean_ref[other, cols] = mean[:BLOCK]
        new_mean_ref[edge, cols] = mean[BLOCK:]
        new_log_ref[other, cols] = logs[:BLOCK]
        new_log_ref[edge, cols] = logs[BLOCK:]


def far_kernel(core_ref, q_ref, edge_ref, early_ref, their_early_ref, late_ref, their_late_ref, mean_ref, log_ref, *refs):
    out_ref = refs[-1]
    count = len(refs) // 2 + 1
    up_refs = refs[:count]
    more_refs = refs[count:-1]
    core = core_ref[0]
    edge, other = spans(core)
    bias = jnp.where(core_ref[1] == 1, 0.0, neg_large)
    for head in range(HEADS):
        cols = slice(head * HEAD_DIM, (head + 1) * HEAD_DIM)

        def parts(which, level):
            early = slice(0, 32) if level == 3 else slice(32, 64)
            theirs = slice(64, 96) if level == 3 else slice(96, 128)
            return [
                early_ref[which, early, cols],
                late_ref[which, early, cols],
                their_early_ref[which, theirs, cols],
                their_late_ref[which, early, cols],
            ]

        coarse = [
            (up_refs[level - 3], parts(0, level), parts(1, level), float(level))
            for level in (3, 4)
        ]
        for level, more_ref in enumerate(more_refs, 5):
            coarse.append(
                (up_refs[level - 3], [more_ref[0, :, cols]], [more_ref[1, :, cols]], float(level))
            )
        mean, _, _ = attend(
            edge,
            other,
            cols,
            (q_ref, edge_ref[0, :, cols], edge_ref[1, :, cols]),
            bias,
            coarse,
            mean_ref,
            log_ref,
        )
        mean = mean.astype(out_ref.dtype)
        out_ref[edge, cols] = mean[:BLOCK]
        out_ref[other, cols] = mean[BLOCK:]


def call(kernel, in_specs, outputs, name, micros, *inputs, scratch=()):
    return pl.pallas_call(
        kernel,
        in_specs=in_specs,
        out_specs=[VMEM] * len(outputs),
        out_shape=[jax.ShapeDtypeStruct(shape, dtype) for shape, dtype in outputs],
        scratch_shapes=[pltpu.VMEM(shape, dtype) for shape, dtype in scratch],
        cost_estimate=pl.CostEstimate(
            flops=micros * 1_000_000_000, bytes_accessed=1 << 20, transcendentals=0
        ),
        compiler_params=pltpu.CompilerParams(vmem_limit_bytes=16 << 20),
        name=name,
    )(*inputs)


def sent(array, stride):
    count = lax.axis_size("seq")
    return lax.ppermute(array, "seq", [(i, i ^ stride) for i in range(count)])


def halve_rows(pairs):
    wide = pairs.reshape(2, pairs.shape[1] // 2, 2, pairs.shape[2]).astype(jnp.float32)
    return ((wide[:, :, 0] + wide[:, :, 1]) * 0.5).astype(jnp.bfloat16)


def on_device(queries, keyval):
    count = lax.axis_size("seq")
    levels = count.bit_length() - 1
    index = lax.axis_index("seq")
    core = index % 2
    inside = jnp.where(core == 0, index > 0, index < count - 1)
    position = jnp.stack((core, inside.astype(core.dtype)))
    rows, features = queries.shape
    narrow = keyval.dtype
    wide = ((rows, features), jnp.float32)
    up = ((rows, features), narrow)

    def some(count):
        return ((2, count, features), narrow)

    own_2, own_3, own_4 = call(
        own_pool_kernel, [VMEM], [some(64), some(32), some(16)], "pool", 1, keyval
    )
    side_2 = sent(own_2, 2)
    inner = sent(keyval, 1)
    early = [sent(own_3, 4), sent(own_4, 8), sent(own_4, 12)]
    mean, log, edge = call(
        own_kernel,
        [SMEM, VMEM, VMEM],
        [wide, wide, some(BLOCK)],
        "own",
        4,
        position,
        queries,
        keyval,
    )
    links = [(i, i + 1) for i in range(1, count - 1, 2)]
    edge = lax.ppermute(edge, "seq", links + [(j, i) for i, j in links])
    side_3, side_4 = call(
        side_pool_kernel, [ANY, VMEM], [some(32), some(16)], "side", 1, log, side_2
    )
    late = [sent(side_3, 4), sent(side_4, 8), sent(side_4, 12)]
    (early,) = call(
        join_kernel, [ANY] + [VMEM] * 3, [some(64)], "early", 1, side_3, *early
    )
    theirs = sent(jnp.concatenate((side_2, early), axis=1), 1)
    mean, log, *ups = call(
        near_kernel,
        [SMEM] + [VMEM] * 6,
        [wide, wide] + [up] * (levels - 2),
        "near",
        4,
        position,
        queries,
        inner,
        side_2,
        theirs,
        mean,
        log,
        scratch=[up, up, ((BLOCK, features), narrow), ((BLOCK, features), narrow)],
    )
    (late,) = call(join_kernel, [ANY] + [VMEM] * 3, [some(64)], "late", 1, log, *late)
    their_late = sent(late, 1)
    more = []
    if levels > 4:
        own = halve_rows(halve_rows(jnp.concatenate((keyval, inner), axis=1)))
        own = halve_rows(jnp.concatenate((own, side_2, theirs[:, :64]), axis=1))
        quarters = (early, late, theirs[:, 64:], their_late)
        own = [own] + [quarter[:, :32] for quarter in quarters]
        own = [halve_rows(jnp.concatenate(own, axis=1))]
        own = halve_rows(jnp.concatenate(own + [part[:, 32:] for part in quarters], axis=1))
        for level in range(5, levels + 1):
            more.append(sent(own, 1 << level - 1))
            own = halve_rows(jnp.concatenate((own, more[-1]), axis=1))
    far = [position, queries, edge, early, theirs, late, their_late, mean, log] + ups + more
    return call(far_kernel, [SMEM] + [VMEM] * (len(far) - 1), [up], "far", 4, *far)[0]


def solution(mesh):
    return jax.shard_map(
        on_device,
        mesh=mesh,
        in_specs=(P(("streams", "seq"), None), P(None, ("streams", "seq"), None)),
        out_specs=P(("streams", "seq"), None),
        check_vma=False,
    )
```

time: 214 us -> 61.4 us (0.29); the launches traced: 210 us -> 61.1 us
  local copies, waits for them, and re-layouts: 78.5 us -> 2.82 us
  other arithmetic: 55.1 us -> 0.16 us
  waiting for transfers between devices: 51.1 us -> 23.2 us
  Pallas kernels: 0 us -> 21 us
  matrix products: 11.3 us -> 0 us
    slice x13 -> x0, local copies, waits for them, and re-layouts: 34.6 us -> none  [the longest x8 25.3 us: on_device(): kv_blocks[1]]
    ppermute x6 -> x11, waiting for transfers between devices: 51.1 us -> 23.2 us  [the longest x10 23.2 us: sent(): return lax.ppermute(array, 'seq', [(i, i ^ stride) for i in range(count)])]
    convert_element_type x11 -> x0, other arithmetic: 23.2 us -> none  [the longest x7 13 us: halve_rows(): return pooled.astype(jnp.bfloat16)]
    pallas_call x0 -> x7, Pallas kernels: none -> 21 us  [call(): pl.pallas_call(kernel, in_specs=in_specs, out_specs=[VMEM] * len(outputs)...]
    convert_element_type x6 -> x0, local copies, waits for them, and re-layouts: 12.3 us -> none  [the longest x5 10.2 us: halve_rows(): widened = pair_rows.reshape(new_shape).astype(jnp.float32)]
    dot_general x10 -> x0, matrix products: 11.3 us -> none  [the longest x5 7.36 us: attend(): jnp.einsum('ghqk,gkhe->gqhe', expons.astype(jnp.bfloat16), value_rows, pr...]
    select_n x4 -> x0, other arithmetic: 11.2 us -> none  [the longest x3 10.6 us: on_device(): lower_half = jnp.where(upper_bit == 0, own_block, partner)]
    another operation x4 -> x0, local copies, waits for them, and re-layouts: 10.7 us -> none  [the longest x2 6.99 us: halve_rows(): jnp.take(widened, 1, axis=along + 1)]
  transfers between devices with their start and end apart: 6 -> 11, of which waited for: 3 -> 5; matrix products, arithmetic and copies ran while one was open for 37% -> 0% of each run, Pallas kernels for 0% -> 24%
where the time goes in v2:
time: 61.4 us; the launch traced here: 61.1 us
  waiting for transfers between devices  23.2 us (38%)
  Pallas kernels  21 us (34%)
  starting transfers between devices  13.9 us (23%)
  local copies, waits for them, and re-layouts  2.82 us (5%)
    ppermute x10, waiting for transfers between devices, sent(): return lax.ppermute(array, 'seq', [(i, i ^ stride) for i in range(count)])  23.2 us
    pallas_call x7, Pallas kernels, call(): pl.pallas_call(kernel, in_specs=in_specs, out_specs=[VMEM] * len(outputs)...  21 us
    ppermute x10, starting transfers between devices, sent(): return lax.ppermute(array, 'seq', [(i, i ^ stride) for i in range(count)])  13 us
    unnamed x8, local copies, waits for them, and re-layouts  2.82 us
  transfers between devices with their start and end apart: 11, of which 5 were waited for; matrix products, arithmetic and copies ran while one was open for 0% of the time, Pallas kernels for 24%

profile of v2, /device:TPU:0, one launch (start us, length us, event | category | flops | bytes accessed | tf_op | source)
XLA Modules:
  0.0 61.1 jit_solution(3762640035082460522)
XLA Ops:
  0.0 0.5 collective-permute-start.6
  0.5 0.0 copy-start
  0.5 1.6 %copy-done = bf16[2,256,2048]{2,1,0:T(8,128)(2,1)S(1)} copy-done((bf16[2,256,2048]{2,1,0:T(8,128)(2,1)S(1)}, bf16[2,256,2048]{2,1,0:T(8,128)(2,1)}, u32[]{:S(2)}) %copy-start) | copy-done | bytes 2097176
  2.0 0.0 copy-start.1
  2.0 1.3 %pool.1 = (bf16[2,64,2048]{2,1,0:T(8,128)(2,1)S(1)}, bf16[2,32,2048]{2,1,0:T(8,128)(2,1)S(1)}, bf16[2,16,2048]{2,1,0:T(8,128)(2,1)S(1)}) custom-call(bf16[2,256,2048]{2,1,0:T(8,128)(2,1)S(1)} %copy-done), custom_call_target="tpu_custom_call" | custom-call | flops 1000000000 | bytes 1048576 | tf_op jit(solution)/shard_map/pool/pallas_call | solution.py:214
  3.4 2.5 %collective-permute-start.1 = (bf16[2,64,2048]{2,1,0:T(8,128)(2,1)S(1)}, bf16[2,64,2048]{2,1,0:T(8,128)(2,1)S(1)}, u32[]{:S(2)}, u32[]{:S(2)}) collective-permute-start(bf16[2,64,2048]{2,1,0:T(8,128)(2,1)S(1)} %get-tuple-element.19), channel_id=1, source_target_pairs={{0,2},{1,3},{2,0},{3,1},{4,6},{5,7},{6,4},{7,5},{8,10},{9,11},{10,... | collective-permute-start | bytes 1572872 | tf_op jit(solution)/shard_map/ppermute | solution.py:230
  5.9 2.6 %collective-permute-start.3 = (bf16[2,16,2048]{2,1,0:T(8,128)(2,1)S(1)}, bf16[2,16,2048]{2,1,0:T(8,128)(2,1)}, u32[]{:S(2)}, u32[]{:S(2)}) collective-permute-start(bf16[2,16,2048]{2,1,0:T(8,128)(2,1)S(1)} %get-tuple-element.22), channel_id=1, source_target_pairs={{0,8},{1,9},{2,10},{3,11},{4,12},{5,13},{6,14},{7,15},{8,0},{9,1},... | collective-permute-start | bytes 393224 | tf_op jit(solution)/shard_map/ppermute | solution.py:230
  8.5 1.3 %collective-permute-start.4 = (bf16[2,16,2048]{2,1,0:T(8,128)(2,1)S(1)}, bf16[2,16,2048]{2,1,0:T(8,128)(2,1)}, u32[]{:S(2)}, u32[]{:S(2)}) collective-permute-start(bf16[2,16,2048]{2,1,0:T(8,128)(2,1)S(1)} %get-tuple-element.22), channel_id=1, source_target_pairs={{0,12},{1,13},{2,14},{3,15},{4,8},{5,9},{6,10},{7,11},{8,4},{9,5},... | collective-permute-start | bytes 393224 | tf_op jit(solution)/shard_map/ppermute | solution.py:230
  9.9 0.2 collective-permute-start.2
  10.1 0.1 pad_add_fusion.core_ref
  10.2 0.0 copy-done.1
  10.2 0.0 copy-start.2
  10.2 1.2 %copy-done.2 = bf16[256,2048]{1,0:T(8,128)(2,1)S(1)} copy-done((bf16[256,2048]{1,0:T(8,128)(2,1)S(1)}, bf16[256,2048]{1,0:T(8,128)(2,1)}, u32[]{:S(2)}) %copy-start.2) | copy-done | bytes 1048600
  11.4 2.2 %own.1 = (f32[256,2048]{1,0:T(8,128)S(1)}, f32[256,2048]{1,0:T(8,128)S(1)}, bf16[2,128,2048]{2,1,0:T(8,128)(2,1)S(1)}) custom-call(s32[2]{0:T(128)S(1)} %pad_add_fusion.core_ref, bf16[256,2048]{1,0:T(8,128)(2,1)S(1)} %copy-done.2, bf16[2,256,2048]{2,1,0:T(8,128)(2,1)S(1)} %copy-done.1), custom_call_target="tpu_custom_call" | custom-call | flops 4000000000 | bytes 1048576 | tf_op jit(solution)/shard_map/own/pallas_call | solution.py:214
  13.6 4.9 %collective-permute-done.1.kv_ref.mine_ref = bf16[2,64,2048]{2,1,0:T(8,128)(2,1)S(1)} collective-permute-done((bf16[2,64,2048]{2,1,0:T(8,128)(2,1)S(1)}, bf16[2,64,2048]{2,1,0:T(8,128)(2,1)S(1)}, u32[]{:S(2)}, u32[]{:S(2)}) %collective-permute-start.1) | collective-permute-done | bytes 524320 | tf_op jit(solution)/shard_map/ppermute | solution.py:230
  18.5 0.4 side.1
  19.0 0.0 collective-permute-done.3.refs_1_
  19.0 0.0 collective-permute-done.4.refs_2_
  19.0 3.4 %collective-permute-done.2.refs_0_ = bf16[2,32,2048]{2,1,0:T(8,128)(2,1)} collective-permute-done((bf16[2,32,2048]{2,1,0:T(8,128)(2,1)S(1)}, bf16[2,32,2048]{2,1,0:T(8,128)(2,1)}, u32[]{:S(2)}, u32[]{:S(2)}) %collective-permute-start.2) | collective-permute-done | bytes 262176 | tf_op jit(solution)/shard_map/ppermute | solution.py:230
  22.4 0.0 copy-start.3
  22.4 1.2 %early.1.early_ref = bf16[2,64,2048]{2,1,0:T(8,128)(2,1)S(1)} custom-call(bf16[2,32,2048]{2,1,0:T(8,128)(2,1)S(1)} %get-tuple-element.20.after_ref, bf16[2,32,2048]{2,1,0:T(8,128)(2,1)} %collective-permute-done.2.refs_0_, bf16[2,16,2048]{2,1,0:T(8,128)(2,1)} %collective-permute-done.3.refs_1_, bf16[2,16,2048]{2,1,0:T(8,128)(2,1)} %collective-permute-done.4.refs_2_), custom_call_target="tpu_custom_call" | custom-call | flops 1000000000 | bytes 1048576 | tf_op jit(solution)/shard_map/early/pallas_call | solution.py:214
  23.5 0.1 pad_maximum_fusion
  23.6 0.1 collective-permute-start.5
  23.7 0.9 %collective-permute-start = (bf16[2,128,2048]{2,1,0:T(8,128)(2,1)S(1)}, bf16[2,128,2048]{2,1,0:T(8,128)(2,1)S(1)}, u32[]{:S(2)}, u32[]{:S(2)}) collective-permute-start(bf16[2,128,2048]{2,1,0:T(8,128)(2,1)S(1)} %get-tuple-element.17), channel_id=1, source_target_pairs={{1,2},{3,4},{5,6},{7,8},{9,10},{11,12},{13,14},{2,1},{4,3},{6,5},{... | collective-permute-start | bytes 3145736 | tf_op jit(solution)/shard_map/ppermute | solution.py:270
  24.6 3.3 %collective-permute-start.7 = (bf16[2,32,2048]{2,1,0:T(8,128)(2,1)S(1)}, bf16[2,32,2048]{2,1,0:T(8,128)(2,1)S(1)}, u32[]{:S(2)}, u32[]{:S(2)}) collective-permute-start(bf16[2,32,2048]{2,1,0:T(8,128)(2,1)S(1)} %get-tuple-element.20.after_ref), channel_id=1, source_target_pairs={{0,4},{1,5},{2,6},{3,7},{4,0},{5,1},{6,2},{7,3},{8,12},{9,13},{10,... | collective-permute-start | bytes 786440 | tf_op jit(solution)/shard_map/ppermute | solution.py:230
  27.9 2.1 %collective-permute-start.8 = (bf16[2,16,2048]{2,1,0:T(8,128)(2,1)S(1)}, bf16[2,16,2048]{2,1,0:T(8,128)(2,1)S(1)}, u32[]{:S(2)}, u32[]{:S(2)}) collective-permute-start(bf16[2,16,2048]{2,1,0:T(8,128)(2,1)S(1)} %get-tuple-element.25), channel_id=1, source_target_pairs={{0,8},{1,9},{2,10},{3,11},{4,12},{5,13},{6,14},{7,15},{8,0},{9,1},... | collective-permute-start | bytes 393224 | tf_op jit(solution)/shard_map/ppermute | solution.py:230
  29.9 0.0 collective-permute-done.5.theirs_ref.their_early_ref
  29.9 0.4 collective-permute-start.9
  30.3 0.0 collective-permute-done.6.inner_ref
  30.3 0.0 copy-done.3
  30.3 9.8 %near.1 = (f32[256,2048]{1,0:T(8,128)S(1)}, f32[256,2048]{1,0:T(8,128)S(1)}, bf16[256,2048]{1,0:T(8,128)(2,1)S(1)}, bf16[256,2048]{1,0:T(8,128)(2,1)S(1)}) custom-call(s32[2]{0:T(128)S(1)} %pad_add_fusion.core_ref, bf16[256,2048]{1,0:T(8,128)(2,1)S(1)} %copy-done.3, bf16[2,256,2048]{2,1,0:T(8,128)(2,1)} %collective-permute-done.6.inner_ref, ...), custom_call_target="tpu_custom_call" | custom-call | flops 4000000000 | bytes 1048576 | tf_op jit(solution)/shard_map/near/pallas_call | solution.py:214
  40.1 7.3 %collective-permute-done.8.refs_1_ = bf16[2,16,2048]{2,1,0:T(8,128)(2,1)S(1)} collective-permute-done((bf16[2,16,2048]{2,1,0:T(8,128)(2,1)S(1)}, bf16[2,16,2048]{2,1,0:T(8,128)(2,1)S(1)}, u32[]{:S(2)}, u32[]{:S(2)}) %collective-permute-start.8) | collective-permute-done | bytes 131104 | tf_op jit(solution)/shard_map/ppermute | solution.py:230
  47.4 5.7 %collective-permute-done.9.refs_2_ = bf16[2,16,2048]{2,1,0:T(8,128)(2,1)S(1)} collective-permute-done((bf16[2,16,2048]{2,1,0:T(8,128)(2,1)S(1)}, bf16[2,16,2048]{2,1,0:T(8,128)(2,1)S(1)}, u32[]{:S(2)}, u32[]{:S(2)}) %collective-permute-start.9) | collective-permute-done | bytes 131104 | tf_op jit(solution)/shard_map/ppermute | solution.py:230
  53.1 0.0 collective-permute-done.7.refs_0_
  53.1 0.1 collective-permute-start.10
  53.2 0.0 collective-permute-done.edge_ref
  53.2 1.9 %collective-permute-done.10.their_late_ref = bf16[2,64,2048]{2,1,0:T(8,128)(2,1)S(1)} collective-permute-done((bf16[2,64,2048]{2,1,0:T(8,128)(2,1)S(1)}, bf16[2,64,2048]{2,1,0:T(8,128)(2,1)S(1)}, u32[]{:S(2)}, u32[]{:S(2)}) %collective-permute-start.10) | collective-permute-done | bytes 524320 | tf_op jit(solution)/shard_map/ppermute | solution.py:230
  55.1 6.0 %far.1 = bf16[256,2048]{1,0:T(8,128)(2,1)} custom-call(s32[2]{0:T(128)S(1)} %pad_add_fusion.core_ref, bf16[256,2048]{1,0:T(8,128)(2,1)S(1)} %copy-done.3, bf16[2,128,2048]{2,1,0:T(8,128)(2,1)S(1)} %collective-permute-done.edge_ref, bf16[2,64,2048]{2,1,0:T(8,128)(2,1)S(1)} %early.1.early_ref, ...), custom_call_target="tpu_custom_call" | custom-call | flops 4000000000 | bytes 1048576 | tf_op jit(solution)/shard_map/far/pallas_call | solution.py:214
  (1 shorter events, 0.0 us)
Async XLA Ops:
  0.0 30.3 %collective-permute-start.6 = (bf16[2,256,2048]{2,1,0:T(8,128)(2,1)}, bf16[2,256,2048]{2,1,0:T(8,128)(2,1)}, u32[]{:S(2)}, u32[]{:S(2)}) collective-permute-start(bf16[2,256,2048]{2,1,0:T(8,128)(2,1)} %kv_ref.3), channel_id=1, source_target_pairs={{0,1},{1,0},{2,3},{3,2},{4,5},{5,4},{6,7},{7,6},{8,9},{9,8},{10,11... | collective-permute-start | bytes 6291464 | tf_op jit(solution)/shard_map/ppermute | solution.py:230
  0.5 1.6 %copy-start = (bf16[2,256,2048]{2,1,0:T(8,128)(2,1)S(1)}, bf16[2,256,2048]{2,1,0:T(8,128)(2,1)}, u32[]{:S(2)}) copy-start(bf16[2,256,2048]{2,1,0:T(8,128)(2,1)} %kv_ref.3) | copy-start | bytes 6291460
  2.0 8.1 %copy-start.1 = (bf16[2,256,2048]{2,1,0:T(8,128)(2,1)S(1)}, bf16[2,256,2048]{2,1,0:T(8,128)(2,1)}, u32[]{:S(2)}) copy-start(bf16[2,256,2048]{2,1,0:T(8,128)(2,1)} %kv_ref.3) | copy-start | bytes 6291460
  3.4 15.1 %collective-permute-start.1 = (bf16[2,64,2048]{2,1,0:T(8,128)(2,1)S(1)}, bf16[2,64,2048]{2,1,0:T(8,128)(2,1)S(1)}, u32[]{:S(2)}, u32[]{:S(2)}) collective-permute-start(bf16[2,64,2048]{2,1,0:T(8,128)(2,1)S(1)} %get-tuple-element.19), channel_id=1, source_target_pairs={{0,2},{1,3},{2,0},{3,1},{4,6},{5,7},{6,4},{7,5},{8,10},{9,11},{10,... | collective-permute-start | bytes 1572872 | tf_op jit(solution)/shard_map/ppermute | solution.py:230
  5.9 13.0 %collective-permute-start.3 = (bf16[2,16,2048]{2,1,0:T(8,128)(2,1)S(1)}, bf16[2,16,2048]{2,1,0:T(8,128)(2,1)}, u32[]{:S(2)}, u32[]{:S(2)}) collective-permute-start(bf16[2,16,2048]{2,1,0:T(8,128)(2,1)S(1)} %get-tuple-element.22), channel_id=1, source_target_pairs={{0,8},{1,9},{2,10},{3,11},{4,12},{5,13},{6,14},{7,15},{8,0},{9,1},... | collective-permute-start | bytes 393224 | tf_op jit(solution)/shard_map/ppermute | solution.py:230
  8.5 10.5 %collective-permute-start.4 = (bf16[2,16,2048]{2,1,0:T(8,128)(2,1)S(1)}, bf16[2,16,2048]{2,1,0:T(8,128)(2,1)}, u32[]{:S(2)}, u32[]{:S(2)}) collective-permute-start(bf16[2,16,2048]{2,1,0:T(8,128)(2,1)S(1)} %get-tuple-element.22), channel_id=1, source_target_pairs={{0,12},{1,13},{2,14},{3,15},{4,8},{5,9},{6,10},{7,11},{8,4},{9,5},... | collective-permute-start | bytes 393224 | tf_op jit(solution)/shard_map/ppermute | solution.py:230
  9.9 12.5 %collective-permute-start.2 = (bf16[2,32,2048]{2,1,0:T(8,128)(2,1)S(1)}, bf16[2,32,2048]{2,1,0:T(8,128)(2,1)}, u32[]{:S(2)}, u32[]{:S(2)}) collective-permute-start(bf16[2,32,2048]{2,1,0:T(8,128)(2,1)S(1)} %get-tuple-element.21), channel_id=1, source_target_pairs={{0,4},{1,5},{2,6},{3,7},{4,0},{5,1},{6,2},{7,3},{8,12},{9,13},{10,... | collective-permute-start | bytes 786440 | tf_op jit(solution)/shard_map/ppermute | solution.py:230
  10.2 1.2 %copy-start.2 = (bf16[256,2048]{1,0:T(8,128)(2,1)S(1)}, bf16[256,2048]{1,0:T(8,128)(2,1)}, u32[]{:S(2)}) copy-start(bf16[256,2048]{1,0:T(8,128)(2,1)} %q_ref.5) | copy-start | bytes 3145732
  22.4 8.0 %copy-start.3 = (bf16[256,2048]{1,0:T(8,128)(2,1)S(1)}, bf16[256,2048]{1,0:T(8,128)(2,1)}, u32[]{:S(2)}) copy-start(bf16[256,2048]{1,0:T(8,128)(2,1)} %q_ref.5) | copy-start | bytes 3145732
  23.6 6.3 %collective-permute-start.5 = (bf16[2,128,2048]{2,1,0:T(8,128)(2,1)S(1)}, bf16[2,128,2048]{2,1,0:T(8,128)(2,1)S(1)}, u32[]{:S(2)}, u32[]{:S(2)}) collective-permute-start(bf16[2,128,2048]{2,1,0:T(8,128)(2,1)S(1)} %pad_maximum_fusion), channel_id=1, source_target_pairs={{0,1},{1,0},{2,3},{3,2},{4,5},{5,4},{6,7},{7,6},{8,9},{9,8},{10,11... | collective-permute-start | bytes 3145736 | tf_op jit(solution)/shard_map/ppermute | solution.py:230
  23.7 29.5 %collective-permute-start = (bf16[2,128,2048]{2,1,0:T(8,128)(2,1)S(1)}, bf16[2,128,2048]{2,1,0:T(8,128)(2,1)S(1)}, u32[]{:S(2)}, u32[]{:S(2)}) collective-permute-start(bf16[2,128,2048]{2,1,0:T(8,128)(2,1)S(1)} %get-tuple-element.17), channel_id=1, source_target_pairs={{1,2},{3,4},{5,6},{7,8},{9,10},{11,12},{13,14},{2,1},{4,3},{6,5},{... | collective-permute-start | bytes 3145736 | tf_op jit(solution)/shard_map/ppermute | solution.py:270
  24.6 28.5 %collective-permute-start.7 = (bf16[2,32,2048]{2,1,0:T(8,128)(2,1)S(1)}, bf16[2,32,2048]{2,1,0:T(8,128)(2,1)S(1)}, u32[]{:S(2)}, u32[]{:S(2)}) collective-permute-start(bf16[2,32,2048]{2,1,0:T(8,128)(2,1)S(1)} %get-tuple-element.20.after_ref), channel_id=1, source_target_pairs={{0,4},{1,5},{2,6},{3,7},{4,0},{5,1},{6,2},{7,3},{8,12},{9,13},{10,... | collective-permute-start | bytes 786440 | tf_op jit(solution)/shard_map/ppermute | solution.py:230
  27.9 19.5 %collective-permute-start.8 = (bf16[2,16,2048]{2,1,0:T(8,128)(2,1)S(1)}, bf16[2,16,2048]{2,1,0:T(8,128)(2,1)S(1)}, u32[]{:S(2)}, u32[]{:S(2)}) collective-permute-start(bf16[2,16,2048]{2,1,0:T(8,128)(2,1)S(1)} %get-tuple-element.25), channel_id=1, source_target_pairs={{0,8},{1,9},{2,10},{3,11},{4,12},{5,13},{6,14},{7,15},{8,0},{9,1},... | collective-permute-start | bytes 393224 | tf_op jit(solution)/shard_map/ppermute | solution.py:230
  29.9 23.2 %collective-permute-start.9 = (bf16[2,16,2048]{2,1,0:T(8,128)(2,1)S(1)}, bf16[2,16,2048]{2,1,0:T(8,128)(2,1)S(1)}, u32[]{:S(2)}, u32[]{:S(2)}) collective-permute-start(bf16[2,16,2048]{2,1,0:T(8,128)(2,1)S(1)} %get-tuple-element.25), channel_id=1, source_target_pairs={{0,12},{1,13},{2,14},{3,15},{4,8},{5,9},{6,10},{7,11},{8,4},{9,5},... | collective-permute-start | bytes 393224 | tf_op jit(solution)/shard_map/ppermute | solution.py:230
  53.1 2.0 %collective-permute-start.10 = (bf16[2,64,2048]{2,1,0:T(8,128)(2,1)S(1)}, bf16[2,64,2048]{2,1,0:T(8,128)(2,1)S(1)}, u32[]{:S(2)}, u32[]{:S(2)}) collective-permute-start(bf16[2,64,2048]{2,1,0:T(8,128)(2,1)S(1)} %late.1.late_ref), channel_id=1, source_target_pairs={{0,1},{1,0},{2,3},{3,2},{4,5},{5,4},{6,7},{7,6},{8,9},{9,8},{10,11... | collective-permute-start | bytes 1572872 | tf_op jit(solution)/shard_map/ppermute | solution.py:230

commit v3 on v2

v3 whole, which is shorter than its diff:
```python
import functools
import math

import jax
import jax.numpy as jnp
from jax import lax
from jax.experimental import pallas as pl
from jax.experimental.pallas import tpu as pltpu
from jax.sharding import PartitionSpec as P

HEADS = 16
HEAD_DIM = 128
BLOCK = 128
neg_large = -1e30
log_two = 0.6931471805599453
to_log2 = 1.0 / (math.sqrt(HEAD_DIM) * log_two)
VMEM = pl.BlockSpec(memory_space=pltpu.VMEM)
ANY = pl.BlockSpec(memory_space=pl.ANY)
SMEM = pl.BlockSpec(memory_space=pltpu.SMEM)


def dot(left, right):
    return lax.dot_general(
        left, right, (((1,), (0,)), ((), ())), preferred_element_type=jnp.float32
    )


def dot_t(left, right):
    return lax.dot_general(
        left, right, (((1,), (1,)), ((), ())), preferred_element_type=jnp.float32
    )


def iota(shape, dim):
    return lax.broadcasted_iota(jnp.int32, shape, dim)


def halve(rows):
    shape = (rows.shape[0] // 2, rows.shape[0])
    pairs = jnp.where(iota(shape, 1) >> 1 == iota(shape, 0), 0.5, 0.0).astype(jnp.bfloat16)
    return dot(pairs, rows).astype(jnp.bfloat16)


def repeated_halve(rows, level):
    count = rows.shape[0]
    shape = (count, count)
    first = iota(shape, 0) >> level << level
    hit = (iota(shape, 1) == first) | (iota(shape, 1) == first + (1 << level - 1))
    return dot(jnp.where(hit, 0.5, 0.0).astype(jnp.bfloat16), rows).astype(jnp.bfloat16)


def with_ones(values):
    return jnp.concatenate([values, jnp.ones(values.shape, values.dtype)], axis=1)


def row_max(scores):
    return jnp.max(scores, axis=1, keepdims=True)


def own_pool_kernel(core_ref, kv_ref, edge_ref, *out_refs):
    outer = pl.ds(pl.multiple_of(core_ref[0] * BLOCK, BLOCK), BLOCK)
    edge_ref[...] = kv_ref[:, outer, :]
    for which in range(2):
        rows = halve(kv_ref[which])
        for out_ref in out_refs:
            rows = halve(rows)
            out_ref[which] = rows


def side_pool_kernel(*refs):
    kv_ref, _, *out_refs = refs[-4:]
    for which in range(2):
        rows = kv_ref[which]
        for out_ref in out_refs:
            rows = halve(rows)
            out_ref[which] = rows


def join_kernel(after_1, after_2, *refs):
    start = 0
    for ref in refs[:-1]:
        refs[-1][:, start : start + ref.shape[1], :] = ref[...]
        start += ref.shape[1]


def ups_kernel(after_ref, q_ref, *refs):
    up = q_ref[...]
    for level, ref in enumerate(refs, 1):
        up = repeated_halve(up, level)
        ref[...] = up


def own_kernel(after_ref, q_ref, kv_ref, mean_ref, log_ref):
    for head in range(HEADS):
        cols = slice(head * HEAD_DIM, (head + 1) * HEAD_DIM)
        scores = dot_t(q_ref[:, cols], kv_ref[0, :, cols])
        peak = row_max(scores) * to_log2
        weights = jnp.exp2(scores * to_log2 - peak).astype(jnp.bfloat16)
        both = dot(weights, with_ones(kv_ref[1, :, cols]))
        total = both[:, HEAD_DIM:]
        mean_ref[:, cols] = both[:, :HEAD_DIM] / total
        log_ref[:, cols] = jnp.log2(total) + peak


def by_core(core_ref, body):
    blocks = slice(0, BLOCK), slice(BLOCK, 2 * BLOCK)

    @pl.when(core_ref[0] == 0)
    def _():
        body(*blocks)

    @pl.when(core_ref[0] == 1)
    def _():
        body(*blocks[::-1])


def attend(first, second, cols, fine, bias, coarse, mean_ref, log_ref):
    def rows(ref):
        return jnp.concatenate([ref[first, cols], ref[second, cols]], axis=0)

    query_ref, key, value = fine
    near = dot_t(query_ref[first, cols], key)
    if bias is not None:
        near = near + bias
    scores = [dot_t(rows(level[0]), level[1]) for level in coarse]
    peak = functools.reduce(jnp.maximum, scores)
    peak = jnp.concatenate([jnp.maximum(peak[:BLOCK], near), peak[BLOCK:]], axis=0)
    logs = rows(log_ref)
    peak = jnp.maximum(row_max(peak) * to_log2, logs)
    weights = [
        jnp.exp2(score * to_log2 - (peak - level)).astype(jnp.bfloat16)
        for score, (_, _, _, level) in zip(scores, coarse)
    ]
    values = jnp.concatenate([level[2] for level in coarse], axis=0)
    both = dot(jnp.concatenate(weights, axis=1), with_ones(values))
    weights = jnp.exp2(near * to_log2 - peak[:BLOCK]).astype(jnp.bfloat16)
    near = dot(weights, with_ones(value))
    both = jnp.concatenate([both[:BLOCK] + near, both[BLOCK:]], axis=0)
    factor = jnp.exp2(logs - peak)
    total = both[:, HEAD_DIM:] + factor
    mean = (both[:, :HEAD_DIM] + factor * rows(mean_ref)) / total
    return mean, total, peak


def near_kernel(after_1, after_2, after_3, after_4, core_ref, q_ref, up_1_ref, up_2_ref, inner_ref, mine_ref, theirs_ref, mean_ref, log_ref, *refs):
    new_mean_ref, new_log_ref, keys_ref, values_ref = refs
    keys_ref[...] = halve(inner_ref[0])
    values_ref[...] = halve(inner_ref[1])
    by_core(core_ref, functools.partial(near_body, q_ref, inner_ref, mine_ref, theirs_ref, mean_ref, log_ref, new_mean_ref, new_log_ref, up_1_ref, up_2_ref, keys_ref, values_ref))


def near_body(q_ref, inner_ref, mine_ref, theirs_ref, mean_ref, log_ref, new_mean_ref, new_log_ref, up_1_ref, up_2_ref, keys_ref, values_ref, edge, other):
    for head in range(HEADS):
        cols = slice(head * HEAD_DIM, (head + 1) * HEAD_DIM)
        mean, total, peak = attend(
            other,
            edge,
            cols,
            (q_ref, inner_ref[0, edge, cols], inner_ref[1, edge, cols]),
            None,
            [
                (up_1_ref, keys_ref[:, cols], values_ref[:, cols], 1.0),
                (
                    up_2_ref,
                    jnp.concatenate([mine_ref[0, :, cols], theirs_ref[0, :, cols]], 0),
                    jnp.concatenate([mine_ref[1, :, cols], theirs_ref[1, :, cols]], 0),
                    2.0,
                ),
            ],
            mean_ref,
            log_ref,
        )
        logs = jnp.log2(total) + peak
        new_mean_ref[other, cols] = mean[:BLOCK]
        new_mean_ref[edge, cols] = mean[BLOCK:]
        new_log_ref[other, cols] = logs[:BLOCK]
        new_log_ref[edge, cols] = logs[BLOCK:]


def far_kernel(core_ref, q_ref, edge_ref, mine_ref, theirs_ref, mean_ref, log_ref, *refs):
    out_ref = refs[-1]
    count = len(refs) // 2 + 1
    up_refs = refs[:count]
    more_refs = refs[count:-1]
    by_core(core_ref, functools.partial(far_body, core_ref,q_ref, edge_ref, mine_ref, theirs_ref, mean_ref, log_ref, up_refs, more_refs, out_ref))


def far_body(core_ref,q_ref, edge_ref, mine_ref, theirs_ref, mean_ref, log_ref, up_refs, more_refs, out_ref, edge, other):
    bias = jnp.where(core_ref[1] == 1, 0.0, neg_large)
    for head in range(HEADS):
        cols = slice(head * HEAD_DIM, (head + 1) * HEAD_DIM)

        def parts(which, level):
            part = slice(64 * (level - 3), 64 * (level - 2))
            return jnp.concatenate([mine_ref[which, part, cols], theirs_ref[which, part, cols]], 0)

        coarse = [
            (up_refs[level - 3], parts(0, level), parts(1, level), float(level))
            for level in (3, 4)
        ]
        for level, more_ref in enumerate(more_refs, 5):
            coarse.append(
                (up_refs[level - 3], more_ref[0, :, cols], more_ref[1, :, cols], float(level))
            )
        mean, _, _ = attend(
            edge,
            other,
            cols,
            (q_ref, edge_ref[0, :, cols], edge_ref[1, :, cols]),
            bias,
            coarse,
            mean_ref,
            log_ref,
        )
        mean = mean.astype(out_ref.dtype)
        out_ref[edge, cols] = mean[:BLOCK]
        out_ref[other, cols] = mean[BLOCK:]


def call(kernel, in_specs, outputs, name, micros, *inputs, scratch=(), aliases=()):
    return pl.pallas_call(
        kernel,
        in_specs=in_specs,
        out_specs=[VMEM] * len(outputs),
        out_shape=[jax.ShapeDtypeStruct(shape, dtype) for shape, dtype in outputs],
        scratch_shapes=[pltpu.VMEM(shape, dtype) for shape, dtype in scratch],
        cost_estimate=pl.CostEstimate(
            flops=micros * 1_000_000_000, bytes_accessed=0, transcendentals=0
        ),
        input_output_aliases=dict(aliases),
        compiler_params=pltpu.CompilerParams(vmem_limit_bytes=16 << 20),
        name=name,
    )(*inputs)


def sent(array, stride):
    count = lax.axis_size("seq")
    return lax.ppermute(array, "seq", [(i, i ^ stride) for i in range(count)])


def halve_rows(pairs):
    wide = pairs.reshape(2, pairs.shape[1] // 2, 2, pairs.shape[2]).astype(jnp.float32)
    return ((wide[:, :, 0] + wide[:, :, 1]) * 0.5).astype(jnp.bfloat16)


def on_device(queries, keyval):
    count = lax.axis_size("seq")
    levels = count.bit_length() - 1
    index = lax.axis_index("seq")
    core = index % 2
    inside = jnp.where(core == 0, index > 0, index < count - 1)
    position = jnp.stack((core, inside.astype(core.dtype)))
    rows, features = queries.shape
    narrow = keyval.dtype
    wide = ((rows, features), jnp.float32)
    up = ((rows, features), narrow)

    def some(count):
        return ((2, count, features), narrow)

    edge, own_2, own_3, own_4 = call(
        own_pool_kernel,
        [SMEM, VMEM],
        [some(BLOCK), some(64), some(32), some(16)],
        "pool",
        0,
        position,
        keyval,
    )
    side_2 = sent(own_2, 2)
    inner = sent(keyval, 1)
    early = [sent(own_3, 4), sent(own_4, 8), sent(own_4, 12)]
    edge, side_3, side_4 = call(
        side_pool_kernel,
        [ANY] * 3 + [VMEM] * 2,
        [some(BLOCK), some(32), some(16)],
        "side",
        0,
        *early,
        edge,
        side_2,
        aliases={3: 0},
    )
    links = [(i, i + 1) for i in range(1, count - 1, 2)]
    edge = lax.ppermute(edge, "seq", links + [(j, i) for i, j in links])
    late = [sent(side_3, 4), sent(side_4, 8), sent(side_4, 12)]
    other_2 = sent(side_2, 1)
    mean, log = call(
        own_kernel, [ANY] + [VMEM] * 2, [wide, wide], "own", 0, side_3, queries, keyval
    )
    up_1, up_2, *ups = call(ups_kernel, [ANY, VMEM], [up] * levels, "ups", 0, side_3, queries)
    mean, log = call(
        near_kernel,
        [ANY] * 4 + [SMEM] + [VMEM] * 8,
        [wide, wide],
        "near",
        0,
        *early,
        side_3,
        position,
        queries,
        up_1,
        up_2,
        inner,
        side_2,
        other_2,
        mean,
        log,
        scratch=[((BLOCK, features), narrow), ((BLOCK, features), narrow)],
    )
    pieces = (early[0], late[0], early[1], early[2], late[1], late[2])
    (late,) = call(join_kernel, [ANY] * 2 + [VMEM] * 6, [some(128)], "join", 0, edge, log, *pieces)
    their_late = sent(late, 1)
    more = []
    if levels > 4:
        own = halve_rows(halve_rows(jnp.concatenate((keyval, inner), axis=1)))
        own = halve_rows(jnp.concatenate((own, side_2, other_2), axis=1))
        own = jnp.concatenate((own, late[:, :64], their_late[:, :64]), axis=1)
        own = jnp.concatenate((halve_rows(own), late[:, 64:], their_late[:, 64:]), axis=1)
        own = halve_rows(own)
        for level in range(5, levels + 1):
            more.append(sent(own, 1 << level - 1))
            own = halve_rows(jnp.concatenate((own, more[-1]), axis=1))
    far = [position, queries, edge, late, their_late, mean, log] + ups + more
    return call(far_kernel, [SMEM] + [VMEM] * (len(far) - 1), [up], "far", 0, *far)[0]


def solution(mesh):
    return jax.shard_map(
        on_device,
        mesh=mesh,
        in_specs=(P(("streams", "seq"), None), P(None, ("streams", "seq"), None)),
        out_specs=P(("streams", "seq"), None),
        check_vma=False,
    )
```

time: 61.4 us -> 58.7 us (0.956)
  Pallas kernels: 21 us -> 14.3 us
  waiting for transfers between devices: 23.2 us -> 28.1 us
  local copies, waits for them, and re-layouts: 2.82 us -> 1.6 us
    pallas_call x7, Pallas kernels: 21 us -> 14.3 us  [call(): pl.pallas_call(kernel, in_specs=in_specs, out_specs=[VMEM] * len(outputs)...]
    ppermute x10, waiting for transfers between devices: 23.2 us -> 28.1 us  [sent(): return lax.ppermute(array, 'seq', [(i, i ^ stride) for i in range(count)])]
    unnamed x8 -> x6, local copies, waits for them, and re-layouts: 2.82 us -> 1.6 us
    ppermute x10, starting transfers between devices: 13 us -> 13.7 us  [sent(): return lax.ppermute(array, 'seq', [(i, i ^ stride) for i in range(count)])]
  transfers between devices with their start and end apart: 11 -> 11, of which waited for: 5 -> 5; matrix products, arithmetic and copies ran while one was open for 0% -> 0% of each run, Pallas kernels for 24% -> 16%
where the time goes in v3:
time: 58.7 us; the launch traced here: 58.6 us
  waiting for transfers between devices  28.1 us (48%)
  starting transfers between devices  14.5 us (25%)
  Pallas kernels  14.3 us (24%)
  local copies, waits for them, and re-layouts  1.6 us (3%)
    ppermute x10, waiting for transfers between devices, sent(): return lax.ppermute(array, 'seq', [(i, i ^ stride) for i in range(count)])  28.1 us
    pallas_call x7, Pallas kernels, call(): pl.pallas_call(kernel, in_specs=in_specs, out_specs=[VMEM] * len(outputs)...  14.3 us
    ppermute x10, starting transfers between devices, sent(): return lax.ppermute(array, 'seq', [(i, i ^ stride) for i in range(count)])  13.7 us
    unnamed x6, local copies, waits for them, and re-layouts  1.6 us
  transfers between devices with their start and end apart: 11, of which 5 were waited for; matrix products, arithmetic and copies ran while one was open for 0% of the time, Pallas kernels for 16%

profile of v3, /device:TPU:0, one launch (start us, length us, event | category | flops | bytes accessed | tf_op | source)
XLA Modules:
  0.0 58.6 jit_solution(9914541262803632896)
XLA Ops:
  0.0 0.5 collective-permute-start.5
  0.5 0.1 pad_add_fusion.core_ref
  0.5 0.0 copy-start.1
  0.5 1.6 %copy-done.1 = bf16[2,256,2048]{2,1,0:T(8,128)(2,1)S(1)} copy-done((bf16[2,256,2048]{2,1,0:T(8,128)(2,1)S(1)}, bf16[2,256,2048]{2,1,0:T(8,128)(2,1)}, u32[]{:S(2)}) %copy-start.1) | copy-done | bytes 2097176
  2.1 0.0 copy-start
  2.1 1.9 %pool.1 = (bf16[2,128,2048]{2,1,0:T(8,128)(2,1)S(1)}, bf16[2,64,2048]{2,1,0:T(8,128)(2,1)S(1)}, bf16[2,32,2048]{2,1,0:T(8,128)(2,1)S(1)}, bf16[2,16,2048]{2,1,0:T(8,128)(2,1)S(1)}) custom-call(s32[2]{0:T(128)S(1)} %pad_add_fusion.core_ref, bf16[2,256,2048]{2,1,0:T(8,128)(2,1)S(1)} %copy-done.1), custom_call_target="tpu_custom_call" | custom-call | tf_op jit(solution)/shard_map/pool/pallas_call | solution.py:221
  4.0 0.0 copy-start.2
  4.0 2.6 %collective-permute-start.3 = (bf16[2,64,2048]{2,1,0:T(8,128)(2,1)S(1)}, bf16[2,64,2048]{2,1,0:T(8,128)(2,1)S(1)}, u32[]{:S(2)}, u32[]{:S(2)}) collective-permute-start(bf16[2,64,2048]{2,1,0:T(8,128)(2,1)S(1)} %get-tuple-element.23), channel_id=1, source_target_pairs={{0,2},{1,3},{2,0},{3,1},{4,6},{5,7},{6,4},{7,5},{8,10},{9,11},{10,... | collective-permute-start | bytes 1572872 | tf_op jit(solution)/shard_map/ppermute | solution.py:238
  6.6 1.6 %collective-permute-start = (bf16[2,32,2048]{2,1,0:T(8,128)(2,1)S(1)}, bf16[2,32,2048]{2,1,0:T(8,128)(2,1)S(1)}, u32[]{:S(2)}, u32[]{:S(2)}) collective-permute-start(bf16[2,32,2048]{2,1,0:T(8,128)(2,1)S(1)} %get-tuple-element.20), channel_id=1, source_target_pairs={{0,4},{1,5},{2,6},{3,7},{4,0},{5,1},{6,2},{7,3},{8,12},{9,13},{10,... | collective-permute-start | bytes 786440 | tf_op jit(solution)/shard_map/ppermute | solution.py:238
  8.2 2.6 %collective-permute-start.1 = (bf16[2,16,2048]{2,1,0:T(8,128)(2,1)S(1)}, bf16[2,16,2048]{2,1,0:T(8,128)(2,1)S(1)}, u32[]{:S(2)}, u32[]{:S(2)}) collective-permute-start(bf16[2,16,2048]{2,1,0:T(8,128)(2,1)S(1)} %get-tuple-element.21), channel_id=1, source_target_pairs={{0,8},{1,9},{2,10},{3,11},{4,12},{5,13},{6,14},{7,15},{8,0},{9,1},... | collective-permute-start | bytes 393224 | tf_op jit(solution)/shard_map/ppermute | solution.py:238
  10.8 0.2 collective-permute-start.2
  11.0 6.7 %collective-permute-done.1.refs_1_.after_2.refs_2_ = bf16[2,16,2048]{2,1,0:T(8,128)(2,1)S(1)} collective-permute-done((bf16[2,16,2048]{2,1,0:T(8,128)(2,1)S(1)}, bf16[2,16,2048]{2,1,0:T(8,128)(2,1)S(1)}, u32[]{:S(2)}, u32[]{:S(2)}) %collective-permute-start.1) | collective-permute-done | bytes 131104 | tf_op jit(solution)/shard_map/ppermute | solution.py:238
  17.7 5.1 %collective-permute-done.2.refs_2_.after_3.refs_3_ = bf16[2,16,2048]{2,1,0:T(8,128)(2,1)S(1)} collective-permute-done((bf16[2,16,2048]{2,1,0:T(8,128)(2,1)S(1)}, bf16[2,16,2048]{2,1,0:T(8,128)(2,1)S(1)}, u32[]{:S(2)}, u32[]{:S(2)}) %collective-permute-start.2) | collective-permute-done | bytes 131104 | tf_op jit(solution)/shard_map/ppermute | solution.py:238
  22.8 0.0 collective-permute-done.refs_0_.after_1
  22.8 0.0 collective-permute-done.3.refs_4_.mine_ref
  22.8 0.4 side.1
  23.3 0.7 %collective-permute-start.4 = (bf16[2,128,2048]{2,1,0:T(8,128)(2,1)S(1)}, bf16[2,128,2048]{2,1,0:T(8,128)(2,1)S(1)}, u32[]{:S(2)}, u32[]{:S(2)}) collective-permute-start(bf16[2,128,2048]{2,1,0:T(8,128)(2,1)S(1)} %get-tuple-element.24), channel_id=1, source_target_pairs={{1,2},{3,4},{5,6},{7,8},{9,10},{11,12},{13,14},{2,1},{4,3},{6,5},{... | collective-permute-start | bytes 3145736 | tf_op jit(solution)/shard_map/ppermute | solution.py:285
  24.0 1.9 %collective-permute-start.6 = (bf16[2,64,2048]{2,1,0:T(8,128)(2,1)S(1)}, bf16[2,64,2048]{2,1,0:T(8,128)(2,1)S(1)}, u32[]{:S(2)}, u32[]{:S(2)}) collective-permute-start(bf16[2,64,2048]{2,1,0:T(8,128)(2,1)S(1)} %collective-permute-done.3.refs_4_.mine_ref), channel_id=1, source_target_pairs={{0,1},{1,0},{2,3},{3,2},{4,5},{5,4},{6,7},{7,6},{8,9},{9,8},{10,11... | collective-permute-start | bytes 1572872 | tf_op jit(solution)/shard_map/ppermute | solution.py:238
  25.9 0.7 %collective-permute-start.7 = (bf16[2,32,2048]{2,1,0:T(8,128)(2,1)S(1)}, bf16[2,32,2048]{2,1,0:T(8,128)(2,1)S(1)}, u32[]{:S(2)}, u32[]{:S(2)}) collective-permute-start(bf16[2,32,2048]{2,1,0:T(8,128)(2,1)S(1)} %get-tuple-element.25.after_ref.after_4), channel_id=1, source_target_pairs={{0,4},{1,5},{2,6},{3,7},{4,0},{5,1},{6,2},{7,3},{8,12},{9,13},{10,... | collective-permute-start | bytes 786440 | tf_op jit(solution)/shard_map/ppermute | solution.py:238
  26.5 1.4 %collective-permute-start.8 = (bf16[2,16,2048]{2,1,0:T(8,128)(2,1)S(1)}, bf16[2,16,2048]{2,1,0:T(8,128)(2,1)S(1)}, u32[]{:S(2)}, u32[]{:S(2)}) collective-permute-start(bf16[2,16,2048]{2,1,0:T(8,128)(2,1)S(1)} %get-tuple-element.31), channel_id=1, source_target_pairs={{0,8},{1,9},{2,10},{3,11},{4,12},{5,13},{6,14},{7,15},{8,0},{9,1},... | collective-permute-start | bytes 393224 | tf_op jit(solution)/shard_map/ppermute | solution.py:238
  27.9 0.0 collective-permute-done.6.theirs_ref
  27.9 2.4 %collective-permute-start.9 = (bf16[2,16,2048]{2,1,0:T(8,128)(2,1)S(1)}, bf16[2,16,2048]{2,1,0:T(8,128)(2,1)S(1)}, u32[]{:S(2)}, u32[]{:S(2)}) collective-permute-start(bf16[2,16,2048]{2,1,0:T(8,128)(2,1)S(1)} %get-tuple-element.31), channel_id=1, source_target_pairs={{0,12},{1,13},{2,14},{3,15},{4,8},{5,9},{6,10},{7,11},{8,4},{9,5},... | collective-permute-start | bytes 393224 | tf_op jit(solution)/shard_map/ppermute | solution.py:238
  30.2 0.0 copy-done
  30.2 1.3 %ups.1 = (bf16[256,2048]{1,0:T(8,128)(2,1)S(1)}, bf16[256,2048]{1,0:T(8,128)(2,1)S(1)}, bf16[256,2048]{1,0:T(8,128)(2,1)S(1)}, bf16[256,2048]{1,0:T(8,128)(2,1)S(1)}) custom-call(bf16[2,32,2048]{2,1,0:T(8,128)(2,1)S(1)} %get-tuple-element.25.after_ref.after_4, bf16[256,2048]{1,0:T(8,128)(2,1)S(1)} %copy-done), custom_call_target="tpu_custom_call" | custom-call | tf_op jit(solution)/shard_map/ups/pallas_call | solution.py:221
  31.6 0.0 copy-done.2
  31.6 1.6 %own.1 = (f32[256,2048]{1,0:T(8,128)S(1)}, f32[256,2048]{1,0:T(8,128)S(1)}) custom-call(bf16[2,32,2048]{2,1,0:T(8,128)(2,1)S(1)} %get-tuple-element.25.after_ref.after_4, bf16[256,2048]{1,0:T(8,128)(2,1)S(1)} %copy-done, bf16[2,256,2048]{2,1,0:T(8,128)(2,1)S(1)} %copy-done.2), custom_call_target="tpu_custom_call" | custom-call | tf_op jit(solution)/shard_map/own/pallas_call | solution.py:221
  33.2 0.0 collective-permute-done.5.inner_ref
  33.2 4.1 %near.1 = (f32[256,2048]{1,0:T(8,128)S(1)}, f32[256,2048]{1,0:T(8,128)S(1)}) custom-call(bf16[2,32,2048]{2,1,0:T(8,128)(2,1)S(1)} %collective-permute-done.refs_0_.after_1, bf16[2,16,2048]{2,1,0:T(8,128)(2,1)S(1)} %collective-permute-done.1.refs_1_.after_2.refs_2_, bf16[2,16,2048]{2,1,0:T(8,128)(2,1)S(1)} %collective-permute-done.2.refs_2_.after_3.refs_3_, ...), custom_call_target="tpu_custom_call" | custom-call | tf_op jit(solution)/shard_map/near/pallas_call | solution.py:221
  37.4 9.4 %collective-permute-done.8.refs_4_ = bf16[2,16,2048]{2,1,0:T(8,128)(2,1)S(1)} collective-permute-done((bf16[2,16,2048]{2,1,0:T(8,128)(2,1)S(1)}, bf16[2,16,2048]{2,1,0:T(8,128)(2,1)S(1)}, u32[]{:S(2)}, u32[]{:S(2)}) %collective-permute-start.8) | collective-permute-done | bytes 131104 | tf_op jit(solution)/shard_map/ppermute | solution.py:238
  46.8 4.2 %collective-permute-done.9.refs_5_ = bf16[2,16,2048]{2,1,0:T(8,128)(2,1)S(1)} collective-permute-done((bf16[2,16,2048]{2,1,0:T(8,128)(2,1)S(1)}, bf16[2,16,2048]{2,1,0:T(8,128)(2,1)S(1)}, u32[]{:S(2)}, u32[]{:S(2)}) %collective-permute-start.9) | collective-permute-done | bytes 131104 | tf_op jit(solution)/shard_map/ppermute | solution.py:238
  51.0 0.0 collective-permute-done.7.refs_1_
  51.0 0.0 collective-permute-done.4.after_1.edge_ref
  51.0 0.1 join.1.mine_ref
  51.1 0.1 collective-permute-start.10
  51.2 2.6 %collective-permute-done.10.theirs_ref = bf16[2,128,2048]{2,1,0:T(8,128)(2,1)S(1)} collective-permute-done((bf16[2,128,2048]{2,1,0:T(8,128)(2,1)S(1)}, bf16[2,128,2048]{2,1,0:T(8,128)(2,1)S(1)}, u32[]{:S(2)}, u32[]{:S(2)}) %collective-permute-start.10) | collective-permute-done | bytes 1048608 | tf_op jit(solution)/shard_map/ppermute | solution.py:238
  53.8 4.8 %far.1 = bf16[256,2048]{1,0:T(8,128)(2,1)} custom-call(s32[2]{0:T(128)S(1)} %pad_add_fusion.core_ref, bf16[256,2048]{1,0:T(8,128)(2,1)S(1)} %copy-done, bf16[2,128,2048]{2,1,0:T(8,128)(2,1)S(1)} %collective-permute-done.4.after_1.edge_ref, bf16[2,128,2048]{2,1,0:T(8,128)(2,1)S(1)} %join.1.mine_ref, ...), custom_call_target="tpu_custom_call" | custom-call | tf_op jit(solution)/shard_map/far/pallas_call | solution.py:221
Async XLA Ops:
  0.0 33.2 %collective-permute-start.5 = (bf16[2,256,2048]{2,1,0:T(8,128)(2,1)}, bf16[2,256,2048]{2,1,0:T(8,128)(2,1)S(1)}, u32[]{:S(2)}, u32[]{:S(2)}) collective-permute-start(bf16[2,256,2048]{2,1,0:T(8,128)(2,1)} %kv_ref.3), channel_id=1, source_target_pairs={{0,1},{1,0},{2,3},{3,2},{4,5},{5,4},{6,7},{7,6},{8,9},{9,8},{10,11... | collective-permute-start | bytes 6291464 | tf_op jit(solution)/shard_map/ppermute | solution.py:238
  0.5 1.6 %copy-start.1 = (bf16[2,256,2048]{2,1,0:T(8,128)(2,1)S(1)}, bf16[2,256,2048]{2,1,0:T(8,128)(2,1)}, u32[]{:S(2)}) copy-start(bf16[2,256,2048]{2,1,0:T(8,128)(2,1)} %kv_ref.3) | copy-start | bytes 6291460
  2.1 28.1 %copy-start = (bf16[256,2048]{1,0:T(8,128)(2,1)S(1)}, bf16[256,2048]{1,0:T(8,128)(2,1)}, u32[]{:S(2)}) copy-start(bf16[256,2048]{1,0:T(8,128)(2,1)} %q_ref.7) | copy-start | bytes 3145732
  4.0 27.6 %copy-start.2 = (bf16[2,256,2048]{2,1,0:T(8,128)(2,1)S(1)}, bf16[2,256,2048]{2,1,0:T(8,128)(2,1)}, u32[]{:S(2)}) copy-start(bf16[2,256,2048]{2,1,0:T(8,128)(2,1)} %kv_ref.3) | copy-start | bytes 6291460
  4.0 18.8 %collective-permute-start.3 = (bf16[2,64,2048]{2,1,0:T(8,128)(2,1)S(1)}, bf16[2,64,2048]{2,1,0:T(8,128)(2,1)S(1)}, u32[]{:S(2)}, u32[]{:S(2)}) collective-permute-start(bf16[2,64,2048]{2,1,0:T(8,128)(2,1)S(1)} %get-tuple-element.23), channel_id=1, source_target_pairs={{0,2},{1,3},{2,0},{3,1},{4,6},{5,7},{6,4},{7,5},{8,10},{9,11},{10,... | collective-permute-start | bytes 1572872 | tf_op jit(solution)/shard_map/ppermute | solution.py:238
  6.6 16.2 %collective-permute-start = (bf16[2,32,2048]{2,1,0:T(8,128)(2,1)S(1)}, bf16[2,32,2048]{2,1,0:T(8,128)(2,1)S(1)}, u32[]{:S(2)}, u32[]{:S(2)}) collective-permute-start(bf16[2,32,2048]{2,1,0:T(8,128)(2,1)S(1)} %get-tuple-element.20), channel_id=1, source_target_pairs={{0,4},{1,5},{2,6},{3,7},{4,0},{5,1},{6,2},{7,3},{8,12},{9,13},{10,... | collective-permute-start | bytes 786440 | tf_op jit(solution)/shard_map/ppermute | solution.py:238
  8.2 9.5 %collective-permute-start.1 = (bf16[2,16,2048]{2,1,0:T(8,128)(2,1)S(1)}, bf16[2,16,2048]{2,1,0:T(8,128)(2,1)S(1)}, u32[]{:S(2)}, u32[]{:S(2)}) collective-permute-start(bf16[2,16,2048]{2,1,0:T(8,128)(2,1)S(1)} %get-tuple-element.21), channel_id=1, source_target_pairs={{0,8},{1,9},{2,10},{3,11},{4,12},{5,13},{6,14},{7,15},{8,0},{9,1},... | collective-permute-start | bytes 393224 | tf_op jit(solution)/shard_map/ppermute | solution.py:238
  10.8 12.0 %collective-permute-start.2 = (bf16[2,16,2048]{2,1,0:T(8,128)(2,1)S(1)}, bf16[2,16,2048]{2,1,0:T(8,128)(2,1)S(1)}, u32[]{:S(2)}, u32[]{:S(2)}) collective-permute-start(bf16[2,16,2048]{2,1,0:T(8,128)(2,1)S(1)} %get-tuple-element.21), channel_id=1, source_target_pairs={{0,12},{1,13},{2,14},{3,15},{4,8},{5,9},{6,10},{7,11},{8,4},{9,5},... | collective-permute-start | bytes 393224 | tf_op jit(solution)/shard_map/ppermute | solution.py:238
  23.3 27.8 %collective-permute-start.4 = (bf16[2,128,2048]{2,1,0:T(8,128)(2,1)S(1)}, bf16[2,128,2048]{2,1,0:T(8,128)(2,1)S(1)}, u32[]{:S(2)}, u32[]{:S(2)}) collective-permute-start(bf16[2,128,2048]{2,1,0:T(8,128)(2,1)S(1)} %get-tuple-element.24), channel_id=1, source_target_pairs={{1,2},{3,4},{5,6},{7,8},{9,10},{11,12},{13,14},{2,1},{4,3},{6,5},{... | collective-permute-start | bytes 3145736 | tf_op jit(solution)/shard_map/ppermute | solution.py:285
  24.0 3.9 %collective-permute-start.6 = (bf16[2,64,2048]{2,1,0:T(8,128)(2,1)S(1)}, bf16[2,64,2048]{2,1,0:T(8,128)(2,1)S(1)}, u32[]{:S(2)}, u32[]{:S(2)}) collective-permute-start(bf16[2,64,2048]{2,1,0:T(8,128)(2,1)S(1)} %collective-permute-done.3.refs_4_.mine_ref), channel_id=1, source_target_pairs={{0,1},{1,0},{2,3},{3,2},{4,5},{5,4},{6,7},{7,6},{8,9},{9,8},{10,11... | collective-permute-start | bytes 1572872 | tf_op jit(solution)/shard_map/ppermute | solution.py:238
  25.9 25.2 %collective-permute-start.7 = (bf16[2,32,2048]{2,1,0:T(8,128)(2,1)S(1)}, bf16[2,32,2048]{2,1,0:T(8,128)(2,1)S(1)}, u32[]{:S(2)}, u32[]{:S(2)}) collective-permute-start(bf16[2,32,2048]{2,1,0:T(8,128)(2,1)S(1)} %get-tuple-element.25.after_ref.after_4), channel_id=1, source_target_pairs={{0,4},{1,5},{2,6},{3,7},{4,0},{5,1},{6,2},{7,3},{8,12},{9,13},{10,... | collective-permute-start | bytes 786440 | tf_op jit(solution)/shard_map/ppermute | solution.py:238
  26.5 20.3 %collective-permute-start.8 = (bf16[2,16,2048]{2,1,0:T(8,128)(2,1)S(1)}, bf16[2,16,2048]{2,1,0:T(8,128)(2,1)S(1)}, u32[]{:S(2)}, u32[]{:S(2)}) collective-permute-start(bf16[2,16,2048]{2,1,0:T(8,128)(2,1)S(1)} %get-tuple-element.31), channel_id=1, source_target_pairs={{0,8},{1,9},{2,10},{3,11},{4,12},{5,13},{6,14},{7,15},{8,0},{9,1},... | collective-permute-start | bytes 393224 | tf_op jit(solution)/shard_map/ppermute | solution.py:238
  27.9 23.1 %collective-permute-start.9 = (bf16[2,16,2048]{2,1,0:T(8,128)(2,1)S(1)}, bf16[2,16,2048]{2,1,0:T(8,128)(2,1)S(1)}, u32[]{:S(2)}, u32[]{:S(2)}) collective-permute-start(bf16[2,16,2048]{2,1,0:T(8,128)(2,1)S(1)} %get-tuple-element.31), channel_id=1, source_target_pairs={{0,12},{1,13},{2,14},{3,15},{4,8},{5,9},{6,10},{7,11},{8,4},{9,5},... | collective-permute-start | bytes 393224 | tf_op jit(solution)/shard_map/ppermute | solution.py:238
  51.1 2.7 %collective-permute-start.10 = (bf16[2,128,2048]{2,1,0:T(8,128)(2,1)S(1)}, bf16[2,128,2048]{2,1,0:T(8,128)(2,1)S(1)}, u32[]{:S(2)}, u32[]{:S(2)}) collective-permute-start(bf16[2,128,2048]{2,1,0:T(8,128)(2,1)S(1)} %join.1.mine_ref), channel_id=1, source_target_pairs={{0,1},{1,0},{2,3},{3,2},{4,5},{5,4},{6,7},{7,6},{8,9},{9,8},{10,11... | collective-permute-start | bytes 3145736 | tf_op jit(solution)/shard_map/ppermute | solution.py:238

commit v4 on v3

--- a/solution.py
+++ b/solution.py
@@ -11,6 +11,7 @@
 HEADS = 16
 HEAD_DIM = 128
 BLOCK = 128
+GROUP = 8
 neg_large = -1e30
 log_two = 0.6931471805599453
 to_log2 = 1.0 / (math.sqrt(HEAD_DIM) * log_two)
@@ -114,17 +115,16 @@
         body(*blocks[::-1])
 
 
-def attend(first, second, cols, fine, bias, coarse, mean_ref, log_ref):
+def attend(first, second, cols, fine, coarse, mean_ref, log_ref):
     def rows(ref):
         return jnp.concatenate([ref[first, cols], ref[second, cols]], axis=0)
 
-    query_ref, key, value = fine
-    near = dot_t(query_ref[first, cols], key)
-    if bias is not None:
-        near = near + bias
     scores = [dot_t(rows(level[0]), level[1]) for level in coarse]
     peak = functools.reduce(jnp.maximum, scores)
-    peak = jnp.concatenate([jnp.maximum(peak[:BLOCK], near), peak[BLOCK:]], axis=0)
+    if fine is not None:
+        query_ref, key, value = fine
+        near = dot_t(query_ref[first, cols], key)
+        peak = jnp.concatenate([jnp.maximum(peak[:BLOCK], near), peak[BLOCK:]], axis=0)
     logs = rows(log_ref)
     peak = jnp.maximum(row_max(peak) * to_log2, logs)
     weights = [
@@ -133,23 +133,24 @@
     ]
     values = jnp.concatenate([level[2] for level in coarse], axis=0)
     both = dot(jnp.concatenate(weights, axis=1), with_ones(values))
-    weights = jnp.exp2(near * to_log2 - peak[:BLOCK]).astype(jnp.bfloat16)
-    near = dot(weights, with_ones(value))
-    both = jnp.concatenate([both[:BLOCK] + near, both[BLOCK:]], axis=0)
+    if fine is not None:
+        weights = jnp.exp2(near * to_log2 - peak[:BLOCK]).astype(jnp.bfloat16)
+        near = dot(weights, with_ones(value))
+        both = jnp.concatenate([both[:BLOCK] + near, both[BLOCK:]], axis=0)
     factor = jnp.exp2(logs - peak)
     total = both[:, HEAD_DIM:] + factor
     mean = (both[:, :HEAD_DIM] + factor * rows(mean_ref)) / total
     return mean, total, peak
 
 
-def near_kernel(after_1, after_2, after_3, after_4, core_ref, q_ref, up_1_ref, up_2_ref, inner_ref, mine_ref, theirs_ref, mean_ref, log_ref, *refs):
+def near_kernel(after_1, after_2, after_3, after_4, core_ref, q_ref, up_1_ref, up_2_ref, inner_ref, mine_ref, their_key_ref, their_value_ref, mean_ref, log_ref, *refs):
     new_mean_ref, new_log_ref, keys_ref, values_ref = refs
     keys_ref[...] = halve(inner_ref[0])
     values_ref[...] = halve(inner_ref[1])
-    by_core(core_ref, functools.partial(near_body, q_ref, inner_ref, mine_ref, theirs_ref, mean_ref, log_ref, new_mean_ref, new_log_ref, up_1_ref, up_2_ref, keys_ref, values_ref))
-
-
-def near_body(q_ref, inner_ref, mine_ref, theirs_ref, mean_ref, log_ref, new_mean_ref, new_log_ref, up_1_ref, up_2_ref, keys_ref, values_ref, edge, other):
+    by_core(core_ref, functools.partial(near_body, q_ref, inner_ref, mine_ref, their_key_ref, their_value_ref, mean_ref, log_ref, new_mean_ref, new_log_ref, up_1_ref, up_2_ref, keys_ref, values_ref))
+
+
+def near_body(q_ref, inner_ref, mine_ref, their_key_ref, their_value_ref, mean_ref, log_ref, new_mean_ref, new_log_ref, up_1_ref, up_2_ref, keys_ref, values_ref, edge, other):
     for head in range(HEADS):
         cols = slice(head * HEAD_DIM, (head + 1) * HEAD_DIM)
         mean, total, peak = attend(
@@ -157,13 +158,12 @@
             edge,
             cols,
             (q_ref, inner_ref[0, edge, cols], inner_ref[1, edge, cols]),
-            None,
             [
                 (up_1_ref, keys_ref[:, cols], values_ref[:, cols], 1.0),
                 (
                     up_2_ref,
-                    jnp.concatenate([mine_ref[0, :, cols], theirs_ref[0, :, cols]], 0),
-                    jnp.concatenate([mine_ref[1, :, cols], theirs_ref[1, :, cols]], 0),
+                    jnp.concatenate([mine_ref[0, :, cols], their_key_ref[0, :, cols]], 0),
+                    jnp.concatenate([mine_ref[1, :, cols], their_value_ref[0, :, cols]], 0),
                     2.0,
                 ),
             ],
@@ -177,44 +177,81 @@
         new_log_ref[edge, cols] = logs[BLOCK:]
 
 
-def far_kernel(core_ref, q_ref, edge_ref, mine_ref, theirs_ref, mean_ref, log_ref, *refs):
+def edge_kernel(after_ref, core_ref, q_ref, edge_ref, mean_ref, log_ref, new_mean_ref, new_log_ref):
+    bias = jnp.where(core_ref[1] == 1, 0.0, neg_large)
+
+    def body(edge, other):
+        spans = [slice(head * HEAD_DIM, (head + 1) * HEAD_DIM) for head in range(HEADS)]
+        scores = [dot_t(q_ref[edge, cols], edge_ref[0, :, cols]) + bias for cols in spans]
+        logs = [log_ref[edge, cols] for cols in spans]
+        peaks = [
+            jnp.maximum(row_max(score) * to_log2, log) for score, log in zip(scores, logs)
+        ]
+        weights = [
+            jnp.exp2(score * to_log2 - peak).astype(jnp.bfloat16)
+            for score, peak in zip(scores, peaks)
+        ]
+        boths = [
+            dot(weight, with_ones(edge_ref[1, :, cols])) for weight, cols in zip(weights, spans)
+        ]
+        means = []
+        for cols, log, peak, both in zip(spans, logs, peaks, boths):
+            factor = jnp.exp2(log - peak)
+            total = both[:, HEAD_DIM:] + factor
+            sums = both[:, :HEAD_DIM] + factor * mean_ref[edge, cols]
+            means.append((sums / total, jnp.log2(total) + peak))
+        for cols, (mean, log) in zip(spans, means):
+            new_mean_ref[edge, cols] = mean
+            new_log_ref[edge, cols] = log
+
+    by_core(core_ref, body)
+
+
+def far_kernel(mine_ref, theirs_ref, mean_ref, log_ref, *refs):
     out_ref = refs[-1]
     count = len(refs) // 2 + 1
     up_refs = refs[:count]
     more_refs = refs[count:-1]
-    by_core(core_ref, functools.partial(far_body, core_ref,q_ref, edge_ref, mine_ref, theirs_ref, mean_ref, log_ref, up_refs, more_refs, out_ref))
-
-
-def far_body(core_ref,q_ref, edge_ref, mine_ref, theirs_ref, mean_ref, log_ref, up_refs, more_refs, out_ref, edge, other):
-    bias = jnp.where(core_ref[1] == 1, 0.0, neg_large)
-    for head in range(HEADS):
-        cols = slice(head * HEAD_DIM, (head + 1) * HEAD_DIM)
-
-        def parts(which, level):
-            part = slice(64 * (level - 3), 64 * (level - 2))
-            return jnp.concatenate([mine_ref[which, part, cols], theirs_ref[which, part, cols]], 0)
-
-        coarse = [
-            (up_refs[level - 3], parts(0, level), parts(1, level), float(level))
-            for level in (3, 4)
-        ]
-        for level, more_ref in enumerate(more_refs, 5):
-            coarse.append(
-                (up_refs[level - 3], more_ref[0, :, cols], more_ref[1, :, cols], float(level))
+
+    def parts(which, level, cols):
+        if level > 4:
+            return more_refs[level - 5][which, :, cols]
+        part = slice(64 * (level - 3), 64 * (level - 2))
+        return jnp.concatenate([mine_ref[which, part, cols], theirs_ref[which, part, cols]], 0)
+
+    levels = range(3, 3 + count)
+    for start in range(0, HEADS, GROUP):
+        spans = [
+            slice(head * HEAD_DIM, (head + 1) * HEAD_DIM) for head in range(start, start + GROUP)
+        ]
+        scores = [
+            [dot_t(up_refs[level - 3][:, cols], parts(0, level, cols)) for level in levels]
+            for cols in spans
+        ]
+        logs = [log_ref[:, cols] for cols in spans]
+        peaks = [
+            jnp.maximum(row_max(functools.reduce(jnp.maximum, score)) * to_log2, log)
+            for score, log in zip(scores, logs)
+        ]
+        weights = [
+            [
+                jnp.exp2(part * to_log2 - (peak - float(level))).astype(jnp.bfloat16)
+                for level, part in zip(levels, score)
+            ]
+            for score, peak in zip(scores, peaks)
+        ]
+        boths = [
+            dot(
+                jnp.concatenate(weight, axis=1),
+                with_ones(jnp.concatenate([parts(1, level, cols) for level in levels], axis=0)),
             )
-        mean, _, _ = attend(
-            edge,
-            other,
-            cols,
-            (q_ref, edge_ref[0, :, cols], edge_ref[1, :, cols]),
-            bias,
-            coarse,
-            mean_ref,
-            log_ref,
-        )
-        mean = mean.astype(out_ref.dtype)
-        out_ref[edge, cols] = mean[:BLOCK]
-        out_ref[other, cols] = mean[BLOCK:]
+            for weight, cols in zip(weights, spans)
+        ]
+        for cols, log, peak, both in zip(spans, logs, peaks, boths):
+            factor = jnp.exp2(log - peak)
+            total = both[:, HEAD_DIM:] + factor
+            sums = both[:, :HEAD_DIM] + factor * mean_ref[:, cols]
+            out_ref[:, cols] = (sums / total).astype(out_ref.dtype)
 
 
 def call(kernel, in_specs, outputs, name, micros, *inputs, scratch=(), aliases=()):
@@ -284,14 +321,14 @@
     links = [(i, i + 1) for i in range(1, count - 1, 2)]
     edge = lax.ppermute(edge, "seq", links + [(j, i) for i, j in links])
     late = [sent(side_3, 4), sent(side_4, 8), sent(side_4, 12)]
-    other_2 = sent(side_2, 1)
+    other_2 = [sent(side_2[which : which + 1], 1) for which in range(2)]
     mean, log = call(
         own_kernel, [ANY] + [VMEM] * 2, [wide, wide], "own", 0, side_3, queries, keyval
     )
     up_1, up_2, *ups = call(ups_kernel, [ANY, VMEM], [up] * levels, "ups", 0, side_3, queries)
     mean, log = call(
         near_kernel,
-        [ANY] * 4 + [SMEM] + [VMEM] * 8,
+        [ANY] * 4 + [SMEM] + [VMEM] * 9,
         [wide, wide],
         "near",
         0,
@@ -303,7 +340,7 @@
         up_2,
         inner,
         side_2,
-        other_2,
+        *other_2,
         mean,
         log,
         scratch=[((BLOCK, features), narrow), ((BLOCK, features), narrow)],
@@ -314,15 +351,29 @@
     more = []
     if levels > 4:
         own = halve_rows(halve_rows(jnp.concatenate((keyval, inner), axis=1)))
-        own = halve_rows(jnp.concatenate((own, side_2, other_2), axis=1))
+        own = halve_rows(jnp.concatenate((own, side_2, jnp.concatenate(other_2)), axis=1))
         own = jnp.concatenate((own, late[:, :64], their_late[:, :64]), axis=1)
         own = jnp.concatenate((halve_rows(own), late[:, 64:], their_late[:, 64:]), axis=1)
         own = halve_rows(own)
         for level in range(5, levels + 1):
             more.append(sent(own, 1 << level - 1))
             own = halve_rows(jnp.concatenate((own, more[-1]), axis=1))
-    far = [position, queries, edge, late, their_late, mean, log] + ups + more
-    return call(far_kernel, [SMEM] + [VMEM] * (len(far) - 1), [up], "far", 0, *far)[0]
+    mean, log = call(
+        edge_kernel,
+        [ANY, SMEM] + [VMEM] * 4,
+        [wide, wide],
+        "edge",
+        0,
+        late,
+        position,
+        queries,
+        edge,
+        mean,
+        log,
+        aliases={4: 0, 5: 1},
+    )
+    far = [late, their_late, mean, log] + ups + more
+    return call(far_kernel, [VMEM] * len(far), [up], "far", 0, *far)[0]
 
 
 def solution(mesh):

time: 58.7 us -> 56.5 us (0.963)
  waiting for transfers between devices: 28.1 us -> 25.9 us
  starting transfers between devices: 14.5 us -> 13.5 us
  Pallas kernels: 14.3 us -> 15.2 us
    ppermute x10 -> x11, waiting for transfers between devices: 28.1 us -> 25.9 us  [sent(): return lax.ppermute(array, 'seq', [(i, i ^ stride) for i in range(count)])]
    ppermute x10 -> x11, starting transfers between devices: 13.7 us -> 12.6 us  [sent(): return lax.ppermute(array, 'seq', [(i, i ^ stride) for i in range(count)])]
    pallas_call x7 -> x8, Pallas kernels: 14.3 us -> 15.2 us  [call(): pl.pallas_call(kernel, in_specs=in_specs, out_specs=[VMEM] * len(outputs)...]
  transfers between devices with their start and end apart: 11 -> 12, of which waited for: 5 -> 6; matrix products, arithmetic and copies ran while one was open for 0% -> 0% of each run, Pallas kernels for 16% -> 21%
where the time goes in v4:
time: 56.5 us; the launch traced here: 56.4 us
  waiting for transfers between devices  25.9 us (46%)
  Pallas kernels  15.2 us (27%)
  starting transfers between devices  13.5 us (24%)
  local copies, waits for them, and re-layouts  1.64 us (3%)
    ppermute x11, waiting for transfers between devices, sent(): return lax.ppermute(array, 'seq', [(i, i ^ stride) for i in range(count)])  25.9 us
    pallas_call x8, Pallas kernels, call(): pl.pallas_call(kernel, in_specs=in_specs, out_specs=[VMEM] * len(outputs)...  15.2 us
    ppermute x11, starting transfers between devices, sent(): return lax.ppermute(array, 'seq', [(i, i ^ stride) for i in range(count)])  12.6 us
    unnamed x6, local copies, waits for them, and re-layouts  1.6 us
  transfers between devices with their start and end apart: 12, of which 6 were waited for; matrix products, arithmetic and copies ran while one was open for 0% of the time, Pallas kernels for 21%

profile of v4, /device:TPU:0, one launch (start us, length us, event | category | flops | bytes accessed | tf_op | source)
XLA Modules:
  0.0 56.4 jit_solution(16824670325549472347)
XLA Ops:
  0.0 0.5 collective-permute-start.5
  0.5 0.1 pad_add_fusion.core_ref
  0.5 0.0 copy-start.1
  0.5 1.6 %copy-done.1 = bf16[2,256,2048]{2,1,0:T(8,128)(2,1)S(1)} copy-done((bf16[2,256,2048]{2,1,0:T(8,128)(2,1)S(1)}, bf16[2,256,2048]{2,1,0:T(8,128)(2,1)}, u32[]{:S(2)}) %copy-start.1) | copy-done | bytes 2097176
  2.1 1.9 %pool.1 = (bf16[2,128,2048]{2,1,0:T(8,128)(2,1)S(1)}, bf16[2,64,2048]{2,1,0:T(8,128)(2,1)S(1)}, bf16[2,32,2048]{2,1,0:T(8,128)(2,1)S(1)}, bf16[2,16,2048]{2,1,0:T(8,128)(2,1)S(1)}) custom-call(s32[2]{0:T(128)S(1)} %pad_add_fusion.core_ref, bf16[2,256,2048]{2,1,0:T(8,128)(2,1)S(1)} %copy-done.1), custom_call_target="tpu_custom_call" | custom-call | tf_op jit(solution)/shard_map/pool/pallas_call | solution.py:258
  4.0 0.0 copy-start
  4.0 2.6 %collective-permute-start.3 = (bf16[2,64,2048]{2,1,0:T(8,128)(2,1)S(1)}, bf16[2,64,2048]{2,1,0:T(8,128)(2,1)S(1)}, u32[]{:S(2)}, u32[]{:S(2)}) collective-permute-start(bf16[2,64,2048]{2,1,0:T(8,128)(2,1)S(1)} %get-tuple-element.25), channel_id=1, source_target_pairs={{0,2},{1,3},{2,0},{3,1},{4,6},{5,7},{6,4},{7,5},{8,10},{9,11},{10,... | collective-permute-start | bytes 1572872 | tf_op jit(solution)/shard_map/ppermute | solution.py:275
  6.6 1.6 %collective-permute-start = (bf16[2,32,2048]{2,1,0:T(8,128)(2,1)S(1)}, bf16[2,32,2048]{2,1,0:T(8,128)(2,1)S(1)}, u32[]{:S(2)}, u32[]{:S(2)}) collective-permute-start(bf16[2,32,2048]{2,1,0:T(8,128)(2,1)S(1)} %get-tuple-element.22), channel_id=1, source_target_pairs={{0,4},{1,5},{2,6},{3,7},{4,0},{5,1},{6,2},{7,3},{8,12},{9,13},{10,... | collective-permute-start | bytes 786440 | tf_op jit(solution)/shard_map/ppermute | solution.py:275
  8.2 2.6 %collective-permute-start.1 = (bf16[2,16,2048]{2,1,0:T(8,128)(2,1)S(1)}, bf16[2,16,2048]{2,1,0:T(8,128)(2,1)S(1)}, u32[]{:S(2)}, u32[]{:S(2)}) collective-permute-start(bf16[2,16,2048]{2,1,0:T(8,128)(2,1)S(1)} %get-tuple-element.23), channel_id=1, source_target_pairs={{0,8},{1,9},{2,10},{3,11},{4,12},{5,13},{6,14},{7,15},{8,0},{9,1},... | collective-permute-start | bytes 393224 | tf_op jit(solution)/shard_map/ppermute | solution.py:275
  10.8 0.2 collective-permute-start.2
  11.0 6.7 %collective-permute-done.1.refs_1_.after_2.refs_2_ = bf16[2,16,2048]{2,1,0:T(8,128)(2,1)S(1)} collective-permute-done((bf16[2,16,2048]{2,1,0:T(8,128)(2,1)S(1)}, bf16[2,16,2048]{2,1,0:T(8,128)(2,1)S(1)}, u32[]{:S(2)}, u32[]{:S(2)}) %collective-permute-start.1) | collective-permute-done | bytes 131104 | tf_op jit(solution)/shard_map/ppermute | solution.py:275
  17.7 5.1 %collective-permute-done.2.refs_2_.after_3.refs_3_ = bf16[2,16,2048]{2,1,0:T(8,128)(2,1)S(1)} collective-permute-done((bf16[2,16,2048]{2,1,0:T(8,128)(2,1)S(1)}, bf16[2,16,2048]{2,1,0:T(8,128)(2,1)S(1)}, u32[]{:S(2)}, u32[]{:S(2)}) %collective-permute-start.2) | collective-permute-done | bytes 131104 | tf_op jit(solution)/shard_map/ppermute | solution.py:275
  22.8 0.0 collective-permute-done.refs_0_.after_1
  22.8 0.0 collective-permute-done.3.refs_4_.mine_ref
  22.8 0.0 copy-start.2
  22.8 0.4 side.1
  23.3 0.9 %collective-permute-start.4 = (bf16[2,128,2048]{2,1,0:T(8,128)(2,1)S(1)}, bf16[2,128,2048]{2,1,0:T(8,128)(2,1)S(1)}, u32[]{:S(2)}, u32[]{:S(2)}) collective-permute-start(bf16[2,128,2048]{2,1,0:T(8,128)(2,1)S(1)} %get-tuple-element.26), channel_id=1, source_target_pairs={{1,2},{3,4},{5,6},{7,8},{9,10},{11,12},{13,14},{2,1},{4,3},{6,5},{... | collective-permute-start | bytes 3145736 | tf_op jit(solution)/shard_map/ppermute | solution.py:322
  24.2 1.9 %collective-permute-start.6 = (bf16[1,64,2048]{2,1,0:T(8,128)(2,1)S(1)}, bf16[1,64,2048]{2,1,0:T(8,128)(2,1)S(1)}, u32[]{:S(2)}, u32[]{:S(2)}) collective-permute-start(bf16[1,64,2048]{2,1,0:T(8,128)(2,1)S(1)} %get-tuple-element.40), channel_id=1, source_target_pairs={{0,1},{1,0},{2,3},{3,2},{4,5},{5,4},{6,7},{7,6},{8,9},{9,8},{10,11... | collective-permute-start | bytes 786440 | tf_op jit(solution)/shard_map/ppermute | solution.py:275
  26.0 0.1 collective-permute-start.7
  26.1 0.8 %collective-permute-start.8 = (bf16[2,32,2048]{2,1,0:T(8,128)(2,1)S(1)}, bf16[2,32,2048]{2,1,0:T(8,128)(2,1)S(1)}, u32[]{:S(2)}, u32[]{:S(2)}) collective-permute-start(bf16[2,32,2048]{2,1,0:T(8,128)(2,1)S(1)} %get-tuple-element.27.after_ref.after_4), channel_id=1, source_target_pairs={{0,4},{1,5},{2,6},{3,7},{4,0},{5,1},{6,2},{7,3},{8,12},{9,13},{10,... | collective-permute-start | bytes 786440 | tf_op jit(solution)/shard_map/ppermute | solution.py:275
  26.9 0.3 collective-permute-done.6.their_key_ref
  27.2 2.1 %collective-permute-start.10 = (bf16[2,16,2048]{2,1,0:T(8,128)(2,1)S(1)}, bf16[2,16,2048]{2,1,0:T(8,128)(2,1)S(1)}, u32[]{:S(2)}, u32[]{:S(2)}) collective-permute-start(bf16[2,16,2048]{2,1,0:T(8,128)(2,1)S(1)} %get-tuple-element.33), channel_id=1, source_target_pairs={{0,12},{1,13},{2,14},{3,15},{4,8},{5,9},{6,10},{7,11},{8,4},{9,5},... | collective-permute-start | bytes 393224 | tf_op jit(solution)/shard_map/ppermute | solution.py:275
  29.3 0.0 collective-permute-done.7.their_value_ref
  29.3 0.3 collective-permute-start.9
  29.6 0.0 copy-done
  29.6 1.3 %ups.1 = (bf16[256,2048]{1,0:T(8,128)(2,1)S(1)}, bf16[256,2048]{1,0:T(8,128)(2,1)S(1)}, bf16[256,2048]{1,0:T(8,128)(2,1)S(1)}, bf16[256,2048]{1,0:T(8,128)(2,1)S(1)}) custom-call(bf16[2,32,2048]{2,1,0:T(8,128)(2,1)S(1)} %get-tuple-element.27.after_ref.after_4, bf16[256,2048]{1,0:T(8,128)(2,1)S(1)} %copy-done), custom_call_target="tpu_custom_call" | custom-call | tf_op jit(solution)/shard_map/ups/pallas_call | solution.py:258
  31.0 0.0 copy-done.2
  31.0 1.6 %own.1 = (f32[256,2048]{1,0:T(8,128)S(1)}, f32[256,2048]{1,0:T(8,128)S(1)}) custom-call(bf16[2,32,2048]{2,1,0:T(8,128)(2,1)S(1)} %get-tuple-element.27.after_ref.after_4, bf16[256,2048]{1,0:T(8,128)(2,1)S(1)} %copy-done, bf16[2,256,2048]{2,1,0:T(8,128)(2,1)S(1)} %copy-done.2), custom_call_target="tpu_custom_call" | custom-call | tf_op jit(solution)/shard_map/own/pallas_call | solution.py:258
  32.6 0.0 collective-permute-done.5.inner_ref
  32.6 4.3 %near.1 = (f32[256,2048]{1,0:T(8,128)S(1)}, f32[256,2048]{1,0:T(8,128)S(1)}) custom-call(bf16[2,32,2048]{2,1,0:T(8,128)(2,1)S(1)} %collective-permute-done.refs_0_.after_1, bf16[2,16,2048]{2,1,0:T(8,128)(2,1)S(1)} %collective-permute-done.1.refs_1_.after_2.refs_2_, bf16[2,16,2048]{2,1,0:T(8,128)(2,1)S(1)} %collective-permute-done.2.refs_2_.after_3.refs_3_, ...), custom_call_target="tpu_custom_call" | custom-call | tf_op jit(solution)/shard_map/near/pallas_call | solution.py:258
  36.9 12.9 %collective-permute-done.10.refs_5_ = bf16[2,16,2048]{2,1,0:T(8,128)(2,1)S(1)} collective-permute-done((bf16[2,16,2048]{2,1,0:T(8,128)(2,1)S(1)}, bf16[2,16,2048]{2,1,0:T(8,128)(2,1)S(1)}, u32[]{:S(2)}, u32[]{:S(2)}) %collective-permute-start.10) | collective-permute-done | bytes 131104 | tf_op jit(solution)/shard_map/ppermute | solution.py:275
  49.8 0.0 collective-permute-done.9.refs_4_
  49.8 0.4 collective-permute-done.8.refs_1_
  50.3 0.0 collective-permute-done.4.after_1.edge_ref
  50.3 0.1 join.1.after_ref.mine_ref
  50.3 0.1 collective-permute-start.11
  50.4 2.3 %edge.1 = (f32[256,2048]{1,0:T(8,128)S(1)}, f32[256,2048]{1,0:T(8,128)S(1)}) custom-call(bf16[2,128,2048]{2,1,0:T(8,128)(2,1)S(1)} %join.1.after_ref.mine_ref, s32[2]{0:T(128)S(1)} %pad_add_fusion.core_ref, bf16[256,2048]{1,0:T(8,128)(2,1)S(1)} %copy-done, ...), custom_call_target="tpu_custom_call", output_to_operand_aliasing={{0}: (4, {}), {1}: (5, {})} | custom-call | tf_op jit(solution)/shard_map/edge/pallas_call | solution.py:258
  52.7 0.3 collective-permute-done.11.theirs_ref
  53.1 3.3 %far.1 = bf16[256,2048]{1,0:T(8,128)(2,1)} custom-call(bf16[2,128,2048]{2,1,0:T(8,128)(2,1)S(1)} %join.1.after_ref.mine_ref, bf16[2,128,2048]{2,1,0:T(8,128)(2,1)S(1)} %collective-permute-done.11.theirs_ref, f32[256,2048]{1,0:T(8,128)S(1)} %get-tuple-element.35.mean_ref, f32[256,2048]{1,0:T(8,128)S(1)} %get-tuple-element.36.log_ref, ...), custom_call_target="tpu_custom_call" | custom-call | tf_op jit(solution)/shard_map/far/pallas_call | solution.py:258
  (1 shorter events, 0.0 us)
Async XLA Ops:
  0.0 32.6 %collective-permute-start.5 = (bf16[2,256,2048]{2,1,0:T(8,128)(2,1)}, bf16[2,256,2048]{2,1,0:T(8,128)(2,1)S(1)}, u32[]{:S(2)}, u32[]{:S(2)}) collective-permute-start(bf16[2,256,2048]{2,1,0:T(8,128)(2,1)} %kv_ref.3), channel_id=1, source_target_pairs={{0,1},{1,0},{2,3},{3,2},{4,5},{5,4},{6,7},{7,6},{8,9},{9,8},{10,11... | collective-permute-start | bytes 6291464 | tf_op jit(solution)/shard_map/ppermute | solution.py:275
  0.5 1.6 %copy-start.1 = (bf16[2,256,2048]{2,1,0:T(8,128)(2,1)S(1)}, bf16[2,256,2048]{2,1,0:T(8,128)(2,1)}, u32[]{:S(2)}) copy-start(bf16[2,256,2048]{2,1,0:T(8,128)(2,1)} %kv_ref.3) | copy-start | bytes 6291460
  4.0 25.6 %copy-start = (bf16[256,2048]{1,0:T(8,128)(2,1)S(1)}, bf16[256,2048]{1,0:T(8,128)(2,1)}, u32[]{:S(2)}) copy-start(bf16[256,2048]{1,0:T(8,128)(2,1)} %q_ref.7) | copy-start | bytes 3145732
  4.0 18.8 %collective-permute-start.3 = (bf16[2,64,2048]{2,1,0:T(8,128)(2,1)S(1)}, bf16[2,64,2048]{2,1,0:T(8,128)(2,1)S(1)}, u32[]{:S(2)}, u32[]{:S(2)}) collective-permute-start(bf16[2,64,2048]{2,1,0:T(8,128)(2,1)S(1)} %get-tuple-element.25), channel_id=1, source_target_pairs={{0,2},{1,3},{2,0},{3,1},{4,6},{5,7},{6,4},{7,5},{8,10},{9,11},{10,... | collective-permute-start | bytes 1572872 | tf_op jit(solution)/shard_map/ppermute | solution.py:275
  6.6 16.2 %collective-permute-start = (bf16[2,32,2048]{2,1,0:T(8,128)(2,1)S(1)}, bf16[2,32,2048]{2,1,0:T(8,128)(2,1)S(1)}, u32[]{:S(2)}, u32[]{:S(2)}) collective-permute-start(bf16[2,32,2048]{2,1,0:T(8,128)(2,1)S(1)} %get-tuple-element.22), channel_id=1, source_target_pairs={{0,4},{1,5},{2,6},{3,7},{4,0},{5,1},{6,2},{7,3},{8,12},{9,13},{10,... | collective-permute-start | bytes 786440 | tf_op jit(solution)/shard_map/ppermute | solution.py:275
  8.2 9.5 %collective-permute-start.1 = (bf16[2,16,2048]{2,1,0:T(8,128)(2,1)S(1)}, bf16[2,16,2048]{2,1,0:T(8,128)(2,1)S(1)}, u32[]{:S(2)}, u32[]{:S(2)}) collective-permute-start(bf16[2,16,2048]{2,1,0:T(8,128)(2,1)S(1)} %get-tuple-element.23), channel_id=1, source_target_pairs={{0,8},{1,9},{2,10},{3,11},{4,12},{5,13},{6,14},{7,15},{8,0},{9,1},... | collective-permute-start | bytes 393224 | tf_op jit(solution)/shard_map/ppermute | solution.py:275
  10.8 12.0 %collective-permute-start.2 = (bf16[2,16,2048]{2,1,0:T(8,128)(2,1)S(1)}, bf16[2,16,2048]{2,1,0:T(8,128)(2,1)S(1)}, u32[]{:S(2)}, u32[]{:S(2)}) collective-permute-start(bf16[2,16,2048]{2,1,0:T(8,128)(2,1)S(1)} %get-tuple-element.23), channel_id=1, source_target_pairs={{0,12},{1,13},{2,14},{3,15},{4,8},{5,9},{6,10},{7,11},{8,4},{9,5},... | collective-permute-start | bytes 393224 | tf_op jit(solution)/shard_map/ppermute | solution.py:275
  22.8 8.2 %copy-start.2 = (bf16[2,256,2048]{2,1,0:T(8,128)(2,1)S(1)}, bf16[2,256,2048]{2,1,0:T(8,128)(2,1)}, u32[]{:S(2)}) copy-start(bf16[2,256,2048]{2,1,0:T(8,128)(2,1)} %kv_ref.3) | copy-start | bytes 6291460
  23.3 27.0 %collective-permute-start.4 = (bf16[2,128,2048]{2,1,0:T(8,128)(2,1)S(1)}, bf16[2,128,2048]{2,1,0:T(8,128)(2,1)S(1)}, u32[]{:S(2)}, u32[]{:S(2)}) collective-permute-start(bf16[2,128,2048]{2,1,0:T(8,128)(2,1)S(1)} %get-tuple-element.26), channel_id=1, source_target_pairs={{1,2},{3,4},{5,6},{7,8},{9,10},{11,12},{13,14},{2,1},{4,3},{6,5},{... | collective-permute-start | bytes 3145736 | tf_op jit(solution)/shard_map/ppermute | solution.py:322
  24.2 3.0 %collective-permute-start.6 = (bf16[1,64,2048]{2,1,0:T(8,128)(2,1)S(1)}, bf16[1,64,2048]{2,1,0:T(8,128)(2,1)S(1)}, u32[]{:S(2)}, u32[]{:S(2)}) collective-permute-start(bf16[1,64,2048]{2,1,0:T(8,128)(2,1)S(1)} %get-tuple-element.40), channel_id=1, source_target_pairs={{0,1},{1,0},{2,3},{3,2},{4,5},{5,4},{6,7},{7,6},{8,9},{9,8},{10,11... | collective-permute-start | bytes 786440 | tf_op jit(solution)/shard_map/ppermute | solution.py:275
  26.0 3.2 %collective-permute-start.7 = (bf16[1,64,2048]{2,1,0:T(8,128)(2,1)S(1)}, bf16[1,64,2048]{2,1,0:T(8,128)(2,1)S(1)}, u32[]{:S(2)}, u32[]{:S(2)}) collective-permute-start(bf16[1,64,2048]{2,1,0:T(8,128)(2,1)S(1)} %get-tuple-element.39), channel_id=1, source_target_pairs={{0,1},{1,0},{2,3},{3,2},{4,5},{5,4},{6,7},{7,6},{8,9},{9,8},{10,11... | collective-permute-start | bytes 786440 | tf_op jit(solution)/shard_map/ppermute | solution.py:275
  26.1 24.1 %collective-permute-start.8 = (bf16[2,32,2048]{2,1,0:T(8,128)(2,1)S(1)}, bf16[2,32,2048]{2,1,0:T(8,128)(2,1)S(1)}, u32[]{:S(2)}, u32[]{:S(2)}) collective-permute-start(bf16[2,32,2048]{2,1,0:T(8,128)(2,1)S(1)} %get-tuple-element.27.after_ref.after_4), channel_id=1, source_target_pairs={{0,4},{1,5},{2,6},{3,7},{4,0},{5,1},{6,2},{7,3},{8,12},{9,13},{10,... | collective-permute-start | bytes 786440 | tf_op jit(solution)/shard_map/ppermute | solution.py:275
  27.2 22.6 %collective-permute-start.10 = (bf16[2,16,2048]{2,1,0:T(8,128)(2,1)S(1)}, bf16[2,16,2048]{2,1,0:T(8,128)(2,1)S(1)}, u32[]{:S(2)}, u32[]{:S(2)}) collective-permute-start(bf16[2,16,2048]{2,1,0:T(8,128)(2,1)S(1)} %get-tuple-element.33), channel_id=1, source_target_pairs={{0,12},{1,13},{2,14},{3,15},{4,8},{5,9},{6,10},{7,11},{8,4},{9,5},... | collective-permute-start | bytes 393224 | tf_op jit(solution)/shard_map/ppermute | solution.py:275
  29.3 20.6 %collective-permute-start.9 = (bf16[2,16,2048]{2,1,0:T(8,128)(2,1)S(1)}, bf16[2,16,2048]{2,1,0:T(8,128)(2,1)S(1)}, u32[]{:S(2)}, u32[]{:S(2)}) collective-permute-start(bf16[2,16,2048]{2,1,0:T(8,128)(2,1)S(1)} %get-tuple-element.33), channel_id=1, source_target_pairs={{0,8},{1,9},{2,10},{3,11},{4,12},{5,13},{6,14},{7,15},{8,0},{9,1},... | collective-permute-start | bytes 393224 | tf_op jit(solution)/shard_map/ppermute | solution.py:275
  50.3 2.7 %collective-permute-start.11 = (bf16[2,128,2048]{2,1,0:T(8,128)(2,1)S(1)}, bf16[2,128,2048]{2,1,0:T(8,128)(2,1)S(1)}, u32[]{:S(2)}, u32[]{:S(2)}) collective-permute-start(bf16[2,128,2048]{2,1,0:T(8,128)(2,1)S(1)} %join.1.after_ref.mine_ref), channel_id=1, source_target_pairs={{0,1},{1,0},{2,3},{3,2},{4,5},{5,4},{6,7},{7,6},{8,9},{9,8},{10,11... | collective-permute-start | bytes 3145736 | tf_op jit(solution)/shard_map/ppermute | solution.py:275

commit v5 on v4

--- a/solution.py
+++ b/solution.py
@@ -58,9 +58,12 @@
     return jnp.max(scores, axis=1, keepdims=True)
 
 
-def own_pool_kernel(core_ref, kv_ref, edge_ref, *out_refs):
+def rim_kernel(after_ref, core_ref, kv_ref, edge_ref):
     outer = pl.ds(pl.multiple_of(core_ref[0] * BLOCK, BLOCK), BLOCK)
     edge_ref[...] = kv_ref[:, outer, :]
+
+
+def own_pool_kernel(kv_ref, *out_refs):
     for which in range(2):
         rows = halve(kv_ref[which])
         for out_ref in out_refs:
@@ -201,17 +204,24 @@
             sums = both[:, :HEAD_DIM] + factor * mean_ref[edge, cols]
             means.append((sums / total, jnp.log2(total) + peak))
         for cols, (mean, log) in zip(spans, means):
-            new_mean_ref[edge, cols] = mean
-            new_log_ref[edge, cols] = log
+            new_mean_ref[:, cols] = mean
+            new_log_ref[:, cols] = log
 
     by_core(core_ref, body)
 
 
-def far_kernel(mine_ref, theirs_ref, mean_ref, log_ref, *refs):
-    out_ref = refs[-1]
-    count = len(refs) // 2 + 1
+def far_kernel(core_ref, *refs):
+    by_core(core_ref, functools.partial(far_body, *refs))
+
+
+def far_body(
+    mine_ref, theirs_ref, mean_ref, log_ref, edge_mean_ref, edge_log_ref, *refs
+):
+    *refs, hbm_ref, out_ref, sems, edge, other = refs
+    count = (len(refs) + 2) // 2
     up_refs = refs[:count]
-    more_refs = refs[count:-1]
+    more_refs = refs[count:]
+    copies = []
 
     def parts(which, level, cols):
         if level > 4:
@@ -219,6 +229,10 @@
         part = slice(64 * (level - 3), 64 * (level - 2))
         return jnp.concatenate([mine_ref[which, part, cols], theirs_ref[which, part, cols]], 0)
 
+    def state(ref, edge_ref, cols):
+        pair = [edge_ref[:, cols], ref[other, cols]]
+        return jnp.concatenate(pair if edge.start == 0 else pair[::-1], axis=0)
+
     levels = range(3, 3 + count)
     for start in range(0, HEADS, GROUP):
         spans = [
@@ -228,7 +242,7 @@
             [dot_t(up_refs[level - 3][:, cols], parts(0, level, cols)) for level in levels]
             for cols in spans
         ]
-        logs = [log_ref[:, cols] for cols in spans]
+        logs = [state(log_ref, edge_log_ref, cols) for cols in spans]
         peaks = [
             jnp.maximum(row_max(functools.reduce(jnp.maximum, score)) * to_log2, log)
             for score, log in zip(scores, logs)
@@ -250,17 +264,26 @@
         for cols, log, peak, both in zip(spans, logs, peaks, boths):
             factor = jnp.exp2(log - peak)
             total = both[:, HEAD_DIM:] + factor
-            sums = both[:, :HEAD_DIM] + factor * mean_ref[:, cols]
+            sums = both[:, :HEAD_DIM] + factor * state(mean_ref, edge_mean_ref, cols)
             out_ref[:, cols] = (sums / total).astype(out_ref.dtype)
-
-
-def call(kernel, in_specs, outputs, name, micros, *inputs, scratch=(), aliases=()):
+        done = slice(start * HEAD_DIM, (start + GROUP) * HEAD_DIM)
+        copies.append(
+            pltpu.make_async_copy(
+                out_ref.at[:, done], hbm_ref.at[:, done], sems.at[start // GROUP]
+            )
+        )
+        copies[-1].start()
+    for copy in copies:
+        copy.wait()
+
+
+def call(kernel, in_specs, outputs, name, micros, *inputs, scratch=(), aliases=(), out_specs=None):
     return pl.pallas_call(
         kernel,
         in_specs=in_specs,
-        out_specs=[VMEM] * len(outputs),
+        out_specs=out_specs or [VMEM] * len(outputs),
         out_shape=[jax.ShapeDtypeStruct(shape, dtype) for shape, dtype in outputs],
-        scratch_shapes=[pltpu.VMEM(shape, dtype) for shape, dtype in scratch],
+        scratch_shapes=list(scratch),
         cost_estimate=pl.CostEstimate(
             flops=micros * 1_000_000_000, bytes_accessed=0, transcendentals=0
         ),
@@ -295,21 +318,18 @@
     def some(count):
         return ((2, count, features), narrow)
 
-    edge, own_2, own_3, own_4 = call(
-        own_pool_kernel,
-        [SMEM, VMEM],
-        [some(BLOCK), some(64), some(32), some(16)],
-        "pool",
-        0,
-        position,
-        keyval,
+    own_2, own_3, own_4 = call(
+        own_pool_kernel, [VMEM], [some(64), some(32), some(16)], "pool", 0, keyval
     )
     side_2 = sent(own_2, 2)
     inner = sent(keyval, 1)
     early = [sent(own_3, 4), sent(own_4, 8), sent(own_4, 12)]
+    (edge,) = call(
+        rim_kernel, [ANY, SMEM, VMEM], [some(BLOCK)], "rim", 0, early[1], position, keyval
+    )
     edge, side_3, side_4 = call(
         side_pool_kernel,
-        [ANY] * 3 + [VMEM] * 2,
+        [ANY] * 4 + [VMEM],
         [some(BLOCK), some(32), some(16)],
         "side",
         0,
@@ -317,6 +337,7 @@
         edge,
         side_2,
         aliases={3: 0},
+        out_specs=[ANY, VMEM, VMEM],
     )
     links = [(i, i + 1) for i in range(1, count - 1, 2)]
     edge = lax.ppermute(edge, "seq", links + [(j, i) for i, j in links])
@@ -343,7 +364,7 @@
         *other_2,
         mean,
         log,
-        scratch=[((BLOCK, features), narrow), ((BLOCK, features), narrow)],
+        scratch=[pltpu.VMEM((BLOCK, features), narrow)] * 2,
     )
     pieces = (early[0], late[0], early[1], early[2], late[1], late[2])
     (late,) = call(join_kernel, [ANY] * 2 + [VMEM] * 6, [some(128)], "join", 0, edge, log, *pieces)
@@ -358,10 +379,10 @@
         for level in range(5, levels + 1):
             more.append(sent(own, 1 << level - 1))
             own = halve_rows(jnp.concatenate((own, more[-1]), axis=1))
-    mean, log = call(
+    edge_mean, edge_log = call(
         edge_kernel,
         [ANY, SMEM] + [VMEM] * 4,
-        [wide, wide],
+        [((BLOCK, features), jnp.float32)] * 2,
         "edge",
         0,
         late,
@@ -370,10 +391,18 @@
         edge,
         mean,
         log,
-        aliases={4: 0, 5: 1},
-    )
-    far = [late, their_late, mean, log] + ups + more
-    return call(far_kernel, [VMEM] * len(far), [up], "far", 0, *far)[0]
+    )
+    far = [position, late, their_late, mean, log, edge_mean, edge_log] + ups + more
+    return call(
+        far_kernel,
+        [SMEM] + [VMEM] * (len(far) - 1),
+        [up],
+        "far",
+        0,
+        *far,
+        scratch=[pltpu.VMEM(*up), pltpu.SemaphoreType.DMA((HEADS // GROUP,))],
+        out_specs=[ANY],
+    )[0]
 
 
 def solution(mesh):

time: 56.5 us -> 56.9 us (level)
  Pallas kernels: 15.2 us -> 17 us
  waiting for transfers between devices: 25.9 us -> 24.5 us
    pallas_call x8 -> x9, Pallas kernels: 15.2 us -> 17 us  [call(): pl.pallas_call(kernel, in_specs=in_specs, out_specs=out_specs or [VMEM] *...]
    ppermute x11, waiting for transfers between devices: 25.9 us -> 24.5 us  [sent(): return lax.ppermute(array, 'seq', [(i, i ^ stride) for i in range(count)])]
  transfers between devices with their start and end apart: 12 -> 12, of which waited for: 6 -> 6; matrix products, arithmetic and copies ran while one was open for 0% -> 0% of each run, Pallas kernels for 21% -> 23%
where the time goes in v5:
time: 56.9 us; the launch traced here: 56.7 us
  waiting for transfers between devices  24.5 us (43%)
  Pallas kernels  17 us (30%)
  starting transfers between devices  13.2 us (23%)
  local copies, waits for them, and re-layouts  1.64 us (3%)
    ppermute x11, waiting for transfers between devices, sent(): return lax.ppermute(array, 'seq', [(i, i ^ stride) for i in range(count)])  24.5 us
    pallas_call x9, Pallas kernels, call(): pl.pallas_call(kernel, in_specs=in_specs, out_specs=out_specs or [VMEM] *...  17 us
    ppermute x11, starting transfers between devices, sent(): return lax.ppermute(array, 'seq', [(i, i ^ stride) for i in range(count)])  12.5 us
    unnamed x6, local copies, waits for them, and re-layouts  1.6 us
  transfers between devices with their start and end apart: 12, of which 6 were waited for; matrix products, arithmetic and copies ran while one was open for 0% of the time, Pallas kernels for 23%

profile of v5, /device:TPU:0, one launch (start us, length us, event | category | flops | bytes accessed | tf_op | source)
XLA Modules:
  0.0 56.7 jit_solution(1365496579927895990)
XLA Ops:
  0.0 0.5 collective-permute-start.5
  0.5 0.0 copy-start
  0.5 1.6 %copy-done = bf16[2,256,2048]{2,1,0:T(8,128)(2,1)S(1)} copy-done((bf16[2,256,2048]{2,1,0:T(8,128)(2,1)S(1)}, bf16[2,256,2048]{2,1,0:T(8,128)(2,1)}, u32[]{:S(2)}) %copy-start) | copy-done | bytes 2097176
  2.0 0.0 copy-start.1
  2.0 1.9 %pool.1 = (bf16[2,64,2048]{2,1,0:T(8,128)(2,1)}, bf16[2,32,2048]{2,1,0:T(8,128)(2,1)S(1)}, bf16[2,16,2048]{2,1,0:T(8,128)(2,1)S(1)}) custom-call(bf16[2,256,2048]{2,1,0:T(8,128)(2,1)S(1)} %copy-done), custom_call_target="tpu_custom_call" | custom-call | tf_op jit(solution)/shard_map/pool/pallas_call | solution.py:281
  3.9 2.5 %collective-permute-start.3 = (bf16[2,64,2048]{2,1,0:T(8,128)(2,1)}, bf16[2,64,2048]{2,1,0:T(8,128)(2,1)S(1)}, u32[]{:S(2)}, u32[]{:S(2)}) collective-permute-start(bf16[2,64,2048]{2,1,0:T(8,128)(2,1)} %get-tuple-element.23), channel_id=1, source_target_pairs={{0,2},{1,3},{2,0},{3,1},{4,6},{5,7},{6,4},{7,5},{8,10},{9,11},{10,... | collective-permute-start | bytes 1572872 | tf_op jit(solution)/shard_map/ppermute | solution.py:298
  6.5 1.6 %collective-permute-start = (bf16[2,32,2048]{2,1,0:T(8,128)(2,1)S(1)}, bf16[2,32,2048]{2,1,0:T(8,128)(2,1)S(1)}, u32[]{:S(2)}, u32[]{:S(2)}) collective-permute-start(bf16[2,32,2048]{2,1,0:T(8,128)(2,1)S(1)} %get-tuple-element.21), channel_id=1, source_target_pairs={{0,4},{1,5},{2,6},{3,7},{4,0},{5,1},{6,2},{7,3},{8,12},{9,13},{10,... | collective-permute-start | bytes 786440 | tf_op jit(solution)/shard_map/ppermute | solution.py:298
  8.0 2.6 %collective-permute-start.1 = (bf16[2,16,2048]{2,1,0:T(8,128)(2,1)S(1)}, bf16[2,16,2048]{2,1,0:T(8,128)(2,1)S(1)}, u32[]{:S(2)}, u32[]{:S(2)}) collective-permute-start(bf16[2,16,2048]{2,1,0:T(8,128)(2,1)S(1)} %get-tuple-element.22), channel_id=1, source_target_pairs={{0,8},{1,9},{2,10},{3,11},{4,12},{5,13},{6,14},{7,15},{8,0},{9,1},... | collective-permute-start | bytes 393224 | tf_op jit(solution)/shard_map/ppermute | solution.py:298
  10.6 0.2 collective-permute-start.2
  10.8 0.1 pad_add_fusion.core_ref
  10.9 6.6 %collective-permute-done.1.after_ref.refs_1_.after_2.refs_2_ = bf16[2,16,2048]{2,1,0:T(8,128)(2,1)S(1)} collective-permute-done((bf16[2,16,2048]{2,1,0:T(8,128)(2,1)S(1)}, bf16[2,16,2048]{2,1,0:T(8,128)(2,1)S(1)}, u32[]{:S(2)}, u32[]{:S(2)}) %collective-permute-start.1) | collective-permute-done | bytes 131104 | tf_op jit(solution)/shard_map/ppermute | solution.py:298
  17.6 0.0 copy-done.1
  17.6 0.6 %rim.1.refs_3_ = bf16[2,128,2048]{2,1,0:T(8,128)(2,1)S(1)} custom-call(bf16[2,16,2048]{2,1,0:T(8,128)(2,1)S(1)} %collective-permute-done.1.after_ref.refs_1_.after_2.refs_2_, s32[2]{0:T(128)S(1)} %pad_add_fusion.core_ref, bf16[2,256,2048]{2,1,0:T(8,128)(2,1)S(1)} %copy-done.1), custom_call_target="tpu_custom_call" | custom-call | tf_op jit(solution)/shard_map/rim/pallas_call | solution.py:281
  18.2 0.0 copy-start.2
  18.2 4.5 %collective-permute-done.2.refs_2_.after_3.refs_3_ = bf16[2,16,2048]{2,1,0:T(8,128)(2,1)S(1)} collective-permute-done((bf16[2,16,2048]{2,1,0:T(8,128)(2,1)S(1)}, bf16[2,16,2048]{2,1,0:T(8,128)(2,1)S(1)}, u32[]{:S(2)}, u32[]{:S(2)}) %collective-permute-start.2) | collective-permute-done | bytes 131104 | tf_op jit(solution)/shard_map/ppermute | solution.py:298
  22.7 0.0 collective-permute-done.refs_0_.after_1
  22.7 0.0 collective-permute-done.3.refs_4_.mine_ref
  22.7 0.4 side.1
  23.1 0.7 %collective-permute-start.4 = (bf16[2,128,2048]{2,1,0:T(8,128)(2,1)S(1)}, bf16[2,128,2048]{2,1,0:T(8,128)(2,1)S(1)}, u32[]{:S(2)}, u32[]{:S(2)}) collective-permute-start(bf16[2,128,2048]{2,1,0:T(8,128)(2,1)S(1)} %get-tuple-element.24), channel_id=1, source_target_pairs={{1,2},{3,4},{5,6},{7,8},{9,10},{11,12},{13,14},{2,1},{4,3},{6,5},{... | collective-permute-start | bytes 3145736 | tf_op jit(solution)/shard_map/ppermute | solution.py:343
  23.9 1.9 %collective-permute-start.6 = (bf16[1,64,2048]{2,1,0:T(8,128)(2,1)S(1)}, bf16[1,64,2048]{2,1,0:T(8,128)(2,1)S(1)}, u32[]{:S(2)}, u32[]{:S(2)}) collective-permute-start(bf16[1,64,2048]{2,1,0:T(8,128)(2,1)S(1)} %get-tuple-element.38), channel_id=1, source_target_pairs={{0,1},{1,0},{2,3},{3,2},{4,5},{5,4},{6,7},{7,6},{8,9},{9,8},{10,11... | collective-permute-start | bytes 786440 | tf_op jit(solution)/shard_map/ppermute | solution.py:298
  25.8 0.1 collective-permute-start.7
  25.8 0.7 %collective-permute-start.8 = (bf16[2,32,2048]{2,1,0:T(8,128)(2,1)S(1)}, bf16[2,32,2048]{2,1,0:T(8,128)(2,1)S(1)}, u32[]{:S(2)}, u32[]{:S(2)}) collective-permute-start(bf16[2,32,2048]{2,1,0:T(8,128)(2,1)S(1)} %get-tuple-element.25.after_ref.after_4), channel_id=1, source_target_pairs={{0,4},{1,5},{2,6},{3,7},{4,0},{5,1},{6,2},{7,3},{8,12},{9,13},{10,... | collective-permute-start | bytes 786440 | tf_op jit(solution)/shard_map/ppermute | solution.py:298
  26.6 0.3 collective-permute-done.6.their_key_ref
  26.9 2.1 %collective-permute-start.10 = (bf16[2,16,2048]{2,1,0:T(8,128)(2,1)S(1)}, bf16[2,16,2048]{2,1,0:T(8,128)(2,1)S(1)}, u32[]{:S(2)}, u32[]{:S(2)}) collective-permute-start(bf16[2,16,2048]{2,1,0:T(8,128)(2,1)S(1)} %get-tuple-element.31), channel_id=1, source_target_pairs={{0,12},{1,13},{2,14},{3,15},{4,8},{5,9},{6,10},{7,11},{8,4},{9,5},... | collective-permute-start | bytes 393224 | tf_op jit(solution)/shard_map/ppermute | solution.py:298
  29.0 0.0 collective-permute-done.7.their_value_ref
  29.0 0.3 collective-permute-start.9
  29.3 0.0 copy-done.2
  29.3 1.3 %ups.1 = (bf16[256,2048]{1,0:T(8,128)(2,1)S(1)}, bf16[256,2048]{1,0:T(8,128)(2,1)S(1)}, bf16[256,2048]{1,0:T(8,128)(2,1)S(1)}, bf16[256,2048]{1,0:T(8,128)(2,1)S(1)}) custom-call(bf16[2,32,2048]{2,1,0:T(8,128)(2,1)S(1)} %get-tuple-element.25.after_ref.after_4, bf16[256,2048]{1,0:T(8,128)(2,1)S(1)} %copy-done.2), custom_call_target="tpu_custom_call" | custom-call | tf_op jit(solution)/shard_map/ups/pallas_call | solution.py:281
  30.7 1.6 %own.1 = (f32[256,2048]{1,0:T(8,128)S(1)}, f32[256,2048]{1,0:T(8,128)S(1)}) custom-call(bf16[2,32,2048]{2,1,0:T(8,128)(2,1)S(1)} %get-tuple-element.25.after_ref.after_4, bf16[256,2048]{1,0:T(8,128)(2,1)S(1)} %copy-done.2, bf16[2,256,2048]{2,1,0:T(8,128)(2,1)S(1)} %copy-done.1), custom_call_target="tpu_custom_call" | custom-call | tf_op jit(solution)/shard_map/own/pallas_call | solution.py:281
  32.3 0.0 collective-permute-done.5.inner_ref
  32.3 5.3 %near.1 = (f32[256,2048]{1,0:T(8,128)S(1)}, f32[256,2048]{1,0:T(8,128)S(1)}) custom-call(bf16[2,32,2048]{2,1,0:T(8,128)(2,1)S(1)} %collective-permute-done.refs_0_.after_1, bf16[2,16,2048]{2,1,0:T(8,128)(2,1)S(1)} %collective-permute-done.1.after_ref.refs_1_.after_2.refs_2_, bf16[2,16,2048]{2,1,0:T(8,128)(2,1)S(1)} %collective-permute-done.2.refs_2_.after_3.refs_3_, ...), custom_call_target="tpu_custom_call" | custom-call | tf_op jit(solution)/shard_map/near/pallas_call | solution.py:281
  37.6 11.9 %collective-permute-done.10.refs_5_ = bf16[2,16,2048]{2,1,0:T(8,128)(2,1)S(1)} collective-permute-done((bf16[2,16,2048]{2,1,0:T(8,128)(2,1)S(1)}, bf16[2,16,2048]{2,1,0:T(8,128)(2,1)S(1)}, u32[]{:S(2)}, u32[]{:S(2)}) %collective-permute-start.10) | collective-permute-done | bytes 131104 | tf_op jit(solution)/shard_map/ppermute | solution.py:298
  49.5 0.0 collective-permute-done.9.refs_4_
  49.5 0.4 collective-permute-done.8.refs_1_
  50.0 0.0 collective-permute-done.4.after_1.edge_ref
  50.0 0.1 join.1.after_ref.refs_0_
  50.0 0.1 collective-permute-start.11
  50.1 1.9 %edge.1 = (f32[128,2048]{1,0:T(8,128)S(1)}, f32[128,2048]{1,0:T(8,128)S(1)}) custom-call(bf16[2,128,2048]{2,1,0:T(8,128)(2,1)S(1)} %join.1.after_ref.refs_0_, s32[2]{0:T(128)S(1)} %pad_add_fusion.core_ref, bf16[256,2048]{1,0:T(8,128)(2,1)S(1)} %copy-done.2, bf16[2,128,2048]{2,1,0:T(8,128)(2,1)S(1)} %collective-permute-done.4.after_1.edge_ref, ...), custom_call_target="tpu_custom_call" | custom-call | tf_op jit(solution)/shard_map/edge/pallas_call | solution.py:281
  52.0 0.8 %collective-permute-done.11.refs_1_ = bf16[2,128,2048]{2,1,0:T(8,128)(2,1)S(1)} collective-permute-done((bf16[2,128,2048]{2,1,0:T(8,128)(2,1)S(1)}, bf16[2,128,2048]{2,1,0:T(8,128)(2,1)S(1)}, u32[]{:S(2)}, u32[]{:S(2)}) %collective-permute-start.11) | collective-permute-done | bytes 1048608 | tf_op jit(solution)/shard_map/ppermute | solution.py:298
  52.8 3.8 %far.1 = bf16[256,2048]{1,0:T(8,128)(2,1)} custom-call(s32[2]{0:T(128)S(1)} %pad_add_fusion.core_ref, bf16[2,128,2048]{2,1,0:T(8,128)(2,1)S(1)} %join.1.after_ref.refs_0_, bf16[2,128,2048]{2,1,0:T(8,128)(2,1)S(1)} %collective-permute-done.11.refs_1_, f32[256,2048]{1,0:T(8,128)S(1)} %get-tuple-element.32.mean_ref.refs_2_, ...), custom_call_target="tpu_custom_call" | custom-call | tf_op jit(solution)/shard_map/far/pallas_call | solution.py:281
  (1 shorter events, 0.0 us)
Async XLA Ops:
  0.0 32.3 %collective-permute-start.5 = (bf16[2,256,2048]{2,1,0:T(8,128)(2,1)}, bf16[2,256,2048]{2,1,0:T(8,128)(2,1)}, u32[]{:S(2)}, u32[]{:S(2)}) collective-permute-start(bf16[2,256,2048]{2,1,0:T(8,128)(2,1)} %kv_ref.5), channel_id=1, source_target_pairs={{0,1},{1,0},{2,3},{3,2},{4,5},{5,4},{6,7},{7,6},{8,9},{9,8},{10,11... | collective-permute-start | bytes 6291464 | tf_op jit(solution)/shard_map/ppermute | solution.py:298
  0.5 1.6 %copy-start = (bf16[2,256,2048]{2,1,0:T(8,128)(2,1)S(1)}, bf16[2,256,2048]{2,1,0:T(8,128)(2,1)}, u32[]{:S(2)}) copy-start(bf16[2,256,2048]{2,1,0:T(8,128)(2,1)} %kv_ref.5) | copy-start | bytes 6291460
  2.0 15.5 %copy-start.1 = (bf16[2,256,2048]{2,1,0:T(8,128)(2,1)S(1)}, bf16[2,256,2048]{2,1,0:T(8,128)(2,1)}, u32[]{:S(2)}) copy-start(bf16[2,256,2048]{2,1,0:T(8,128)(2,1)} %kv_ref.5) | copy-start | bytes 6291460
  3.9 18.7 %collective-permute-start.3 = (bf16[2,64,2048]{2,1,0:T(8,128)(2,1)}, bf16[2,64,2048]{2,1,0:T(8,128)(2,1)S(1)}, u32[]{:S(2)}, u32[]{:S(2)}) collective-permute-start(bf16[2,64,2048]{2,1,0:T(8,128)(2,1)} %get-tuple-element.23), channel_id=1, source_target_pairs={{0,2},{1,3},{2,0},{3,1},{4,6},{5,7},{6,4},{7,5},{8,10},{9,11},{10,... | collective-permute-start | bytes 1572872 | tf_op jit(solution)/shard_map/ppermute | solution.py:298
  6.5 16.2 %collective-permute-start = (bf16[2,32,2048]{2,1,0:T(8,128)(2,1)S(1)}, bf16[2,32,2048]{2,1,0:T(8,128)(2,1)S(1)}, u32[]{:S(2)}, u32[]{:S(2)}) collective-permute-start(bf16[2,32,2048]{2,1,0:T(8,128)(2,1)S(1)} %get-tuple-element.21), channel_id=1, source_target_pairs={{0,4},{1,5},{2,6},{3,7},{4,0},{5,1},{6,2},{7,3},{8,12},{9,13},{10,... | collective-permute-start | bytes 786440 | tf_op jit(solution)/shard_map/ppermute | solution.py:298
  8.0 9.5 %collective-permute-start.1 = (bf16[2,16,2048]{2,1,0:T(8,128)(2,1)S(1)}, bf16[2,16,2048]{2,1,0:T(8,128)(2,1)S(1)}, u32[]{:S(2)}, u32[]{:S(2)}) collective-permute-start(bf16[2,16,2048]{2,1,0:T(8,128)(2,1)S(1)} %get-tuple-element.22), channel_id=1, source_target_pairs={{0,8},{1,9},{2,10},{3,11},{4,12},{5,13},{6,14},{7,15},{8,0},{9,1},... | collective-permute-start | bytes 393224 | tf_op jit(solution)/shard_map/ppermute | solution.py:298
  10.6 12.0 %collective-permute-start.2 = (bf16[2,16,2048]{2,1,0:T(8,128)(2,1)S(1)}, bf16[2,16,2048]{2,1,0:T(8,128)(2,1)S(1)}, u32[]{:S(2)}, u32[]{:S(2)}) collective-permute-start(bf16[2,16,2048]{2,1,0:T(8,128)(2,1)S(1)} %get-tuple-element.22), channel_id=1, source_target_pairs={{0,12},{1,13},{2,14},{3,15},{4,8},{5,9},{6,10},{7,11},{8,4},{9,5},... | collective-permute-start | bytes 393224 | tf_op jit(solution)/shard_map/ppermute | solution.py:298
  18.2 11.2 %copy-start.2 = (bf16[256,2048]{1,0:T(8,128)(2,1)S(1)}, bf16[256,2048]{1,0:T(8,128)(2,1)}, u32[]{:S(2)}) copy-start(bf16[256,2048]{1,0:T(8,128)(2,1)} %q_ref.7) | copy-start | bytes 3145732
  23.1 26.9 %collective-permute-start.4 = (bf16[2,128,2048]{2,1,0:T(8,128)(2,1)S(1)}, bf16[2,128,2048]{2,1,0:T(8,128)(2,1)S(1)}, u32[]{:S(2)}, u32[]{:S(2)}) collective-permute-start(bf16[2,128,2048]{2,1,0:T(8,128)(2,1)S(1)} %get-tuple-element.24), channel_id=1, source_target_pairs={{1,2},{3,4},{5,6},{7,8},{9,10},{11,12},{13,14},{2,1},{4,3},{6,5},{... | collective-permute-start | bytes 3145736 | tf_op jit(solution)/shard_map/ppermute | solution.py:343
  23.9 3.0 %collective-permute-start.6 = (bf16[1,64,2048]{2,1,0:T(8,128)(2,1)S(1)}, bf16[1,64,2048]{2,1,0:T(8,128)(2,1)S(1)}, u32[]{:S(2)}, u32[]{:S(2)}) collective-permute-start(bf16[1,64,2048]{2,1,0:T(8,128)(2,1)S(1)} %get-tuple-element.38), channel_id=1, source_target_pairs={{0,1},{1,0},{2,3},{3,2},{4,5},{5,4},{6,7},{7,6},{8,9},{9,8},{10,11... | collective-permute-start | bytes 786440 | tf_op jit(solution)/shard_map/ppermute | solution.py:298
  25.8 3.2 %collective-permute-start.7 = (bf16[1,64,2048]{2,1,0:T(8,128)(2,1)S(1)}, bf16[1,64,2048]{2,1,0:T(8,128)(2,1)S(1)}, u32[]{:S(2)}, u32[]{:S(2)}) collective-permute-start(bf16[1,64,2048]{2,1,0:T(8,128)(2,1)S(1)} %get-tuple-element.37), channel_id=1, source_target_pairs={{0,1},{1,0},{2,3},{3,2},{4,5},{5,4},{6,7},{7,6},{8,9},{9,8},{10,11... | collective-permute-start | bytes 786440 | tf_op jit(solution)/shard_map/ppermute | solution.py:298
  25.8 24.1 %collective-permute-start.8 = (bf16[2,32,2048]{2,1,0:T(8,128)(2,1)S(1)}, bf16[2,32,2048]{2,1,0:T(8,128)(2,1)S(1)}, u32[]{:S(2)}, u32[]{:S(2)}) collective-permute-start(bf16[2,32,2048]{2,1,0:T(8,128)(2,1)S(1)} %get-tuple-element.25.after_ref.after_4), channel_id=1, source_target_pairs={{0,4},{1,5},{2,6},{3,7},{4,0},{5,1},{6,2},{7,3},{8,12},{9,13},{10,... | collective-permute-start | bytes 786440 | tf_op jit(solution)/shard_map/ppermute | solution.py:298
  26.9 22.6 %collective-permute-start.10 = (bf16[2,16,2048]{2,1,0:T(8,128)(2,1)S(1)}, bf16[2,16,2048]{2,1,0:T(8,128)(2,1)S(1)}, u32[]{:S(2)}, u32[]{:S(2)}) collective-permute-start(bf16[2,16,2048]{2,1,0:T(8,128)(2,1)S(1)} %get-tuple-element.31), channel_id=1, source_target_pairs={{0,12},{1,13},{2,14},{3,15},{4,8},{5,9},{6,10},{7,11},{8,4},{9,5},... | collective-permute-start | bytes 393224 | tf_op jit(solution)/shard_map/ppermute | solution.py:298
  29.0 20.6 %collective-permute-start.9 = (bf16[2,16,2048]{2,1,0:T(8,128)(2,1)S(1)}, bf16[2,16,2048]{2,1,0:T(8,128)(2,1)S(1)}, u32[]{:S(2)}, u32[]{:S(2)}) collective-permute-start(bf16[2,16,2048]{2,1,0:T(8,128)(2,1)S(1)} %get-tuple-element.31), channel_id=1, source_target_pairs={{0,8},{1,9},{2,10},{3,11},{4,12},{5,13},{6,14},{7,15},{8,0},{9,1},... | collective-permute-start | bytes 393224 | tf_op jit(solution)/shard_map/ppermute | solution.py:298
  50.0 2.7 %collective-permute-start.11 = (bf16[2,128,2048]{2,1,0:T(8,128)(2,1)S(1)}, bf16[2,128,2048]{2,1,0:T(8,128)(2,1)S(1)}, u32[]{:S(2)}, u32[]{:S(2)}) collective-permute-start(bf16[2,128,2048]{2,1,0:T(8,128)(2,1)S(1)} %join.1.after_ref.refs_0_), channel_id=1, source_target_pairs={{0,1},{1,0},{2,3},{3,2},{4,5},{5,4},{6,7},{7,6},{8,9},{9,8},{10,11... | collective-permute-start | bytes 3145736 | tf_op jit(solution)/shard_map/ppermute | solution.py:298

commit v6 on v5

--- a/solution.py
+++ b/solution.py
@@ -204,20 +204,16 @@
             sums = both[:, :HEAD_DIM] + factor * mean_ref[edge, cols]
             means.append((sums / total, jnp.log2(total) + peak))
         for cols, (mean, log) in zip(spans, means):
-            new_mean_ref[:, cols] = mean
-            new_log_ref[:, cols] = log
+            new_mean_ref[edge, cols] = mean
+            new_log_ref[edge, cols] = log
+        new_mean_ref[other, :] = mean_ref[other, :]
+        new_log_ref[other, :] = log_ref[other, :]
 
     by_core(core_ref, body)
 
 
-def far_kernel(core_ref, *refs):
-    by_core(core_ref, functools.partial(far_body, *refs))
-
-
-def far_body(
-    mine_ref, theirs_ref, mean_ref, log_ref, edge_mean_ref, edge_log_ref, *refs
-):
-    *refs, hbm_ref, out_ref, sems, edge, other = refs
+def far_kernel(mine_ref, theirs_ref, mean_ref, log_ref, *refs):
+    *refs, hbm_ref, out_ref, sems = refs
     count = (len(refs) + 2) // 2
     up_refs = refs[:count]
     more_refs = refs[count:]
@@ -229,10 +225,6 @@
         part = slice(64 * (level - 3), 64 * (level - 2))
         return jnp.concatenate([mine_ref[which, part, cols], theirs_ref[which, part, cols]], 0)
 
-    def state(ref, edge_ref, cols):
-        pair = [edge_ref[:, cols], ref[other, cols]]
-        return jnp.concatenate(pair if edge.start == 0 else pair[::-1], axis=0)
-
     levels = range(3, 3 + count)
     for start in range(0, HEADS, GROUP):
         spans = [
@@ -242,7 +234,7 @@
             [dot_t(up_refs[level - 3][:, cols], parts(0, level, cols)) for level in levels]
             for cols in spans
         ]
-        logs = [state(log_ref, edge_log_ref, cols) for cols in spans]
+        logs = [log_ref[:, cols] for cols in spans]
         peaks = [
             jnp.maximum(row_max(functools.reduce(jnp.maximum, score)) * to_log2, log)
             for score, log in zip(scores, logs)
@@ -264,7 +256,7 @@
         for cols, log, peak, both in zip(spans, logs, peaks, boths):
             factor = jnp.exp2(log - peak)
             total = both[:, HEAD_DIM:] + factor
-            sums = both[:, :HEAD_DIM] + factor * state(mean_ref, edge_mean_ref, cols)
+            sums = both[:, :HEAD_DIM] + factor * mean_ref[:, cols]
             out_ref[:, cols] = (sums / total).astype(out_ref.dtype)
         done = slice(start * HEAD_DIM, (start + GROUP) * HEAD_DIM)
         copies.append(
@@ -379,10 +371,10 @@
         for level in range(5, levels + 1):
             more.append(sent(own, 1 << level - 1))
             own = halve_rows(jnp.concatenate((own, more[-1]), axis=1))
-    edge_mean, edge_log = call(
+    mean, log = call(
         edge_kernel,
         [ANY, SMEM] + [VMEM] * 4,
-        [((BLOCK, features), jnp.float32)] * 2,
+        [wide, wide],
         "edge",
         0,
         late,
@@ -392,10 +384,10 @@
         mean,
         log,
     )
-    far = [position, late, their_late, mean, log, edge_mean, edge_log] + ups + more
+    far = [late, their_late, mean, log] + ups + more
     return call(
         far_kernel,
-        [SMEM] + [VMEM] * (len(far) - 1),
+        [VMEM] * len(far),
         [up],
         "far",
         0,

time: 56.9 us -> 56.2 us (0.988)
  Pallas kernels: 17 us -> 16.4 us
  transfers between devices with their start and end apart: 12 -> 12, of which waited for: 6 -> 6; matrix products, arithmetic and copies ran while one was open for 0% -> 0% of each run, Pallas kernels for 23% -> 24%
where the time goes in v6:
time: 56.2 us; the launch traced here: 56 us
  waiting for transfers between devices  24.4 us (43%)
  Pallas kernels  16.4 us (29%)
  starting transfers between devices  13.2 us (23%)
  local copies, waits for them, and re-layouts  1.64 us (3%)
    ppermute x11, waiting for transfers between devices, sent(): return lax.ppermute(array, 'seq', [(i, i ^ stride) for i in range(count)])  24.4 us
    pallas_call x9, Pallas kernels, call(): pl.pallas_call(kernel, in_specs=in_specs, out_specs=out_specs or [VMEM] *...  16.4 us
    ppermute x11, starting transfers between devices, sent(): return lax.ppermute(array, 'seq', [(i, i ^ stride) for i in range(count)])  12.5 us
    unnamed x6, local copies, waits for them, and re-layouts  1.6 us
  transfers between devices with their start and end apart: 12, of which 6 were waited for; matrix products, arithmetic and copies ran while one was open for 0% of the time, Pallas kernels for 24%

profile of v6, /device:TPU:0, one launch (start us, length us, event | category | flops | bytes accessed | tf_op | source)
XLA Modules:
  0.0 56.0 jit_solution(7937208109398369921)
XLA Ops:
  0.0 0.5 collective-permute-start.5
  0.5 0.0 copy-start
  0.5 1.6 %copy-done = bf16[2,256,2048]{2,1,0:T(8,128)(2,1)S(1)} copy-done((bf16[2,256,2048]{2,1,0:T(8,128)(2,1)S(1)}, bf16[2,256,2048]{2,1,0:T(8,128)(2,1)}, u32[]{:S(2)}) %copy-start) | copy-done | bytes 2097176
  2.0 0.0 copy-start.1
  2.0 1.9 %pool.1 = (bf16[2,64,2048]{2,1,0:T(8,128)(2,1)}, bf16[2,32,2048]{2,1,0:T(8,128)(2,1)S(1)}, bf16[2,16,2048]{2,1,0:T(8,128)(2,1)S(1)}) custom-call(bf16[2,256,2048]{2,1,0:T(8,128)(2,1)S(1)} %copy-done), custom_call_target="tpu_custom_call" | custom-call | tf_op jit(solution)/shard_map/pool/pallas_call | solution.py:273
  3.9 2.5 %collective-permute-start.3 = (bf16[2,64,2048]{2,1,0:T(8,128)(2,1)}, bf16[2,64,2048]{2,1,0:T(8,128)(2,1)S(1)}, u32[]{:S(2)}, u32[]{:S(2)}) collective-permute-start(bf16[2,64,2048]{2,1,0:T(8,128)(2,1)} %get-tuple-element.23), channel_id=1, source_target_pairs={{0,2},{1,3},{2,0},{3,1},{4,6},{5,7},{6,4},{7,5},{8,10},{9,11},{10,... | collective-permute-start | bytes 1572872 | tf_op jit(solution)/shard_map/ppermute | solution.py:290
  6.5 1.6 %collective-permute-start = (bf16[2,32,2048]{2,1,0:T(8,128)(2,1)S(1)}, bf16[2,32,2048]{2,1,0:T(8,128)(2,1)S(1)}, u32[]{:S(2)}, u32[]{:S(2)}) collective-permute-start(bf16[2,32,2048]{2,1,0:T(8,128)(2,1)S(1)} %get-tuple-element.21), channel_id=1, source_target_pairs={{0,4},{1,5},{2,6},{3,7},{4,0},{5,1},{6,2},{7,3},{8,12},{9,13},{10,... | collective-permute-start | bytes 786440 | tf_op jit(solution)/shard_map/ppermute | solution.py:290
  8.0 2.6 %collective-permute-start.1 = (bf16[2,16,2048]{2,1,0:T(8,128)(2,1)S(1)}, bf16[2,16,2048]{2,1,0:T(8,128)(2,1)S(1)}, u32[]{:S(2)}, u32[]{:S(2)}) collective-permute-start(bf16[2,16,2048]{2,1,0:T(8,128)(2,1)S(1)} %get-tuple-element.22), channel_id=1, source_target_pairs={{0,8},{1,9},{2,10},{3,11},{4,12},{5,13},{6,14},{7,15},{8,0},{9,1},... | collective-permute-start | bytes 393224 | tf_op jit(solution)/shard_map/ppermute | solution.py:290
  10.6 0.2 collective-permute-start.2
  10.8 0.1 pad_add_fusion.core_ref
  10.9 6.6 %collective-permute-done.1.after_ref.refs_1_.after_2.refs_2_ = bf16[2,16,2048]{2,1,0:T(8,128)(2,1)S(1)} collective-permute-done((bf16[2,16,2048]{2,1,0:T(8,128)(2,1)S(1)}, bf16[2,16,2048]{2,1,0:T(8,128)(2,1)S(1)}, u32[]{:S(2)}, u32[]{:S(2)}) %collective-permute-start.1) | collective-permute-done | bytes 131104 | tf_op jit(solution)/shard_map/ppermute | solution.py:290
  17.6 0.0 copy-done.1
  17.6 0.6 %rim.1.refs_3_ = bf16[2,128,2048]{2,1,0:T(8,128)(2,1)S(1)} custom-call(bf16[2,16,2048]{2,1,0:T(8,128)(2,1)S(1)} %collective-permute-done.1.after_ref.refs_1_.after_2.refs_2_, s32[2]{0:T(128)S(1)} %pad_add_fusion.core_ref, bf16[2,256,2048]{2,1,0:T(8,128)(2,1)S(1)} %copy-done.1), custom_call_target="tpu_custom_call" | custom-call | tf_op jit(solution)/shard_map/rim/pallas_call | solution.py:273
  18.2 0.0 copy-start.2
  18.2 4.5 %collective-permute-done.2.refs_2_.after_3.refs_3_ = bf16[2,16,2048]{2,1,0:T(8,128)(2,1)S(1)} collective-permute-done((bf16[2,16,2048]{2,1,0:T(8,128)(2,1)S(1)}, bf16[2,16,2048]{2,1,0:T(8,128)(2,1)S(1)}, u32[]{:S(2)}, u32[]{:S(2)}) %collective-permute-start.2) | collective-permute-done | bytes 131104 | tf_op jit(solution)/shard_map/ppermute | solution.py:290
  22.7 0.0 collective-permute-done.refs_0_.after_1
  22.7 0.0 collective-permute-done.3.refs_4_.mine_ref
  22.7 0.4 side.1
  23.1 0.7 %collective-permute-start.4 = (bf16[2,128,2048]{2,1,0:T(8,128)(2,1)S(1)}, bf16[2,128,2048]{2,1,0:T(8,128)(2,1)S(1)}, u32[]{:S(2)}, u32[]{:S(2)}) collective-permute-start(bf16[2,128,2048]{2,1,0:T(8,128)(2,1)S(1)} %get-tuple-element.24), channel_id=1, source_target_pairs={{1,2},{3,4},{5,6},{7,8},{9,10},{11,12},{13,14},{2,1},{4,3},{6,5},{... | collective-permute-start | bytes 3145736 | tf_op jit(solution)/shard_map/ppermute | solution.py:335
  23.9 1.9 %collective-permute-start.6 = (bf16[1,64,2048]{2,1,0:T(8,128)(2,1)S(1)}, bf16[1,64,2048]{2,1,0:T(8,128)(2,1)S(1)}, u32[]{:S(2)}, u32[]{:S(2)}) collective-permute-start(bf16[1,64,2048]{2,1,0:T(8,128)(2,1)S(1)} %get-tuple-element.38), channel_id=1, source_target_pairs={{0,1},{1,0},{2,3},{3,2},{4,5},{5,4},{6,7},{7,6},{8,9},{9,8},{10,11... | collective-permute-start | bytes 786440 | tf_op jit(solution)/shard_map/ppermute | solution.py:290
  25.8 0.1 collective-permute-start.7
  25.8 0.7 %collective-permute-start.8 = (bf16[2,32,2048]{2,1,0:T(8,128)(2,1)S(1)}, bf16[2,32,2048]{2,1,0:T(8,128)(2,1)S(1)}, u32[]{:S(2)}, u32[]{:S(2)}) collective-permute-start(bf16[2,32,2048]{2,1,0:T(8,128)(2,1)S(1)} %get-tuple-element.25.after_ref.after_4), channel_id=1, source_target_pairs={{0,4},{1,5},{2,6},{3,7},{4,0},{5,1},{6,2},{7,3},{8,12},{9,13},{10,... | collective-permute-start | bytes 786440 | tf_op jit(solution)/shard_map/ppermute | solution.py:290
  26.6 0.3 collective-permute-done.6.their_key_ref
  26.9 2.1 %collective-permute-start.10 = (bf16[2,16,2048]{2,1,0:T(8,128)(2,1)S(1)}, bf16[2,16,2048]{2,1,0:T(8,128)(2,1)S(1)}, u32[]{:S(2)}, u32[]{:S(2)}) collective-permute-start(bf16[2,16,2048]{2,1,0:T(8,128)(2,1)S(1)} %get-tuple-element.31), channel_id=1, source_target_pairs={{0,12},{1,13},{2,14},{3,15},{4,8},{5,9},{6,10},{7,11},{8,4},{9,5},... | collective-permute-start | bytes 393224 | tf_op jit(solution)/shard_map/ppermute | solution.py:290
  29.0 0.0 collective-permute-done.7.their_value_ref
  29.0 0.3 collective-permute-start.9
  29.3 0.0 copy-done.2
  29.3 1.3 %ups.1 = (bf16[256,2048]{1,0:T(8,128)(2,1)S(1)}, bf16[256,2048]{1,0:T(8,128)(2,1)S(1)}, bf16[256,2048]{1,0:T(8,128)(2,1)S(1)}, bf16[256,2048]{1,0:T(8,128)(2,1)S(1)}) custom-call(bf16[2,32,2048]{2,1,0:T(8,128)(2,1)S(1)} %get-tuple-element.25.after_ref.after_4, bf16[256,2048]{1,0:T(8,128)(2,1)S(1)} %copy-done.2), custom_call_target="tpu_custom_call" | custom-call | tf_op jit(solution)/shard_map/ups/pallas_call | solution.py:273
  30.7 1.6 %own.1 = (f32[256,2048]{1,0:T(8,128)S(1)}, f32[256,2048]{1,0:T(8,128)S(1)}) custom-call(bf16[2,32,2048]{2,1,0:T(8,128)(2,1)S(1)} %get-tuple-element.25.after_ref.after_4, bf16[256,2048]{1,0:T(8,128)(2,1)S(1)} %copy-done.2, bf16[2,256,2048]{2,1,0:T(8,128)(2,1)S(1)} %copy-done.1), custom_call_target="tpu_custom_call" | custom-call | tf_op jit(solution)/shard_map/own/pallas_call | solution.py:273
  32.3 0.0 collective-permute-done.5.inner_ref
  32.3 5.3 %near.1 = (f32[256,2048]{1,0:T(8,128)S(1)}, f32[256,2048]{1,0:T(8,128)S(1)}) custom-call(bf16[2,32,2048]{2,1,0:T(8,128)(2,1)S(1)} %collective-permute-done.refs_0_.after_1, bf16[2,16,2048]{2,1,0:T(8,128)(2,1)S(1)} %collective-permute-done.1.after_ref.refs_1_.after_2.refs_2_, bf16[2,16,2048]{2,1,0:T(8,128)(2,1)S(1)} %collective-permute-done.2.refs_2_.after_3.refs_3_, ...), custom_call_target="tpu_custom_call" | custom-call | tf_op jit(solution)/shard_map/near/pallas_call | solution.py:273
  37.6 11.9 %collective-permute-done.10.refs_5_ = bf16[2,16,2048]{2,1,0:T(8,128)(2,1)S(1)} collective-permute-done((bf16[2,16,2048]{2,1,0:T(8,128)(2,1)S(1)}, bf16[2,16,2048]{2,1,0:T(8,128)(2,1)S(1)}, u32[]{:S(2)}, u32[]{:S(2)}) %collective-permute-start.10) | collective-permute-done | bytes 131104 | tf_op jit(solution)/shard_map/ppermute | solution.py:290
  49.5 0.0 collective-permute-done.9.refs_4_
  49.5 0.4 collective-permute-done.8.refs_1_
  50.0 0.0 collective-permute-done.4.after_1.edge_ref
  50.0 0.1 join.1.after_ref.mine_ref
  50.0 0.1 collective-permute-start.11
  50.1 2.0 %edge.1 = (f32[256,2048]{1,0:T(8,128)S(1)}, f32[256,2048]{1,0:T(8,128)S(1)}) custom-call(bf16[2,128,2048]{2,1,0:T(8,128)(2,1)S(1)} %join.1.after_ref.mine_ref, s32[2]{0:T(128)S(1)} %pad_add_fusion.core_ref, bf16[256,2048]{1,0:T(8,128)(2,1)S(1)} %copy-done.2, bf16[2,128,2048]{2,1,0:T(8,128)(2,1)S(1)} %collective-permute-done.4.after_1.edge_ref, ...), custom_call_target="tpu_custom_call" | custom-call | tf_op jit(solution)/shard_map/edge/pallas_call | solution.py:273
  52.1 0.6 %collective-permute-done.11.theirs_ref = bf16[2,128,2048]{2,1,0:T(8,128)(2,1)S(1)} collective-permute-done((bf16[2,128,2048]{2,1,0:T(8,128)(2,1)S(1)}, bf16[2,128,2048]{2,1,0:T(8,128)(2,1)S(1)}, u32[]{:S(2)}, u32[]{:S(2)}) %collective-permute-start.11) | collective-permute-done | bytes 1048608 | tf_op jit(solution)/shard_map/ppermute | solution.py:290
  52.8 3.1 %far.1 = bf16[256,2048]{1,0:T(8,128)(2,1)} custom-call(bf16[2,128,2048]{2,1,0:T(8,128)(2,1)S(1)} %join.1.after_ref.mine_ref, bf16[2,128,2048]{2,1,0:T(8,128)(2,1)S(1)} %collective-permute-done.11.theirs_ref, f32[256,2048]{1,0:T(8,128)S(1)} %get-tuple-element.33.mean_ref, f32[256,2048]{1,0:T(8,128)S(1)} %get-tuple-element.34.log_ref, ...), custom_call_target="tpu_custom_call" | custom-call | tf_op jit(solution)/shard_map/far/pallas_call | solution.py:273
  (1 shorter events, 0.0 us)
Async XLA Ops:
  0.0 32.3 %collective-permute-start.5 = (bf16[2,256,2048]{2,1,0:T(8,128)(2,1)}, bf16[2,256,2048]{2,1,0:T(8,128)(2,1)}, u32[]{:S(2)}, u32[]{:S(2)}) collective-permute-start(bf16[2,256,2048]{2,1,0:T(8,128)(2,1)} %kv_ref.5), channel_id=1, source_target_pairs={{0,1},{1,0},{2,3},{3,2},{4,5},{5,4},{6,7},{7,6},{8,9},{9,8},{10,11... | collective-permute-start | bytes 6291464 | tf_op jit(solution)/shard_map/ppermute | solution.py:290
  0.5 1.6 %copy-start = (bf16[2,256,2048]{2,1,0:T(8,128)(2,1)S(1)}, bf16[2,256,2048]{2,1,0:T(8,128)(2,1)}, u32[]{:S(2)}) copy-start(bf16[2,256,2048]{2,1,0:T(8,128)(2,1)} %kv_ref.5) | copy-start | bytes 6291460
  2.0 15.5 %copy-start.1 = (bf16[2,256,2048]{2,1,0:T(8,128)(2,1)S(1)}, bf16[2,256,2048]{2,1,0:T(8,128)(2,1)}, u32[]{:S(2)}) copy-start(bf16[2,256,2048]{2,1,0:T(8,128)(2,1)} %kv_ref.5) | copy-start | bytes 6291460
  3.9 18.7 %collective-permute-start.3 = (bf16[2,64,2048]{2,1,0:T(8,128)(2,1)}, bf16[2,64,2048]{2,1,0:T(8,128)(2,1)S(1)}, u32[]{:S(2)}, u32[]{:S(2)}) collective-permute-start(bf16[2,64,2048]{2,1,0:T(8,128)(2,1)} %get-tuple-element.23), channel_id=1, source_target_pairs={{0,2},{1,3},{2,0},{3,1},{4,6},{5,7},{6,4},{7,5},{8,10},{9,11},{10,... | collective-permute-start | bytes 1572872 | tf_op jit(solution)/shard_map/ppermute | solution.py:290
  6.5 16.2 %collective-permute-start = (bf16[2,32,2048]{2,1,0:T(8,128)(2,1)S(1)}, bf16[2,32,2048]{2,1,0:T(8,128)(2,1)S(1)}, u32[]{:S(2)}, u32[]{:S(2)}) collective-permute-start(bf16[2,32,2048]{2,1,0:T(8,128)(2,1)S(1)} %get-tuple-element.21), channel_id=1, source_target_pairs={{0,4},{1,5},{2,6},{3,7},{4,0},{5,1},{6,2},{7,3},{8,12},{9,13},{10,... | collective-permute-start | bytes 786440 | tf_op jit(solution)/shard_map/ppermute | solution.py:290
  8.0 9.5 %collective-permute-start.1 = (bf16[2,16,2048]{2,1,0:T(8,128)(2,1)S(1)}, bf16[2,16,2048]{2,1,0:T(8,128)(2,1)S(1)}, u32[]{:S(2)}, u32[]{:S(2)}) collective-permute-start(bf16[2,16,2048]{2,1,0:T(8,128)(2,1)S(1)} %get-tuple-element.22), channel_id=1, source_target_pairs={{0,8},{1,9},{2,10},{3,11},{4,12},{5,13},{6,14},{7,15},{8,0},{9,1},... | collective-permute-start | bytes 393224 | tf_op jit(solution)/shard_map/ppermute | solution.py:290
  10.6 12.0 %collective-permute-start.2 = (bf16[2,16,2048]{2,1,0:T(8,128)(2,1)S(1)}, bf16[2,16,2048]{2,1,0:T(8,128)(2,1)S(1)}, u32[]{:S(2)}, u32[]{:S(2)}) collective-permute-start(bf16[2,16,2048]{2,1,0:T(8,128)(2,1)S(1)} %get-tuple-element.22), channel_id=1, source_target_pairs={{0,12},{1,13},{2,14},{3,15},{4,8},{5,9},{6,10},{7,11},{8,4},{9,5},... | collective-permute-start | bytes 393224 | tf_op jit(solution)/shard_map/ppermute | solution.py:290
  18.2 11.2 %copy-start.2 = (bf16[256,2048]{1,0:T(8,128)(2,1)S(1)}, bf16[256,2048]{1,0:T(8,128)(2,1)}, u32[]{:S(2)}) copy-start(bf16[256,2048]{1,0:T(8,128)(2,1)} %q_ref.7) | copy-start | bytes 3145732
  23.1 26.9 %collective-permute-start.4 = (bf16[2,128,2048]{2,1,0:T(8,128)(2,1)S(1)}, bf16[2,128,2048]{2,1,0:T(8,128)(2,1)S(1)}, u32[]{:S(2)}, u32[]{:S(2)}) collective-permute-start(bf16[2,128,2048]{2,1,0:T(8,128)(2,1)S(1)} %get-tuple-element.24), channel_id=1, source_target_pairs={{1,2},{3,4},{5,6},{7,8},{9,10},{11,12},{13,14},{2,1},{4,3},{6,5},{... | collective-permute-start | bytes 3145736 | tf_op jit(solution)/shard_map/ppermute | solution.py:335
  23.9 3.0 %collective-permute-start.6 = (bf16[1,64,2048]{2,1,0:T(8,128)(2,1)S(1)}, bf16[1,64,2048]{2,1,0:T(8,128)(2,1)S(1)}, u32[]{:S(2)}, u32[]{:S(2)}) collective-permute-start(bf16[1,64,2048]{2,1,0:T(8,128)(2,1)S(1)} %get-tuple-element.38), channel_id=1, source_target_pairs={{0,1},{1,0},{2,3},{3,2},{4,5},{5,4},{6,7},{7,6},{8,9},{9,8},{10,11... | collective-permute-start | bytes 786440 | tf_op jit(solution)/shard_map/ppermute | solution.py:290
  25.8 3.2 %collective-permute-start.7 = (bf16[1,64,2048]{2,1,0:T(8,128)(2,1)S(1)}, bf16[1,64,2048]{2,1,0:T(8,128)(2,1)S(1)}, u32[]{:S(2)}, u32[]{:S(2)}) collective-permute-start(bf16[1,64,2048]{2,1,0:T(8,128)(2,1)S(1)} %get-tuple-element.37), channel_id=1, source_target_pairs={{0,1},{1,0},{2,3},{3,2},{4,5},{5,4},{6,7},{7,6},{8,9},{9,8},{10,11... | collective-permute-start | bytes 786440 | tf_op jit(solution)/shard_map/ppermute | solution.py:290
  25.8 24.1 %collective-permute-start.8 = (bf16[2,32,2048]{2,1,0:T(8,128)(2,1)S(1)}, bf16[2,32,2048]{2,1,0:T(8,128)(2,1)S(1)}, u32[]{:S(2)}, u32[]{:S(2)}) collective-permute-start(bf16[2,32,2048]{2,1,0:T(8,128)(2,1)S(1)} %get-tuple-element.25.after_ref.after_4), channel_id=1, source_target_pairs={{0,4},{1,5},{2,6},{3,7},{4,0},{5,1},{6,2},{7,3},{8,12},{9,13},{10,... | collective-permute-start | bytes 786440 | tf_op jit(solution)/shard_map/ppermute | solution.py:290
  26.9 22.6 %collective-permute-start.10 = (bf16[2,16,2048]{2,1,0:T(8,128)(2,1)S(1)}, bf16[2,16,2048]{2,1,0:T(8,128)(2,1)S(1)}, u32[]{:S(2)}, u32[]{:S(2)}) collective-permute-start(bf16[2,16,2048]{2,1,0:T(8,128)(2,1)S(1)} %get-tuple-element.31), channel_id=1, source_target_pairs={{0,12},{1,13},{2,14},{3,15},{4,8},{5,9},{6,10},{7,11},{8,4},{9,5},... | collective-permute-start | bytes 393224 | tf_op jit(solution)/shard_map/ppermute | solution.py:290
  29.0 20.6 %collective-permute-start.9 = (bf16[2,16,2048]{2,1,0:T(8,128)(2,1)S(1)}, bf16[2,16,2048]{2,1,0:T(8,128)(2,1)S(1)}, u32[]{:S(2)}, u32[]{:S(2)}) collective-permute-start(bf16[2,16,2048]{2,1,0:T(8,128)(2,1)S(1)} %get-tuple-element.31), channel_id=1, source_target_pairs={{0,8},{1,9},{2,10},{3,11},{4,12},{5,13},{6,14},{7,15},{8,0},{9,1},... | collective-permute-start | bytes 393224 | tf_op jit(solution)/shard_map/ppermute | solution.py:290
  50.0 2.7 %collective-permute-start.11 = (bf16[2,128,2048]{2,1,0:T(8,128)(2,1)S(1)}, bf16[2,128,2048]{2,1,0:T(8,128)(2,1)S(1)}, u32[]{:S(2)}, u32[]{:S(2)}) collective-permute-start(bf16[2,128,2048]{2,1,0:T(8,128)(2,1)S(1)} %join.1.after_ref.mine_ref), channel_id=1, source_target_pairs={{0,1},{1,0},{2,3},{3,2},{4,5},{5,4},{6,7},{7,6},{8,9},{9,8},{10,11... | collective-permute-start | bytes 3145736 | tf_op jit(solution)/shard_map/ppermute | solution.py:290

commit v7 on v6

--- a/solution.py
+++ b/solution.py
@@ -11,7 +11,7 @@
 HEADS = 16
 HEAD_DIM = 128
 BLOCK = 128
-GROUP = 8
+GROUP = 16
 neg_large = -1e30
 log_two = 0.6931471805599453
 to_log2 = 1.0 / (math.sqrt(HEAD_DIM) * log_two)

time: 56.2 us -> 56.4 us (level)
  no operation moved by 1% of the time
where the time goes in v7:
time: 56.4 us; the launch traced here: 56.2 us
  waiting for transfers between devices  24.4 us (43%)
  Pallas kernels  16.6 us (29%)
  starting transfers between devices  13.2 us (23%)
  local copies, waits for them, and re-layouts  1.64 us (3%)
    ppermute x11, waiting for transfers between devices, sent(): return lax.ppermute(array, 'seq', [(i, i ^ stride) for i in range(count)])  24.4 us
    pallas_call x9, Pallas kernels, call(): pl.pallas_call(kernel, in_specs=in_specs, out_specs=out_specs or [VMEM] *...  16.6 us
    ppermute x11, starting transfers between devices, sent(): return lax.ppermute(array, 'seq', [(i, i ^ stride) for i in range(count)])  12.5 us
    unnamed x6, local copies, waits for them, and re-layouts  1.6 us
  transfers between devices with their start and end apart: 12, of which 6 were waited for; matrix products, arithmetic and copies ran while one was open for 0% of the time, Pallas kernels for 24%

profile of v7, /device:TPU:0, one launch (start us, length us, event | category | flops | bytes accessed | tf_op | source)
XLA Modules:
  0.0 56.2 jit_solution(6561321745693537363)
XLA Ops:
  0.0 0.5 collective-permute-start.5
  0.5 0.0 copy-start
  0.5 1.6 %copy-done = bf16[2,256,2048]{2,1,0:T(8,128)(2,1)S(1)} copy-done((bf16[2,256,2048]{2,1,0:T(8,128)(2,1)S(1)}, bf16[2,256,2048]{2,1,0:T(8,128)(2,1)}, u32[]{:S(2)}) %copy-start) | copy-done | bytes 2097176
  2.0 0.0 copy-start.1
  2.0 1.9 %pool.1 = (bf16[2,64,2048]{2,1,0:T(8,128)(2,1)}, bf16[2,32,2048]{2,1,0:T(8,128)(2,1)S(1)}, bf16[2,16,2048]{2,1,0:T(8,128)(2,1)S(1)}) custom-call(bf16[2,256,2048]{2,1,0:T(8,128)(2,1)S(1)} %copy-done), custom_call_target="tpu_custom_call" | custom-call | tf_op jit(solution)/shard_map/pool/pallas_call | solution.py:273
  3.9 2.5 %collective-permute-start.3 = (bf16[2,64,2048]{2,1,0:T(8,128)(2,1)}, bf16[2,64,2048]{2,1,0:T(8,128)(2,1)S(1)}, u32[]{:S(2)}, u32[]{:S(2)}) collective-permute-start(bf16[2,64,2048]{2,1,0:T(8,128)(2,1)} %get-tuple-element.23), channel_id=1, source_target_pairs={{0,2},{1,3},{2,0},{3,1},{4,6},{5,7},{6,4},{7,5},{8,10},{9,11},{10,... | collective-permute-start | bytes 1572872 | tf_op jit(solution)/shard_map/ppermute | solution.py:290
  6.5 1.6 %collective-permute-start = (bf16[2,32,2048]{2,1,0:T(8,128)(2,1)S(1)}, bf16[2,32,2048]{2,1,0:T(8,128)(2,1)S(1)}, u32[]{:S(2)}, u32[]{:S(2)}) collective-permute-start(bf16[2,32,2048]{2,1,0:T(8,128)(2,1)S(1)} %get-tuple-element.21), channel_id=1, source_target_pairs={{0,4},{1,5},{2,6},{3,7},{4,0},{5,1},{6,2},{7,3},{8,12},{9,13},{10,... | collective-permute-start | bytes 786440 | tf_op jit(solution)/shard_map/ppermute | solution.py:290
  8.0 2.6 %collective-permute-start.1 = (bf16[2,16,2048]{2,1,0:T(8,128)(2,1)S(1)}, bf16[2,16,2048]{2,1,0:T(8,128)(2,1)S(1)}, u32[]{:S(2)}, u32[]{:S(2)}) collective-permute-start(bf16[2,16,2048]{2,1,0:T(8,128)(2,1)S(1)} %get-tuple-element.22), channel_id=1, source_target_pairs={{0,8},{1,9},{2,10},{3,11},{4,12},{5,13},{6,14},{7,15},{8,0},{9,1},... | collective-permute-start | bytes 393224 | tf_op jit(solution)/shard_map/ppermute | solution.py:290
  10.6 0.2 collective-permute-start.2
  10.8 0.1 pad_add_fusion.core_ref
  10.9 6.6 %collective-permute-done.1.after_ref.refs_1_.after_2.refs_2_ = bf16[2,16,2048]{2,1,0:T(8,128)(2,1)S(1)} collective-permute-done((bf16[2,16,2048]{2,1,0:T(8,128)(2,1)S(1)}, bf16[2,16,2048]{2,1,0:T(8,128)(2,1)S(1)}, u32[]{:S(2)}, u32[]{:S(2)}) %collective-permute-start.1) | collective-permute-done | bytes 131104 | tf_op jit(solution)/shard_map/ppermute | solution.py:290
  17.6 0.0 copy-done.1
  17.6 0.6 %rim.1.refs_3_ = bf16[2,128,2048]{2,1,0:T(8,128)(2,1)S(1)} custom-call(bf16[2,16,2048]{2,1,0:T(8,128)(2,1)S(1)} %collective-permute-done.1.after_ref.refs_1_.after_2.refs_2_, s32[2]{0:T(128)S(1)} %pad_add_fusion.core_ref, bf16[2,256,2048]{2,1,0:T(8,128)(2,1)S(1)} %copy-done.1), custom_call_target="tpu_custom_call" | custom-call | tf_op jit(solution)/shard_map/rim/pallas_call | solution.py:273
  18.2 0.0 copy-start.2
  18.2 4.5 %collective-permute-done.2.refs_2_.after_3.refs_3_ = bf16[2,16,2048]{2,1,0:T(8,128)(2,1)S(1)} collective-permute-done((bf16[2,16,2048]{2,1,0:T(8,128)(2,1)S(1)}, bf16[2,16,2048]{2,1,0:T(8,128)(2,1)S(1)}, u32[]{:S(2)}, u32[]{:S(2)}) %collective-permute-start.2) | collective-permute-done | bytes 131104 | tf_op jit(solution)/shard_map/ppermute | solution.py:290
  22.7 0.0 collective-permute-done.refs_0_.after_1
  22.7 0.0 collective-permute-done.3.refs_4_.mine_ref
  22.7 0.4 side.1
  23.1 0.7 %collective-permute-start.4 = (bf16[2,128,2048]{2,1,0:T(8,128)(2,1)S(1)}, bf16[2,128,2048]{2,1,0:T(8,128)(2,1)S(1)}, u32[]{:S(2)}, u32[]{:S(2)}) collective-permute-start(bf16[2,128,2048]{2,1,0:T(8,128)(2,1)S(1)} %get-tuple-element.24), channel_id=1, source_target_pairs={{1,2},{3,4},{5,6},{7,8},{9,10},{11,12},{13,14},{2,1},{4,3},{6,5},{... | collective-permute-start | bytes 3145736 | tf_op jit(solution)/shard_map/ppermute | solution.py:335
  23.9 1.9 %collective-permute-start.6 = (bf16[1,64,2048]{2,1,0:T(8,128)(2,1)S(1)}, bf16[1,64,2048]{2,1,0:T(8,128)(2,1)S(1)}, u32[]{:S(2)}, u32[]{:S(2)}) collective-permute-start(bf16[1,64,2048]{2,1,0:T(8,128)(2,1)S(1)} %get-tuple-element.38), channel_id=1, source_target_pairs={{0,1},{1,0},{2,3},{3,2},{4,5},{5,4},{6,7},{7,6},{8,9},{9,8},{10,11... | collective-permute-start | bytes 786440 | tf_op jit(solution)/shard_map/ppermute | solution.py:290
  25.8 0.1 collective-permute-start.7
  25.8 0.7 %collective-permute-start.8 = (bf16[2,32,2048]{2,1,0:T(8,128)(2,1)S(1)}, bf16[2,32,2048]{2,1,0:T(8,128)(2,1)S(1)}, u32[]{:S(2)}, u32[]{:S(2)}) collective-permute-start(bf16[2,32,2048]{2,1,0:T(8,128)(2,1)S(1)} %get-tuple-element.25.after_ref.after_4), channel_id=1, source_target_pairs={{0,4},{1,5},{2,6},{3,7},{4,0},{5,1},{6,2},{7,3},{8,12},{9,13},{10,... | collective-permute-start | bytes 786440 | tf_op jit(solution)/shard_map/ppermute | solution.py:290
  26.6 0.3 collective-permute-done.6.their_key_ref
  26.9 2.1 %collective-permute-start.10 = (bf16[2,16,2048]{2,1,0:T(8,128)(2,1)S(1)}, bf16[2,16,2048]{2,1,0:T(8,128)(2,1)S(1)}, u32[]{:S(2)}, u32[]{:S(2)}) collective-permute-start(bf16[2,16,2048]{2,1,0:T(8,128)(2,1)S(1)} %get-tuple-element.31), channel_id=1, source_target_pairs={{0,12},{1,13},{2,14},{3,15},{4,8},{5,9},{6,10},{7,11},{8,4},{9,5},... | collective-permute-start | bytes 393224 | tf_op jit(solution)/shard_map/ppermute | solution.py:290
  29.0 0.0 collective-permute-done.7.their_value_ref
  29.0 0.3 collective-permute-start.9
  29.3 0.0 copy-done.2
  29.3 1.3 %ups.1 = (bf16[256,2048]{1,0:T(8,128)(2,1)S(1)}, bf16[256,2048]{1,0:T(8,128)(2,1)S(1)}, bf16[256,2048]{1,0:T(8,128)(2,1)S(1)}, bf16[256,2048]{1,0:T(8,128)(2,1)S(1)}) custom-call(bf16[2,32,2048]{2,1,0:T(8,128)(2,1)S(1)} %get-tuple-element.25.after_ref.after_4, bf16[256,2048]{1,0:T(8,128)(2,1)S(1)} %copy-done.2), custom_call_target="tpu_custom_call" | custom-call | tf_op jit(solution)/shard_map/ups/pallas_call | solution.py:273
  30.7 1.6 %own.1 = (f32[256,2048]{1,0:T(8,128)S(1)}, f32[256,2048]{1,0:T(8,128)S(1)}) custom-call(bf16[2,32,2048]{2,1,0:T(8,128)(2,1)S(1)} %get-tuple-element.25.after_ref.after_4, bf16[256,2048]{1,0:T(8,128)(2,1)S(1)} %copy-done.2, bf16[2,256,2048]{2,1,0:T(8,128)(2,1)S(1)} %copy-done.1), custom_call_target="tpu_custom_call" | custom-call | tf_op jit(solution)/shard_map/own/pallas_call | solution.py:273
  32.3 0.0 collective-permute-done.5.inner_ref
  32.3 5.3 %near.1 = (f32[256,2048]{1,0:T(8,128)S(1)}, f32[256,2048]{1,0:T(8,128)S(1)}) custom-call(bf16[2,32,2048]{2,1,0:T(8,128)(2,1)S(1)} %collective-permute-done.refs_0_.after_1, bf16[2,16,2048]{2,1,0:T(8,128)(2,1)S(1)} %collective-permute-done.1.after_ref.refs_1_.after_2.refs_2_, bf16[2,16,2048]{2,1,0:T(8,128)(2,1)S(1)} %collective-permute-done.2.refs_2_.after_3.refs_3_, ...), custom_call_target="tpu_custom_call" | custom-call | tf_op jit(solution)/shard_map/near/pallas_call | solution.py:273
  37.6 11.9 %collective-permute-done.10.refs_5_ = bf16[2,16,2048]{2,1,0:T(8,128)(2,1)S(1)} collective-permute-done((bf16[2,16,2048]{2,1,0:T(8,128)(2,1)S(1)}, bf16[2,16,2048]{2,1,0:T(8,128)(2,1)S(1)}, u32[]{:S(2)}, u32[]{:S(2)}) %collective-permute-start.10) | collective-permute-done | bytes 131104 | tf_op jit(solution)/shard_map/ppermute | solution.py:290
  49.5 0.0 collective-permute-done.9.refs_4_
  49.5 0.4 collective-permute-done.8.refs_1_
  50.0 0.0 collective-permute-done.4.after_1.edge_ref
  50.0 0.1 join.1.after_ref.mine_ref
  50.0 0.1 collective-permute-start.11
  50.1 2.0 %edge.1 = (f32[256,2048]{1,0:T(8,128)S(1)}, f32[256,2048]{1,0:T(8,128)S(1)}) custom-call(bf16[2,128,2048]{2,1,0:T(8,128)(2,1)S(1)} %join.1.after_ref.mine_ref, s32[2]{0:T(128)S(1)} %pad_add_fusion.core_ref, bf16[256,2048]{1,0:T(8,128)(2,1)S(1)} %copy-done.2, bf16[2,128,2048]{2,1,0:T(8,128)(2,1)S(1)} %collective-permute-done.4.after_1.edge_ref, ...), custom_call_target="tpu_custom_call" | custom-call | tf_op jit(solution)/shard_map/edge/pallas_call | solution.py:273
  52.1 0.6 %collective-permute-done.11.theirs_ref = bf16[2,128,2048]{2,1,0:T(8,128)(2,1)S(1)} collective-permute-done((bf16[2,128,2048]{2,1,0:T(8,128)(2,1)S(1)}, bf16[2,128,2048]{2,1,0:T(8,128)(2,1)S(1)}, u32[]{:S(2)}, u32[]{:S(2)}) %collective-permute-start.11) | collective-permute-done | bytes 1048608 | tf_op jit(solution)/shard_map/ppermute | solution.py:290
  52.8 3.3 %far.1 = bf16[256,2048]{1,0:T(8,128)(2,1)} custom-call(bf16[2,128,2048]{2,1,0:T(8,128)(2,1)S(1)} %join.1.after_ref.mine_ref, bf16[2,128,2048]{2,1,0:T(8,128)(2,1)S(1)} %collective-permute-done.11.theirs_ref, f32[256,2048]{1,0:T(8,128)S(1)} %get-tuple-element.33.mean_ref, f32[256,2048]{1,0:T(8,128)S(1)} %get-tuple-element.34.log_ref, ...), custom_call_target="tpu_custom_call" | custom-call | tf_op jit(solution)/shard_map/far/pallas_call | solution.py:273
  (1 shorter events, 0.0 us)
Async XLA Ops:
  0.0 32.3 %collective-permute-start.5 = (bf16[2,256,2048]{2,1,0:T(8,128)(2,1)}, bf16[2,256,2048]{2,1,0:T(8,128)(2,1)}, u32[]{:S(2)}, u32[]{:S(2)}) collective-permute-start(bf16[2,256,2048]{2,1,0:T(8,128)(2,1)} %kv_ref.5), channel_id=1, source_target_pairs={{0,1},{1,0},{2,3},{3,2},{4,5},{5,4},{6,7},{7,6},{8,9},{9,8},{10,11... | collective-permute-start | bytes 6291464 | tf_op jit(solution)/shard_map/ppermute | solution.py:290
  0.5 1.6 %copy-start = (bf16[2,256,2048]{2,1,0:T(8,128)(2,1)S(1)}, bf16[2,256,2048]{2,1,0:T(8,128)(2,1)}, u32[]{:S(2)}) copy-start(bf16[2,256,2048]{2,1,0:T(8,128)(2,1)} %kv_ref.5) | copy-start | bytes 6291460
  2.0 15.5 %copy-start.1 = (bf16[2,256,2048]{2,1,0:T(8,128)(2,1)S(1)}, bf16[2,256,2048]{2,1,0:T(8,128)(2,1)}, u32[]{:S(2)}) copy-start(bf16[2,256,2048]{2,1,0:T(8,128)(2,1)} %kv_ref.5) | copy-start | bytes 6291460
  3.9 18.7 %collective-permute-start.3 = (bf16[2,64,2048]{2,1,0:T(8,128)(2,1)}, bf16[2,64,2048]{2,1,0:T(8,128)(2,1)S(1)}, u32[]{:S(2)}, u32[]{:S(2)}) collective-permute-start(bf16[2,64,2048]{2,1,0:T(8,128)(2,1)} %get-tuple-element.23), channel_id=1, source_target_pairs={{0,2},{1,3},{2,0},{3,1},{4,6},{5,7},{6,4},{7,5},{8,10},{9,11},{10,... | collective-permute-start | bytes 1572872 | tf_op jit(solution)/shard_map/ppermute | solution.py:290
  6.5 16.2 %collective-permute-start = (bf16[2,32,2048]{2,1,0:T(8,128)(2,1)S(1)}, bf16[2,32,2048]{2,1,0:T(8,128)(2,1)S(1)}, u32[]{:S(2)}, u32[]{:S(2)}) collective-permute-start(bf16[2,32,2048]{2,1,0:T(8,128)(2,1)S(1)} %get-tuple-element.21), channel_id=1, source_target_pairs={{0,4},{1,5},{2,6},{3,7},{4,0},{5,1},{6,2},{7,3},{8,12},{9,13},{10,... | collective-permute-start | bytes 786440 | tf_op jit(solution)/shard_map/ppermute | solution.py:290
  8.0 9.5 %collective-permute-start.1 = (bf16[2,16,2048]{2,1,0:T(8,128)(2,1)S(1)}, bf16[2,16,2048]{2,1,0:T(8,128)(2,1)S(1)}, u32[]{:S(2)}, u32[]{:S(2)}) collective-permute-start(bf16[2,16,2048]{2,1,0:T(8,128)(2,1)S(1)} %get-tuple-element.22), channel_id=1, source_target_pairs={{0,8},{1,9},{2,10},{3,11},{4,12},{5,13},{6,14},{7,15},{8,0},{9,1},... | collective-permute-start | bytes 393224 | tf_op jit(solution)/shard_map/ppermute | solution.py:290
  10.6 12.0 %collective-permute-start.2 = (bf16[2,16,2048]{2,1,0:T(8,128)(2,1)S(1)}, bf16[2,16,2048]{2,1,0:T(8,128)(2,1)S(1)}, u32[]{:S(2)}, u32[]{:S(2)}) collective-permute-start(bf16[2,16,2048]{2,1,0:T(8,128)(2,1)S(1)} %get-tuple-element.22), channel_id=1, source_target_pairs={{0,12},{1,13},{2,14},{3,15},{4,8},{5,9},{6,10},{7,11},{8,4},{9,5},... | collective-permute-start | bytes 393224 | tf_op jit(solution)/shard_map/ppermute | solution.py:290
  18.2 11.2 %copy-start.2 = (bf16[256,2048]{1,0:T(8,128)(2,1)S(1)}, bf16[256,2048]{1,0:T(8,128)(2,1)}, u32[]{:S(2)}) copy-start(bf16[256,2048]{1,0:T(8,128)(2,1)} %q_ref.7) | copy-start | bytes 3145732
  23.1 26.9 %collective-permute-start.4 = (bf16[2,128,2048]{2,1,0:T(8,128)(2,1)S(1)}, bf16[2,128,2048]{2,1,0:T(8,128)(2,1)S(1)}, u32[]{:S(2)}, u32[]{:S(2)}) collective-permute-start(bf16[2,128,2048]{2,1,0:T(8,128)(2,1)S(1)} %get-tuple-element.24), channel_id=1, source_target_pairs={{1,2},{3,4},{5,6},{7,8},{9,10},{11,12},{13,14},{2,1},{4,3},{6,5},{... | collective-permute-start | bytes 3145736 | tf_op jit(solution)/shard_map/ppermute | solution.py:335
  23.9 3.0 %collective-permute-start.6 = (bf16[1,64,2048]{2,1,0:T(8,128)(2,1)S(1)}, bf16[1,64,2048]{2,1,0:T(8,128)(2,1)S(1)}, u32[]{:S(2)}, u32[]{:S(2)}) collective-permute-start(bf16[1,64,2048]{2,1,0:T(8,128)(2,1)S(1)} %get-tuple-element.38), channel_id=1, source_target_pairs={{0,1},{1,0},{2,3},{3,2},{4,5},{5,4},{6,7},{7,6},{8,9},{9,8},{10,11... | collective-permute-start | bytes 786440 | tf_op jit(solution)/shard_map/ppermute | solution.py:290
  25.8 3.2 %collective-permute-start.7 = (bf16[1,64,2048]{2,1,0:T(8,128)(2,1)S(1)}, bf16[1,64,2048]{2,1,0:T(8,128)(2,1)S(1)}, u32[]{:S(2)}, u32[]{:S(2)}) collective-permute-start(bf16[1,64,2048]{2,1,0:T(8,128)(2,1)S(1)} %get-tuple-element.37), channel_id=1, source_target_pairs={{0,1},{1,0},{2,3},{3,2},{4,5},{5,4},{6,7},{7,6},{8,9},{9,8},{10,11... | collective-permute-start | bytes 786440 | tf_op jit(solution)/shard_map/ppermute | solution.py:290
  25.8 24.1 %collective-permute-start.8 = (bf16[2,32,2048]{2,1,0:T(8,128)(2,1)S(1)}, bf16[2,32,2048]{2,1,0:T(8,128)(2,1)S(1)}, u32[]{:S(2)}, u32[]{:S(2)}) collective-permute-start(bf16[2,32,2048]{2,1,0:T(8,128)(2,1)S(1)} %get-tuple-element.25.after_ref.after_4), channel_id=1, source_target_pairs={{0,4},{1,5},{2,6},{3,7},{4,0},{5,1},{6,2},{7,3},{8,12},{9,13},{10,... | collective-permute-start | bytes 786440 | tf_op jit(solution)/shard_map/ppermute | solution.py:290
  26.9 22.6 %collective-permute-start.10 = (bf16[2,16,2048]{2,1,0:T(8,128)(2,1)S(1)}, bf16[2,16,2048]{2,1,0:T(8,128)(2,1)S(1)}, u32[]{:S(2)}, u32[]{:S(2)}) collective-permute-start(bf16[2,16,2048]{2,1,0:T(8,128)(2,1)S(1)} %get-tuple-element.31), channel_id=1, source_target_pairs={{0,12},{1,13},{2,14},{3,15},{4,8},{5,9},{6,10},{7,11},{8,4},{9,5},... | collective-permute-start | bytes 393224 | tf_op jit(solution)/shard_map/ppermute | solution.py:290
  29.0 20.6 %collective-permute-start.9 = (bf16[2,16,2048]{2,1,0:T(8,128)(2,1)S(1)}, bf16[2,16,2048]{2,1,0:T(8,128)(2,1)S(1)}, u32[]{:S(2)}, u32[]{:S(2)}) collective-permute-start(bf16[2,16,2048]{2,1,0:T(8,128)(2,1)S(1)} %get-tuple-element.31), channel_id=1, source_target_pairs={{0,8},{1,9},{2,10},{3,11},{4,12},{5,13},{6,14},{7,15},{8,0},{9,1},... | collective-permute-start | bytes 393224 | tf_op jit(solution)/shard_map/ppermute | solution.py:290
  50.0 2.7 %collective-permute-start.11 = (bf16[2,128,2048]{2,1,0:T(8,128)(2,1)S(1)}, bf16[2,128,2048]{2,1,0:T(8,128)(2,1)S(1)}, u32[]{:S(2)}, u32[]{:S(2)}) collective-permute-start(bf16[2,128,2048]{2,1,0:T(8,128)(2,1)S(1)} %join.1.after_ref.mine_ref), channel_id=1, source_target_pairs={{0,1},{1,0},{2,3},{3,2},{4,5},{5,4},{6,7},{7,6},{8,9},{9,8},{10,11... | collective-permute-start | bytes 3145736 | tf_op jit(solution)/shard_map/ppermute | solution.py:290
